TPU v7x, 256 devices: a whole 4x4x8 slice. The times are simulated.
256 devices in a mesh: scen: 16 (over z, y_lo), blk: 16 (over y_hi, x, core).
Axes of the slice: x: 4, y: 4 (y_hi: 2, y_lo: 2; y = y_hi * 2 + y_lo), z: 8, core: 2. Of those that a mesh axis runs over, the one named last changes fastest.
Arguments:
- draws: bfloat16 [8192, 8192], P('blk', 'scen'), may hold values from -6 to 6
- factor: bfloat16 [8192, 8192], P('scen', 'blk'), may hold values from -0.1875 to 0.1875
- occupancy: int32 [16, 16], replicated, may hold values from 0 to 1, as said below
Outputs:
- scenarios: bfloat16 [8192, 8192], P('blk', 'scen')
Inputs may be any that keep to these rules, and one draw needn't show every extreme that they name: occupancy[i, i] is 1 for every i, occupancy[i, j] is 0 for j > i, and each entry below the diagonal is 0 or 1.
All inputs are finite; a program needn't handle non-finite values.
Results may differ from a plain program's by a relative error of at most 0.001.
Values may be sent and summed in bfloat16 or wider, within the bound.
No kernel may reach another device: no remote copies, remote signals or barrier semaphores. Data moves between devices by JAX's collectives and lax.ppermute only.
A program may use at most 64 MiB of HBM per device.

v0:
```python
import jax
import jax.numpy as jnp
from jax import lax
from jax.sharding import PartitionSpec as P

TILE = 512


def keep_mask(row_start, row_count, col_count, occ_float):
    tile_ids = jnp.arange(occ_float.shape[0], dtype=jnp.int32)
    rows = row_start + jnp.arange(row_count, dtype=jnp.int32)
    cols = jnp.arange(col_count, dtype=jnp.int32)
    row_hot = (rows[:, None] // TILE == tile_ids[None, :]).astype(jnp.float32)
    col_hot = (cols[:, None] // TILE == tile_ids[None, :]).astype(jnp.float32)
    occ_rows = jnp.dot(row_hot, occ_float)
    marked = jnp.dot(occ_rows, col_hot.T) > 0.5
    return marked & (cols[None, :] <= rows[:, None])


def times_transposed(left, right):
    return lax.dot_general(
        left, right, (((1,), (1,)), ((), ())), preferred_element_type=jnp.float32
    )


def local(draws, factor, occupancy):
    rows_own = factor.shape[0]
    row_start = lax.axis_index("scen") * rows_own
    occ_float = occupancy.astype(jnp.float32)
    zero_value = jnp.zeros((), factor.dtype)
    whole = lax.all_gather(draws, "scen", axis=1, tiled=True)
    piece = lax.all_gather(factor, "blk", axis=1, tiled=True)
    count = piece.shape[1]
    keep = keep_mask(row_start, rows_own, count, occ_float)
    used = jnp.where(keep, piece, zero_value)
    result = times_transposed(whole, used)
    return result.astype(jnp.bfloat16)


def solution(mesh):
    return jax.shard_map(
        local,
        mesh=mesh,
        in_specs=(P("blk", "scen"), P("scen", "blk"), P()),
        out_specs=P("blk", "scen"),
        check_vma=False,
    )
```

profile of v0, /device:TPU:1, one launch (start us, length us, event | category | flops | bytes accessed | tf_op | source)
XLA Modules:
  0.0 305.0 jit_solution(14901550465227781415)
XLA Ops:
  6.5 0.0 all-gather.5.cloned.1.call-start
  6.5 0.7 all-gather.5.cloned.1.call-update
  7.3 0.0 all-gather.3.cloned.1.call-start
  7.3 0.7 all-gather.3.cloned.1.call-update
  8.0 0.9 fusion.7
  9.0 186.5 %all-gather.5.cloned.1.call-done = bf16[512,8192]{1,0:T(8,128)(2,1)} async-done(((bf16[512,512]{1,0:T(8,128)(2,1)}), bf16[512,8192]{1,0:T(8,128)(2,1)}) %all-gather.5.cloned.1.call-update) | async-done | bytes 8388624 | tf_op jit(solution)/shard_map/all_gather | solution.py:31
  195.4 89.2 %all-gather.3.cloned.1.call-done = bf16[512,8192]{1,0:T(8,128)(2,1)} async-done(((bf16[512,512]{1,0:T(8,128)(2,1)}), bf16[512,8192]{1,0:T(8,128)(2,1)}) %all-gather.3.cloned.1.call-update) | async-done | bytes 8388624 | tf_op jit(solution)/shard_map/all_gather | solution.py:32
  284.7 12.5 %fusion.4 = bf16[512,512]{0,1:T(8,128)(2,1)S(1)} fusion(bf16[512,8192]{1,0:T(8,128)(2,1)} %all-gather.5.cloned.1.call-done, bf16[512,8192]{1,0:T(8,128)(2,1)} %all-gather.3.cloned.1.call-done, bf16[512,16]{1,0:T(8,128)(2,1)S(1)} %fusion.7, s32[512]{0:T(512)S(1)} %get-tuple-element.6, s32[8192]{0:T(1024)S(1)} %add_select_fusion), kind=kOutput, calls=%fused_computation.5 | convolution fusion | flops 4446355456 | bytes 17352704 | tf_op jit(solution)/shard_map/dot_general | solution.py:21
  297.2 1.0 copy.5
  (2 shorter events, 0.0 us)
Async XLA Ops:
  6.5 188.9 %all-gather.5.cloned.1.call-start = ((), (), s32[]{:S(2)}) async-start(), calls=%async_computation.1 | async-start | bytes 8912896 | tf_op jit(solution)/shard_map/all_gather | solution.py:31
  7.3 277.4 %all-gather.3.cloned.1.call-start = ((), (), s32[]{:S(2)}) async-start(), calls=%async_computation | async-start | bytes 8912896 | tf_op jit(solution)/shard_map/all_gather | solution.py:32
Sparse Core Ops, SparseCore 0:
  9.1 186.2 all-gather.4
  198.0 86.6 all-gather.2
where the time goes:
time: 305 us
  waiting for transfers between devices  277 us (91%)
  matrix products  13.4 us (4%)
  between operations  13.4 us (4%)
    all_gather x1, waiting for transfers between devices, local(): whole = lax.all_gather(draws, 'scen', axis=1, tiled=True)  186 us
    all_gather x1, waiting for transfers between devices, local(): piece = lax.all_gather(factor, 'blk', axis=1, tiled=True)  89.2 us
    dot_general x1, matrix products, times_transposed(): lax.dot_general(left, right, (((1,), (1,)), ((), ())), preferred_element_...  12.5 us
  transfers between devices with their start and end apart: 2, of which 2 were waited for; matrix products, arithmetic and copies ran while one was open for 0% of the time, Pallas kernels for 0%

commit v1 on v0

v1 whole, which is shorter than its diff:
```python
import functools

import jax
import jax.numpy as jnp
from jax import lax
from jax.experimental import pallas as pl
from jax.experimental.pallas import tpu as pltpu
from jax.sharding import Mesh
from jax.sharding import PartitionSpec as P

TILE = 512
HALF = TILE // 2
OFFSETS = (0, -1, 1, 2)
SWAP = [(0, 0), (1, 2), (2, 1), (3, 3)]


def shift(count, by):
    return [(i, (i + by) % count) for i in range(count)]


def y_shift(by):
    pairs = []
    for y in range(4):
        to = (y + by) % 4
        pairs.append(((y % 2) * 2 + y // 2, (to % 2) * 2 + to // 2))
    return pairs


def send_x(piece, by):
    return lax.ppermute(piece, "x", shift(4, by))


def send_y(piece, by):
    return lax.ppermute(piece, ("yl", "yh"), y_shift(by))


def gather_ring(piece, send):
    half = piece.shape[0] // 2
    before = send(piece, 1)
    after = send(piece, -1)
    return piece, before, after, send(before[:half], 1), send(after[half:], -1)


def gather_plane(tile):
    top = jnp.concatenate(gather_ring(tile[:HALF], send_x), axis=0)
    low = jnp.concatenate(gather_ring(tile[HALF:], send_y), axis=0)
    return gather_ring(top, send_y), gather_ring(low, send_x)


def kernel(meta, draws, *refs):
    tops, lows = refs[:5], refs[5:10]
    keep, send, own, other = refs[10:]
    size = keep.shape[0]
    own[...] = jnp.zeros_like(own)
    other[...] = jnp.zeros_like(other)

    def add(total, column, row_at, ref, at, piece):
        flag = meta[piece]
        begin = pl.multiple_of(meta[16 + piece] * size, size)

        def step(tile):
            total[:, column : column + HALF] += lax.dot_general(
                draws[pl.ds(begin, size), :],
                tile,
                (((1,), (1,)), ((), ())),
                preferred_element_type=jnp.float32,
            )

        @pl.when(flag == 1)
        def _():
            step(ref[pl.ds(at, HALF), :])

        @pl.when(flag == 2)
        def _():
            tile = ref[pl.ds(at, HALF), :]
            rows = row_at + lax.broadcasted_iota(jnp.int32, tile.shape, 0)
            cols = lax.broadcasted_iota(jnp.int32, tile.shape, 1)
            step(jnp.where(cols <= rows, tile, jnp.zeros_like(tile)))

    for n, (first, count) in enumerate(((0, 4), (4, 4), (8, 4), (12, 2), (14, 2))):
        total = other if n in (1, 2) else own

        def body(k, carry, total=total, ref=tops[n], first=first):
            add(total, 0, 0, ref, pl.multiple_of(k * HALF, HALF), first + k)
            return carry

        lax.fori_loop(0, count, body, 0)
    for n, (ix, iy0, count) in enumerate(
        ((0, 0, 4), (1, 0, 4), (2, 0, 4), (3, 0, 2), (3, 2, 2))
    ):
        for k in range(count):
            iy = iy0 + k
            total = other if iy in (1, 2) else own
            add(total, HALF, HALF, lows[n], k * HALF, iy * 4 + ix)

    inside = meta[32] == 1

    @pl.when(inside)
    def _():
        keep[...] = own[...]
        send[...] = other[...]

    @pl.when(jnp.logical_not(inside))
    def _():
        keep[...] = other[...]
        send[...] = own[...]


def products(meta, draws, tops, lows, size):
    out = jax.ShapeDtypeStruct((size, TILE), jnp.float32)
    vmem = pl.BlockSpec(memory_space=pltpu.VMEM)
    return pl.pallas_call(
        kernel,
        out_shape=(out, out),
        in_specs=[pl.BlockSpec(memory_space=pltpu.SMEM)] + [vmem] * 11,
        out_specs=(vmem, vmem),
        scratch_shapes=[pltpu.VMEM((size, TILE), jnp.float32)] * 2,
        compiler_params=pltpu.CompilerParams(vmem_limit_bytes=48 * 1024 * 1024),
        name="products",
    )(meta, draws, *tops, *lows)


def describe(occupancy):
    z, yl, yh, x, c = (lax.axis_index(n) for n in ("z", "yl", "yh", "x", "c"))
    off = jnp.array(OFFSETS, jnp.int32)
    y_of = ((yh * 2 + yl + off) % 4)[:, None]
    x_of = ((x + off) % 4)[None, :]
    row = 2 * z + y_of % 2 + 0 * x_of
    block = (y_of // 2) * 4 + x_of
    column = 2 * block + c
    held = occupancy[row, column] == 1
    flags = jnp.where(held & (column <= row), jnp.where(column == row, 2, 1), 0)
    inside = (yl == c).astype(jnp.int32)
    return jnp.concatenate(
        [flags.reshape(-1), block.reshape(-1), inside[None]]
    ).astype(jnp.int32)


def local(draws, factor, occupancy):
    meta = describe(occupancy)
    swapped = lax.ppermute(draws, ("yl", "c"), SWAP)
    every = lax.all_gather(swapped, "z", axis=0, tiled=True)
    tops, lows = gather_plane(factor)
    keep, send = products(meta, every, tops, lows, TILE)
    total = keep + lax.ppermute(send, "c", shift(2, 1))
    return lax.ppermute(total.astype(jnp.bfloat16), ("yl", "c"), SWAP)


def solution(mesh):
    fine = Mesh(mesh.devices.reshape(8, 2, 2, 4, 2), ("z", "yl", "yh", "x", "c"))
    scen, blk = ("z", "yl"), ("yh", "x", "c")
    return jax.shard_map(
        local,
        mesh=fine,
        in_specs=(P(blk, scen), P(scen, blk), P()),
        out_specs=P(blk, scen),
        check_vma=False,
    )
```

time: 305 us -> 117 us (0.38)
  the two profiles are of different devices: /device:TPU:1 before, /device:TPU:225 now
where the time goes in v1:
time: 117 us
  waiting for transfers between devices  49.4 us (42%)
  starting transfers between devices  31.1 us (27%)
  local copies, waits for them, and re-layouts  14.1 us (12%)
  between operations  13.5 us (12%)
  Pallas kernels  8.33 us (7%)
    ppermute x8, waiting for transfers between devices, send_y(): return lax.ppermute(piece, ('yl', 'yh'), y_shift(by))  23.9 us
    pallas_call x1, Pallas kernels, products(): pl.pallas_call(kernel, out_shape=(out, out), in_specs=[pl.BlockSpec(memor...  8.33 us
    ppermute x8, starting transfers between devices, send_y(): return lax.ppermute(piece, ('yl', 'yh'), y_shift(by))  8.32 us
    ppermute x1, starting transfers between devices, local(): total = keep + lax.ppermute(send, 'c', shift(2, 1))  8.25 us
    ppermute x8, waiting for transfers between devices, send_x(): return lax.ppermute(piece, 'x', shift(4, by))  8.2 us
    ppermute x8, starting transfers between devices, send_x(): return lax.ppermute(piece, 'x', shift(4, by))  8.05 us
    ppermute x1, waiting for transfers between devices, local(): return lax.ppermute(total.astype(jnp.bfloat16), ('yl', 'c'), SWAP)  7.95 us
    ppermute x1, waiting for transfers between devices, local(): swapped = lax.ppermute(draws, ('yl', 'c'), SWAP)  7.06 us
  transfers between devices with their start and end apart: 20, of which 10 were waited for; matrix products, arithmetic and copies ran while one was open for 10% of the time, Pallas kernels for 0%

profile of v1, /device:TPU:225, one launch (start us, length us, event | category | flops | bytes accessed | tf_op | source)
XLA Modules:
  0.0 117.0 jit_solution(6583786834673363248)
XLA Ops:
  6.5 3.9 %collective-permute-start = (bf16[512,512]{1,0:T(8,128)(2,1)}, bf16[512,512]{1,0:T(8,128)(2,1)S(1)}, u32[]{:S(2)}, u32[]{:S(2)}) collective-permute-start(bf16[512,512]{1,0:T(8,128)(2,1)} %param.4), channel_id=1, source_target_pairs={{0,0},{1,16},{16,1},{17,17},{2,2},{3,18},{18,3},{19,19},{4,4},{5,2... | collective-permute-start | bytes 1572872 | tf_op jit(solution)/shard_map/ppermute | solution.py:141
  10.4 7.1 %collective-permute-done = bf16[512,512]{1,0:T(8,128)(2,1)S(1)} collective-permute-done((bf16[512,512]{1,0:T(8,128)(2,1)}, bf16[512,512]{1,0:T(8,128)(2,1)S(1)}, u32[]{:S(2)}, u32[]{:S(2)}) %collective-permute-start) | collective-permute-done | bytes 524320 | tf_op jit(solution)/shard_map/ppermute | solution.py:141
  17.5 0.8 copy-done.3
  18.3 0.0 all-gather.2.cloned.1.call-update
  18.3 1.8 %fusion.9 = (bf16[256,512]{1,0:T(8,128)(2,1)S(1)}, bf16[1024,512]{1,0:T(8,128)(2,1)S(1)}, bf16[1024,512]{1,0:T(8,128)(2,1)}, bf16[256,512]{1,0:T(8,128)(2,1)S(1)}) fusion(bf16[512,512]{1,0:T(8,128)(2,1)} %param.5), kind=kLoop, calls=%fused_computation.38 | loop fusion | bytes 1572864 | tf_op jit(solution)/shard_map/slice | solution.py:46
  20.2 1.5 %collective-permute-start.9 = (bf16[256,512]{1,0:T(8,128)(2,1)S(1)}, bf16[256,512]{1,0:T(8,128)(2,1)S(1)}, u32[]{:S(2)}, u32[]{:S(2)}) collective-permute-start(bf16[256,512]{1,0:T(8,128)(2,1)S(1)} %get-tuple-element.12), channel_id=1, source_target_pairs={{0,16},{16,8},{8,24},{24,0},{1,17},{17,9},{9,25},{25,1},{2,18},{18... | collective-permute-start | bytes 786440 | tf_op jit(solution)/shard_map/ppermute | solution.py:34
  21.6 2.5 %collective-permute-start.2 = (bf16[256,512]{1,0:T(8,128)(2,1)S(1)}, bf16[256,512]{1,0:T(8,128)(2,1)S(1)}, u32[]{:S(2)}, u32[]{:S(2)}) collective-permute-start(bf16[256,512]{1,0:T(8,128)(2,1)S(1)} %get-tuple-element.15), channel_id=1, source_target_pairs={{0,6},{2,0},{4,2},{6,4},{1,7},{3,1},{5,3},{7,5},{8,14},{10,8},{12,... | collective-permute-start | bytes 786440 | tf_op jit(solution)/shard_map/ppermute | solution.py:30
  24.1 3.9 %collective-permute-done.10 = bf16[256,512]{1,0:T(8,128)(2,1)S(1)} collective-permute-done((bf16[256,512]{1,0:T(8,128)(2,1)S(1)}, bf16[256,512]{1,0:T(8,128)(2,1)S(1)}, u32[]{:S(2)}, u32[]{:S(2)}) %collective-permute-start.10) | collective-permute-done | bytes 262176 | tf_op jit(solution)/shard_map/ppermute | solution.py:34
  28.0 1.1 collective-permute-start.12
  29.2 0.5 collective-permute-start.11
  29.6 2.6 %collective-permute-start.4 = (bf16[128,512]{1,0:T(8,128)(2,1)S(1)}, bf16[128,512]{1,0:T(8,128)(2,1)S(1)}, u32[]{:S(2)}, u32[]{:S(2)}) collective-permute-start(bf16[128,512]{1,0:T(8,128)(2,1)S(1)} %slice.43), channel_id=1, source_target_pairs={{0,6},{2,0},{4,2},{6,4},{1,7},{3,1},{5,3},{7,5},{8,14},{10,8},{12,... | collective-permute-start | bytes 393224 | tf_op jit(solution)/shard_map/ppermute | solution.py:30
  32.2 0.1 collective-permute-start.3
  32.3 0.8 constant_dynamic-update-slice_fusion.8
  33.1 0.7 constant_dynamic-update-slice_fusion.7
  33.8 3.9 %collective-permute-done.3 = bf16[128,512]{1,0:T(8,128)(2,1)S(1)} collective-permute-done((bf16[128,512]{1,0:T(8,128)(2,1)S(1)}, bf16[128,512]{1,0:T(8,128)(2,1)S(1)}, u32[]{:S(2)}, u32[]{:S(2)}) %collective-permute-start.3) | collective-permute-done | bytes 131104 | tf_op jit(solution)/shard_map/ppermute | solution.py:30
  37.8 2.4 %collective-permute-start.6 = (bf16[1024,512]{1,0:T(8,128)(2,1)S(1)}, bf16[1024,512]{1,0:T(8,128)(2,1)S(1)}, u32[]{:S(2)}, u32[]{:S(2)}) collective-permute-start(bf16[1024,512]{1,0:T(8,128)(2,1)S(1)} %constant_dynamic-update-slice_fusion.refs_0_), channel_id=1, source_target_pairs={{0,24},{16,0},{8,16},{24,8},{1,25},{17,1},{9,17},{25,9},{2,26},{18... | collective-permute-start | bytes 3145736 | tf_op jit(solution)/shard_map/ppermute | solution.py:34
  40.1 0.7 constant_dynamic-update-slice_fusion.6
  40.8 0.7 constant_dynamic-update-slice_fusion.5.refs_5_
  41.5 1.5 %collective-permute-start.13 = (bf16[1024,512]{1,0:T(8,128)(2,1)}, bf16[1024,512]{1,0:T(8,128)(2,1)}, u32[]{:S(2)}, u32[]{:S(2)}) collective-permute-start(bf16[1024,512]{1,0:T(8,128)(2,1)} %constant_dynamic-update-slice_fusion.5.refs_5_), channel_id=1, source_target_pairs={{0,2},{2,4},{4,6},{6,0},{1,3},{3,5},{5,7},{7,1},{8,10},{10,12},{12... | collective-permute-start | bytes 3145736 | tf_op jit(solution)/shard_map/ppermute | solution.py:30
  43.0 0.1 fusion.2
  43.1 0.1 reshape.161
  43.2 16.5 %collective-permute-done.6.refs_2_ = bf16[1024,512]{1,0:T(8,128)(2,1)S(1)} collective-permute-done((bf16[1024,512]{1,0:T(8,128)(2,1)S(1)}, bf16[1024,512]{1,0:T(8,128)(2,1)S(1)}, u32[]{:S(2)}, u32[]{:S(2)}) %collective-permute-start.6) | collective-permute-done | bytes 1048608 | tf_op jit(solution)/shard_map/ppermute | solution.py:34
  59.7 1.0 copy-done.1
  60.6 0.8 slice.45
  61.4 2.9 %collective-permute-start.8 = (bf16[512,512]{1,0:T(8,128)(2,1)}, bf16[512,512]{1,0:T(8,128)(2,1)S(1)}, u32[]{:S(2)}, u32[]{:S(2)}) collective-permute-start(bf16[512,512]{1,0:T(8,128)(2,1)} %slice.45), channel_id=1, source_target_pairs={{0,24},{16,0},{8,16},{24,8},{1,25},{17,1},{9,17},{25,9},{2,26},{18... | collective-permute-start | bytes 1572872 | tf_op jit(solution)/shard_map/ppermute | solution.py:34
  64.3 0.9 slice.44
  65.2 0.3 copy-done.2
  65.6 1.9 %slice.49 = bf16[512,512]{1,0:T(8,128)(2,1)} slice(bf16[1024,512]{1,0:T(8,128)(2,1)} %collective-permute-done.14.refs_7_), slice={[512:1024], [0:512]} | slice | bytes 1048576 | tf_op jit(solution)/shard_map/slice | solution.py:41
  67.5 0.2 collective-permute-start.16
  67.6 1.9 %slice.48 = bf16[512,512]{1,0:T(8,128)(2,1)} slice(bf16[1024,512]{1,0:T(8,128)(2,1)} %collective-permute-done.13.refs_6_), slice={[0:512], [0:512]} | slice | bytes 1048576 | tf_op jit(solution)/shard_map/slice | solution.py:41
  69.5 1.3 %collective-permute-start.15 = (bf16[512,512]{1,0:T(8,128)(2,1)}, bf16[512,512]{1,0:T(8,128)(2,1)S(1)}, u32[]{:S(2)}, u32[]{:S(2)}) collective-permute-start(bf16[512,512]{1,0:T(8,128)(2,1)} %slice.48), channel_id=1, source_target_pairs={{0,2},{2,4},{4,6},{6,0},{1,3},{3,5},{5,7},{7,1},{8,10},{10,12},{12... | collective-permute-start | bytes 1572872 | tf_op jit(solution)/shard_map/ppermute | solution.py:30
  70.8 0.1 broadcast_add_fusion
  70.9 0.1 add.143
  71.0 0.1 add.146
  71.0 0.1 add.147
  71.1 0.7 gather_fusion
  71.8 0.1 pad_add_fusion.meta
  71.9 0.7 collective-permute-done.8.refs_4_
  72.6 2.8 %collective-permute-done.7.refs_3_ = bf16[512,512]{1,0:T(8,128)(2,1)S(1)} collective-permute-done((bf16[512,512]{1,0:T(8,128)(2,1)}, bf16[512,512]{1,0:T(8,128)(2,1)S(1)}, u32[]{:S(2)}, u32[]{:S(2)}) %collective-permute-start.7) | collective-permute-done | bytes 524320 | tf_op jit(solution)/shard_map/ppermute | solution.py:34
  75.4 1.0 collective-permute-done.16.refs_9_
  76.4 3.3 %collective-permute-done.15.refs_8_ = bf16[512,512]{1,0:T(8,128)(2,1)S(1)} collective-permute-done((bf16[512,512]{1,0:T(8,128)(2,1)}, bf16[512,512]{1,0:T(8,128)(2,1)S(1)}, u32[]{:S(2)}, u32[]{:S(2)}) %collective-permute-start.15) | collective-permute-done | bytes 524320 | tf_op jit(solution)/shard_map/ppermute | solution.py:30
  79.7 8.3 %products.1 = (f32[512,512]{1,0:T(8,128)S(1)}, f32[512,512]{1,0:T(8,128)S(1)}) custom-call(s32[33]{0:T(128)S(1)} %pad_add_fusion.meta, bf16[4096,512]{1,0:T(8,128)(2,1)} %all-gather.2.cloned.1.call-done.draws, bf16[1024,512]{1,0:T(8,128)(2,1)S(1)} %constant_dynamic-update-slice_fusion.refs_0_, bf16[1024,512]{1,0:T(8,128)(2,1)} %copy-done.2, ...), custom_call_target="tpu_custom_call" | custom-call | tf_op jit(solution)/shard_map/products/pallas_call | solution.py:112
  88.0 8.3 %collective-permute-start.17 = (f32[512,512]{1,0:T(8,128)S(1)}, f32[512,512]{1,0:T(8,128)S(1)}, u32[]{:S(2)}, u32[]{:S(2)}) collective-permute-start(f32[512,512]{1,0:T(8,128)S(1)} %get-tuple-element.8), channel_id=1, source_target_pairs={{0,1},{1,0},{2,3},{3,2},{4,5},{5,4},{6,7},{7,6},{8,9},{9,8},{10,11... | collective-permute-start | bytes 3145736 | tf_op jit(solution)/shard_map/ppermute | solution.py:145
  96.3 2.3 %collective-permute-done.17 = f32[512,512]{1,0:T(8,128)S(1)} collective-permute-done((f32[512,512]{1,0:T(8,128)S(1)}, f32[512,512]{1,0:T(8,128)S(1)}, u32[]{:S(2)}, u32[]{:S(2)}) %collective-permute-start.17) | collective-permute-done | bytes 1048608 | tf_op jit(solution)/shard_map/ppermute | solution.py:145
  98.6 0.3 add_convert_fusion
  98.8 2.5 %collective-permute-start.18 = (bf16[512,512]{1,0:T(8,128)(2,1)S(1)}, bf16[512,512]{1,0:T(8,128)(2,1)S(1)}, u32[]{:S(2)}, u32[]{:S(2)}) collective-permute-start(bf16[512,512]{1,0:T(8,128)(2,1)S(1)} %add_convert_fusion), channel_id=1, source_target_pairs={{0,0},{1,16},{16,1},{17,17},{2,2},{3,18},{18,3},{19,19},{4,4},{5,2... | collective-permute-start | bytes 1572872 | tf_op jit(solution)/shard_map/ppermute | solution.py:146
  101.4 8.0 %collective-permute-done.18 = bf16[512,512]{1,0:T(8,128)(2,1)S(1)} collective-permute-done((bf16[512,512]{1,0:T(8,128)(2,1)S(1)}, bf16[512,512]{1,0:T(8,128)(2,1)S(1)}, u32[]{:S(2)}, u32[]{:S(2)}) %collective-permute-start.18) | collective-permute-done | bytes 524320 | tf_op jit(solution)/shard_map/ppermute | solution.py:146
  109.3 0.8 copy.14
  (35 shorter events, 0.2 us)
Async XLA Ops:
  6.5 64.6 %copy-start = (s32[16,16]{1,0:T(8,128)S(1)}, s32[16,16]{1,0:T(8,128)}, u32[]{:S(2)}) copy-start(s32[16,16]{1,0:T(8,128)} %param.6) | copy-start | bytes 3076
  6.5 36.4 %copy-start.4 = (s32[4]{0:T(128)S(1)}, s32[4]{0:T(128)}, u32[]{:S(2)}) copy-start(s32[4]{0:T(128)} %constant.75.clone) | copy-start | bytes 52
  6.5 73.2 %all-gather.2.cloned.1.call-start = ((), (), s32[]{:S(2)}) async-start(), calls=%async_computation | async-start | bytes 4718592 | tf_op jit(solution)/shard_map/all_gather | solution.py:142
  6.5 11.0 %collective-permute-start = (bf16[512,512]{1,0:T(8,128)(2,1)}, bf16[512,512]{1,0:T(8,128)(2,1)S(1)}, u32[]{:S(2)}, u32[]{:S(2)}) collective-permute-start(bf16[512,512]{1,0:T(8,128)(2,1)} %param.4), channel_id=1, source_target_pairs={{0,0},{1,16},{16,1},{17,17},{2,2},{3,18},{18,3},{19,19},{4,4},{5,2... | collective-permute-start | bytes 1572872 | tf_op jit(solution)/shard_map/ppermute | solution.py:141
  17.5 0.8 copy-start.3
  20.2 7.8 %collective-permute-start.10 = (bf16[256,512]{1,0:T(8,128)(2,1)S(1)}, bf16[256,512]{1,0:T(8,128)(2,1)S(1)}, u32[]{:S(2)}, u32[]{:S(2)}) collective-permute-start(bf16[256,512]{1,0:T(8,128)(2,1)S(1)} %get-tuple-element.12), channel_id=1, source_target_pairs={{0,24},{16,0},{8,16},{24,8},{1,25},{17,1},{9,17},{25,9},{2,26},{18... | collective-permute-start | bytes 786440 | tf_op jit(solution)/shard_map/ppermute | solution.py:34
  20.2 9.0 %collective-permute-start.9 = (bf16[256,512]{1,0:T(8,128)(2,1)S(1)}, bf16[256,512]{1,0:T(8,128)(2,1)S(1)}, u32[]{:S(2)}, u32[]{:S(2)}) collective-permute-start(bf16[256,512]{1,0:T(8,128)(2,1)S(1)} %get-tuple-element.12), channel_id=1, source_target_pairs={{0,16},{16,8},{8,24},{24,0},{1,17},{17,9},{9,25},{25,1},{2,18},{18... | collective-permute-start | bytes 786440 | tf_op jit(solution)/shard_map/ppermute | solution.py:34
  21.6 8.0 %collective-permute-start.2 = (bf16[256,512]{1,0:T(8,128)(2,1)S(1)}, bf16[256,512]{1,0:T(8,128)(2,1)S(1)}, u32[]{:S(2)}, u32[]{:S(2)}) collective-permute-start(bf16[256,512]{1,0:T(8,128)(2,1)S(1)} %get-tuple-element.15), channel_id=1, source_target_pairs={{0,6},{2,0},{4,2},{6,4},{1,7},{3,1},{5,3},{7,5},{8,14},{10,8},{12,... | collective-permute-start | bytes 786440 | tf_op jit(solution)/shard_map/ppermute | solution.py:30
  24.1 8.1 %collective-permute-start.1 = (bf16[256,512]{1,0:T(8,128)(2,1)S(1)}, bf16[256,512]{1,0:T(8,128)(2,1)S(1)}, u32[]{:S(2)}, u32[]{:S(2)}) collective-permute-start(bf16[256,512]{1,0:T(8,128)(2,1)S(1)} %get-tuple-element.15), channel_id=1, source_target_pairs={{0,2},{2,4},{4,6},{6,0},{1,3},{3,5},{5,7},{7,1},{8,10},{10,12},{12... | collective-permute-start | bytes 786440 | tf_op jit(solution)/shard_map/ppermute | solution.py:30
  28.0 12.8 %collective-permute-start.12 = (bf16[128,512]{1,0:T(8,128)(2,1)S(1)}, bf16[128,512]{1,0:T(8,128)(2,1)S(1)}, u32[]{:S(2)}, u32[]{:S(2)}) collective-permute-start(bf16[128,512]{1,0:T(8,128)(2,1)S(1)} %slice.47), channel_id=1, source_target_pairs={{0,24},{16,0},{8,16},{24,8},{1,25},{17,1},{9,17},{25,9},{2,26},{18... | collective-permute-start | bytes 393224 | tf_op jit(solution)/shard_map/ppermute | solution.py:34
  29.2 11.0 %collective-permute-start.11 = (bf16[128,512]{1,0:T(8,128)(2,1)S(1)}, bf16[128,512]{1,0:T(8,128)(2,1)S(1)}, u32[]{:S(2)}, u32[]{:S(2)}) collective-permute-start(bf16[128,512]{1,0:T(8,128)(2,1)S(1)} %slice.46), channel_id=1, source_target_pairs={{0,16},{16,8},{8,24},{24,0},{1,17},{17,9},{9,25},{25,1},{2,18},{18... | collective-permute-start | bytes 393224 | tf_op jit(solution)/shard_map/ppermute | solution.py:34
  29.6 8.1 %collective-permute-start.4 = (bf16[128,512]{1,0:T(8,128)(2,1)S(1)}, bf16[128,512]{1,0:T(8,128)(2,1)S(1)}, u32[]{:S(2)}, u32[]{:S(2)}) collective-permute-start(bf16[128,512]{1,0:T(8,128)(2,1)S(1)} %slice.43), channel_id=1, source_target_pairs={{0,6},{2,0},{4,2},{6,4},{1,7},{3,1},{5,3},{7,5},{8,14},{10,8},{12,... | collective-permute-start | bytes 393224 | tf_op jit(solution)/shard_map/ppermute | solution.py:30
  32.2 5.5 %collective-permute-start.3 = (bf16[128,512]{1,0:T(8,128)(2,1)S(1)}, bf16[128,512]{1,0:T(8,128)(2,1)S(1)}, u32[]{:S(2)}, u32[]{:S(2)}) collective-permute-start(bf16[128,512]{1,0:T(8,128)(2,1)S(1)} %slice.42), channel_id=1, source_target_pairs={{0,2},{2,4},{4,6},{6,0},{1,3},{3,5},{5,7},{7,1},{8,10},{10,12},{12... | collective-permute-start | bytes 393224 | tf_op jit(solution)/shard_map/ppermute | solution.py:30
  37.8 21.9 %collective-permute-start.6 = (bf16[1024,512]{1,0:T(8,128)(2,1)S(1)}, bf16[1024,512]{1,0:T(8,128)(2,1)S(1)}, u32[]{:S(2)}, u32[]{:S(2)}) collective-permute-start(bf16[1024,512]{1,0:T(8,128)(2,1)S(1)} %constant_dynamic-update-slice_fusion.refs_0_), channel_id=1, source_target_pairs={{0,24},{16,0},{8,16},{24,8},{1,25},{17,1},{9,17},{25,9},{2,26},{18... | collective-permute-start | bytes 3145736 | tf_op jit(solution)/shard_map/ppermute | solution.py:34
  40.1 24.2 %collective-permute-start.5 = (bf16[1024,512]{1,0:T(8,128)(2,1)S(1)}, bf16[1024,512]{1,0:T(8,128)(2,1)S(1)}, u32[]{:S(2)}, u32[]{:S(2)}) collective-permute-start(bf16[1024,512]{1,0:T(8,128)(2,1)S(1)} %constant_dynamic-update-slice_fusion.refs_0_), channel_id=1, source_target_pairs={{0,16},{16,8},{8,24},{24,0},{1,17},{17,9},{9,25},{25,1},{2,18},{18... | collective-permute-start | bytes 3145736 | tf_op jit(solution)/shard_map/ppermute | solution.py:34
  41.5 23.8 %collective-permute-start.14 = (bf16[1024,512]{1,0:T(8,128)(2,1)}, bf16[1024,512]{1,0:T(8,128)(2,1)}, u32[]{:S(2)}, u32[]{:S(2)}) collective-permute-start(bf16[1024,512]{1,0:T(8,128)(2,1)} %constant_dynamic-update-slice_fusion.5.refs_5_), channel_id=1, source_target_pairs={{0,6},{2,0},{4,2},{6,4},{1,7},{3,1},{5,3},{7,5},{8,14},{10,8},{12,... | collective-permute-start | bytes 3145736 | tf_op jit(solution)/shard_map/ppermute | solution.py:30
  41.5 26.2 %collective-permute-start.13 = (bf16[1024,512]{1,0:T(8,128)(2,1)}, bf16[1024,512]{1,0:T(8,128)(2,1)}, u32[]{:S(2)}, u32[]{:S(2)}) collective-permute-start(bf16[1024,512]{1,0:T(8,128)(2,1)} %constant_dynamic-update-slice_fusion.5.refs_5_), channel_id=1, source_target_pairs={{0,2},{2,4},{4,6},{6,0},{1,3},{3,5},{5,7},{7,1},{8,10},{10,12},{12... | collective-permute-start | bytes 3145736 | tf_op jit(solution)/shard_map/ppermute | solution.py:30
  59.6 1.0 copy-start.1
  61.4 11.2 %collective-permute-start.8 = (bf16[512,512]{1,0:T(8,128)(2,1)}, bf16[512,512]{1,0:T(8,128)(2,1)S(1)}, u32[]{:S(2)}, u32[]{:S(2)}) collective-permute-start(bf16[512,512]{1,0:T(8,128)(2,1)} %slice.45), channel_id=1, source_target_pairs={{0,24},{16,0},{8,16},{24,8},{1,25},{17,1},{9,17},{25,9},{2,26},{18... | collective-permute-start | bytes 1572872 | tf_op jit(solution)/shard_map/ppermute | solution.py:34
  64.3 1.3 %copy-start.2 = (bf16[1024,512]{1,0:T(8,128)(2,1)}, bf16[1024,512]{1,0:T(8,128)(2,1)S(1)}, u32[]{:S(2)}) copy-start(bf16[1024,512]{1,0:T(8,128)(2,1)S(1)} %collective-permute-done.5.refs_1_) | copy-start | bytes 3145732
  65.2 10.2 %collective-permute-start.7 = (bf16[512,512]{1,0:T(8,128)(2,1)}, bf16[512,512]{1,0:T(8,128)(2,1)S(1)}, u32[]{:S(2)}, u32[]{:S(2)}) collective-permute-start(bf16[512,512]{1,0:T(8,128)(2,1)} %slice.44), channel_id=1, source_target_pairs={{0,16},{16,8},{8,24},{24,0},{1,17},{17,9},{9,25},{25,1},{2,18},{18... | collective-permute-start | bytes 1572872 | tf_op jit(solution)/shard_map/ppermute | solution.py:34
  67.5 9.0 %collective-permute-start.16 = (bf16[512,512]{1,0:T(8,128)(2,1)}, bf16[512,512]{1,0:T(8,128)(2,1)S(1)}, u32[]{:S(2)}, u32[]{:S(2)}) collective-permute-start(bf16[512,512]{1,0:T(8,128)(2,1)} %slice.49), channel_id=1, source_target_pairs={{0,6},{2,0},{4,2},{6,4},{1,7},{3,1},{5,3},{7,5},{8,14},{10,8},{12,... | collective-permute-start | bytes 1572872 | tf_op jit(solution)/shard_map/ppermute | solution.py:30
  69.5 10.2 %collective-permute-start.15 = (bf16[512,512]{1,0:T(8,128)(2,1)}, bf16[512,512]{1,0:T(8,128)(2,1)S(1)}, u32[]{:S(2)}, u32[]{:S(2)}) collective-permute-start(bf16[512,512]{1,0:T(8,128)(2,1)} %slice.48), channel_id=1, source_target_pairs={{0,2},{2,4},{4,6},{6,0},{1,3},{3,5},{5,7},{7,1},{8,10},{10,12},{12... | collective-permute-start | bytes 1572872 | tf_op jit(solution)/shard_map/ppermute | solution.py:30
  88.0 10.5 %collective-permute-start.17 = (f32[512,512]{1,0:T(8,128)S(1)}, f32[512,512]{1,0:T(8,128)S(1)}, u32[]{:S(2)}, u32[]{:S(2)}) collective-permute-start(f32[512,512]{1,0:T(8,128)S(1)} %get-tuple-element.8), channel_id=1, source_target_pairs={{0,1},{1,0},{2,3},{3,2},{4,5},{5,4},{6,7},{7,6},{8,9},{9,8},{10,11... | collective-permute-start | bytes 3145736 | tf_op jit(solution)/shard_map/ppermute | solution.py:145
  98.8 10.5 %collective-permute-start.18 = (bf16[512,512]{1,0:T(8,128)(2,1)S(1)}, bf16[512,512]{1,0:T(8,128)(2,1)S(1)}, u32[]{:S(2)}, u32[]{:S(2)}) collective-permute-start(bf16[512,512]{1,0:T(8,128)(2,1)S(1)} %add_convert_fusion), channel_id=1, source_target_pairs={{0,0},{1,16},{16,1},{17,17},{2,2},{3,18},{18,3},{19,19},{4,4},{5,2... | collective-permute-start | bytes 1572872 | tf_op jit(solution)/shard_map/ppermute | solution.py:146
Sparse Core Ops, SparseCore 0:
  18.4 53.0 all-gather.1

commit v2 on v0

v2 whole, which is shorter than its diff:
```python
import jax
import jax.numpy as jnp
from jax import lax
from jax.experimental import pallas as pl
from jax.experimental.pallas import tpu as pltpu
from jax.sharding import Mesh
from jax.sharding import PartitionSpec as P

TILE = 512
PARTS = 2
OFFSETS = (0, -1, 1, 2)
PLANE = ("yl", "yh", "x", "c")
SWAP = [(0, 0), (1, 2), (2, 1), (3, 3)]


def plane_id(y, x, c):
    return (((y % 2) * 2 + y // 2) * 4 + x) * 2 + c


def send(piece, by, second):
    pairs = []
    for y in range(4):
        for x in range(4):
            for c in range(2):
                along_x = (c == 0) != second
                to = (y, (x + by) % 4) if along_x else ((y + by) % 4, x)
                pairs.append((plane_id(y, x, c), plane_id(*to, c)))
    return lax.ppermute(piece, PLANE, pairs)


def kernel(meta, draws, *refs):
    pieces, (keep, give, total) = refs[:8], refs[8:]
    total[...] = jnp.zeros_like(total)
    for n, ref in enumerate(pieces):

        def body(k, carry, n=n, ref=ref):
            piece = 2 * n + k

            @pl.when(meta[piece] == 1)
            def _():
                row = meta[32 + piece]
                total[row] += jnp.dot(
                    draws[meta[16 + piece]],
                    ref[pl.ds(pl.multiple_of(k * TILE, TILE), TILE), :],
                    preferred_element_type=jnp.float32,
                )

            return carry

        lax.fori_loop(0, 2, body, 0)
    mine = meta[48]
    keep[...] = total[mine]
    give[...] = total[1 - mine]


def products(meta, draws, pieces, part):
    size = TILE // PARTS
    out = jax.ShapeDtypeStruct((size, TILE), jnp.float32)
    whole = pl.BlockSpec(memory_space=pltpu.VMEM)
    return pl.pallas_call(
        kernel,
        grid=(1,),
        out_shape=(out, out),
        in_specs=[
            pl.BlockSpec(memory_space=pltpu.SMEM),
            pl.BlockSpec((8, size, TILE), lambda i: (0, part, 0)),
        ]
        + [whole] * 8,
        out_specs=(whole, whole),
        scratch_shapes=[pltpu.VMEM((2, size, TILE), jnp.float32)],
        compiler_params=pltpu.CompilerParams(vmem_limit_bytes=40 * 1024 * 1024),
        name="products",
    )(meta, draws, *pieces)


def describe(occupancy):
    z, yl, yh, x, c = (lax.axis_index(n) for n in ("z", "yl", "yh", "x", "c"))
    off = jnp.array(OFFSETS, jnp.int32)
    outer, inner = off[:, None], off[None, :]
    x_by = jnp.where(c == 0, inner, outer)
    y_by = jnp.where(c == 0, outer, inner)
    y_of, x_of = (yh * 2 + yl + y_by) % 4, (x + x_by) % 4
    row = y_of % 2
    block = (y_of // 2) * 4 + x_of
    held = (occupancy[2 * z + row, 2 * block + c] == 1).astype(jnp.int32)
    parts = [held.reshape(-1), block.reshape(-1), row.reshape(-1), c[None]]
    return jnp.concatenate(parts).astype(jnp.int32)


def masked(factor, occupancy):
    z, yl, yh, x, c = (lax.axis_index(n) for n in ("z", "yl", "yh", "x", "c"))
    row, column = 2 * z + yl, 8 * yh + 2 * x + c
    i = row * TILE + lax.broadcasted_iota(jnp.int32, factor.shape, 0)
    j = column * TILE + lax.broadcasted_iota(jnp.int32, factor.shape, 1)
    keep = (occupancy[row, column] == 1) & (j <= i)
    return jnp.where(keep, factor, jnp.zeros((), factor.dtype)).T


def local(draws, factor, occupancy):
    meta = describe(occupancy)
    swapped = lax.ppermute(draws, ("yl", "c"), SWAP)
    tile = masked(factor, occupancy)
    before, after = send(tile, 1, False), send(tile, -1, False)
    swapped, before, after = lax.optimization_barrier((swapped, before, after))
    every = lax.all_gather(swapped, "z", axis=0)
    half = TILE // 2
    across = [send(before[:half], 1, False), send(after[half:], -1, False)]
    first = jnp.concatenate([tile, before], axis=0)
    last = jnp.concatenate([after, *across], axis=0)
    first_b, first_a = send(first, 1, True), send(first, -1, True)
    last_b, last_a = send(last, 1, True), send(last, -1, True)
    first_o, last_o = send(first_b, 1, True), send(last_a, -1, True)
    pieces = [first, last, first_b, last_b, first_a, last_a, first_o, last_o]
    sums = []
    for part in range(PARTS):
        keep, give = products(meta, every, pieces, part)
        total = keep + lax.ppermute(give, "c", [(0, 1), (1, 0)])
        sums.append(lax.ppermute(total.astype(jnp.bfloat16), ("yl", "c"), SWAP))
    return jnp.concatenate(sums, axis=0)


def solution(mesh):
    fine = Mesh(mesh.devices.reshape(8, 2, 2, 4, 2), ("z", "yl", "yh", "x", "c"))
    scen, blk = ("z", "yl"), ("yh", "x", "c")
    return jax.shard_map(
        local,
        mesh=fine,
        in_specs=(P(blk, scen), P(scen, blk), P()),
        out_specs=P(blk, scen),
        check_vma=False,
    )
```

time: 305 us -> 110 us (0.36)
  waiting for transfers between devices: 277 us -> 56.2 us
  starting transfers between devices: 0.04 us -> 25.9 us
  matrix products: 13.4 us -> 0 us
  Pallas kernels: 0 us -> 6.36 us
  local copies, waits for them, and re-layouts: 1.01 us -> 5.77 us
    all_gather x2 -> x1, waiting for transfers between devices: 276 us -> 13.4 us  [local(): every = lax.all_gather(swapped, 'z', axis=0)]
    ppermute x0 -> x15, waiting for transfers between devices: none -> 42.8 us  [the longest x10 35.9 us: send(): return lax.ppermute(piece, PLANE, pairs)]
    ppermute x0 -> x15, starting transfers between devices: none -> 25.9 us  [the longest x10 14.7 us: send(): return lax.ppermute(piece, PLANE, pairs)]
    dot_general x2 -> x0, matrix products: 13.4 us -> none  [the longest x1 12.5 us: times_transposed(): lax.dot_general(left, right, (((1,), (1,)), ((), ())), preferred_element_...]
    pallas_call x0 -> x2, Pallas kernels: none -> 6.36 us  [products(): pl.pallas_call(kernel, grid=(1,), out_shape=(out, out), in_specs=[pl.Bloc...]
    unnamed x0 -> x15, local copies, waits for them, and re-layouts: none -> 3.52 us
  transfers between devices with their start and end apart: 2 -> 16, of which waited for: 2 -> 11; matrix products, arithmetic and copies ran while one was open for 0% -> 4% of each run, Pallas kernels for 0% -> 3%
where the time goes in v2:
time: 110 us
  waiting for transfers between devices  56.2 us (51%)
  starting transfers between devices  25.9 us (24%)
  between operations  14.3 us (13%)
  Pallas kernels  6.36 us (6%)
  local copies, waits for them, and re-layouts  5.77 us (5%)
  other arithmetic  1.65 us (2%)
    ppermute x10, waiting for transfers between devices, send(): return lax.ppermute(piece, PLANE, pairs)  35.9 us
    ppermute x10, starting transfers between devices, send(): return lax.ppermute(piece, PLANE, pairs)  14.7 us
    all_gather x1, waiting for transfers between devices, local(): every = lax.all_gather(swapped, 'z', axis=0)  13.4 us
    pallas_call x2, Pallas kernels, products(): pl.pallas_call(kernel, grid=(1,), out_shape=(out, out), in_specs=[pl.Bloc...  6.36 us
    ppermute x2, waiting for transfers between devices, local(): sums.append(lax.ppermute(total.astype(jnp.bfloat16), ('yl', 'c'), SWAP))  5.6 us
    ppermute x2, starting transfers between devices, local(): sums.append(lax.ppermute(total.astype(jnp.bfloat16), ('yl', 'c'), SWAP))  5.56 us
    ppermute x1, starting transfers between devices, local(): swapped = lax.ppermute(draws, ('yl', 'c'), SWAP)  4.58 us
    unnamed x15, local copies, waits for them, and re-layouts  3.52 us
  transfers between devices with their start and end apart: 16, of which 11 were waited for; matrix products, arithmetic and copies ran while one was open for 4% of the time, Pallas kernels for 3%

profile of v2, /device:TPU:1, one launch (start us, length us, event | category | flops | bytes accessed | tf_op | source)
XLA Modules:
  0.0 110.1 jit_solution(2271850999863528321)
XLA Ops:
  6.5 4.6 %collective-permute-start = (bf16[512,512]{1,0:T(8,128)(2,1)}, bf16[512,512]{1,0:T(8,128)(2,1)S(1)}, u32[]{:S(2)}, u32[]{:S(2)}) collective-permute-start(bf16[512,512]{1,0:T(8,128)(2,1)} %param.4), channel_id=1, source_target_pairs={{0,0},{1,16},{16,1},{17,17},{2,2},{3,18},{18,3},{19,19},{4,4},{5,2... | collective-permute-start | bytes 1572872 | tf_op jit(solution)/shard_map/ppermute | solution.py:101
  11.1 1.3 %copy.6 = bf16[512,512]{0,1:T(8,128)(2,1)S(1)} copy(bf16[512,512]{1,0:T(8,128)(2,1)} %param.5) | data formatting | bytes 1048576 | tf_op args[1]
  12.4 1.3 %dynamic_slice.3 = s32[1,1]{1,0:T(1,128)} dynamic-slice(s32[16,16]{1,0:T(8,128)} %param.6, s32[]{:T(128)S(6)} %select_n.154, s32[]{:T(128)S(6)} %select_n.155), dynamic_slice_sizes={1,1} | dynamic-slice | bytes 12 | tf_op jit(solution)/shard_map/dynamic_slice | solution.py:95
  14.3 0.3 fusion
  14.6 0.1 collective-permute-start.1
  14.7 2.7 %collective-permute-start.2 = (bf16[512,512]{1,0:T(8,128)(2,1)S(1)}, bf16[512,512]{1,0:T(8,128)(2,1)S(1)}, u32[]{:S(2)}, u32[]{:S(2)}) collective-permute-start(bf16[512,512]{1,0:T(8,128)(2,1)S(1)} %fusion), channel_id=1, source_target_pairs={{0,6},{1,25},{2,0},{3,27},{4,2},{5,29},{6,4},{7,31},{16,22},{17,1}... | collective-permute-start | bytes 1572872 | tf_op jit(solution)/shard_map/ppermute | solution.py:28
  17.4 1.2 %collective-permute-done = bf16[512,512]{1,0:T(8,128)(2,1)S(1)} collective-permute-done((bf16[512,512]{1,0:T(8,128)(2,1)}, bf16[512,512]{1,0:T(8,128)(2,1)S(1)}, u32[]{:S(2)}, u32[]{:S(2)}) %collective-permute-start) | collective-permute-done | bytes 524320 | tf_op jit(solution)/shard_map/ppermute | solution.py:101
  18.6 5.6 %collective-permute-done.1 = bf16[512,512]{1,0:T(8,128)(2,1)S(1)} collective-permute-done((bf16[512,512]{1,0:T(8,128)(2,1)S(1)}, bf16[512,512]{1,0:T(8,128)(2,1)S(1)}, u32[]{:S(2)}, u32[]{:S(2)}) %collective-permute-start.1) | collective-permute-done | bytes 524320 | tf_op jit(solution)/shard_map/ppermute | solution.py:28
  24.3 0.0 collective-permute-done.2
  24.3 0.0 all-gather.3.cloned.1.call-update
  24.3 0.9 collective-permute-start.3
  25.3 0.0 copy-start.5
  25.3 0.0 copy-start.1
  25.3 2.2 %collective-permute-start.4 = (bf16[256,512]{1,0:T(8,128)(2,1)S(1)}, bf16[256,512]{1,0:T(8,128)(2,1)S(1)}, u32[]{:S(2)}, u32[]{:S(2)}) collective-permute-start(bf16[256,512]{1,0:T(8,128)(2,1)S(1)} %slice.7), channel_id=1, source_target_pairs={{0,6},{1,25},{2,0},{3,27},{4,2},{5,29},{6,4},{7,31},{16,22},{17,1}... | collective-permute-start | bytes 786440 | tf_op jit(solution)/shard_map/ppermute | solution.py:28
  27.5 0.1 pad_maximum_fusion.refs_0_
  27.6 1.3 %collective-permute-start.5 = (bf16[1024,512]{1,0:T(8,128)(2,1)S(1)}, bf16[1024,512]{1,0:T(8,128)(2,1)S(1)}, u32[]{:S(2)}, u32[]{:S(2)}) collective-permute-start(bf16[1024,512]{1,0:T(8,128)(2,1)S(1)} %pad_maximum_fusion.refs_0_), channel_id=1, source_target_pairs={{0,16},{1,3},{2,18},{3,5},{4,20},{5,7},{6,22},{7,1},{16,8},{17,19}... | collective-permute-start | bytes 3145736 | tf_op jit(solution)/shard_map/ppermute | solution.py:28
  28.9 2.2 %collective-permute-done.3 = bf16[256,512]{1,0:T(8,128)(2,1)S(1)} collective-permute-done((bf16[256,512]{1,0:T(8,128)(2,1)S(1)}, bf16[256,512]{1,0:T(8,128)(2,1)S(1)}, u32[]{:S(2)}, u32[]{:S(2)}) %collective-permute-start.3) | collective-permute-done | bytes 262176 | tf_op jit(solution)/shard_map/ppermute | solution.py:28
  31.1 0.0 collective-permute-done.4
  31.2 2.6 %collective-permute-start.8 = (bf16[1024,512]{1,0:T(8,128)(2,1)S(1)}, bf16[1024,512]{1,0:T(8,128)(2,1)}, u32[]{:S(2)}, u32[]{:S(2)}) collective-permute-start(bf16[1024,512]{1,0:T(8,128)(2,1)S(1)} %constant_dynamic-update-slice_fusion.refs_1_), channel_id=1, source_target_pairs={{0,24},{1,7},{2,26},{3,1},{4,28},{5,3},{6,30},{7,5},{16,0},{17,23}... | collective-permute-start | bytes 3145736 | tf_op jit(solution)/shard_map/ppermute | solution.py:28
  33.7 0.2 collective-permute-start.7
  34.0 1.2 %collective-permute-start.6 = (bf16[1024,512]{1,0:T(8,128)(2,1)S(1)}, bf16[1024,512]{1,0:T(8,128)(2,1)}, u32[]{:S(2)}, u32[]{:S(2)}) collective-permute-start(bf16[1024,512]{1,0:T(8,128)(2,1)S(1)} %constant_dynamic-update-slice_fusion.refs_1_), channel_id=1, source_target_pairs={{0,16},{1,3},{2,18},{3,5},{4,20},{5,7},{6,22},{7,1},{16,8},{17,19}... | collective-permute-start | bytes 3145736 | tf_op jit(solution)/shard_map/ppermute | solution.py:28
  35.2 8.9 %collective-permute-done.5.refs_2_ = bf16[1024,512]{1,0:T(8,128)(2,1)S(1)} collective-permute-done((bf16[1024,512]{1,0:T(8,128)(2,1)S(1)}, bf16[1024,512]{1,0:T(8,128)(2,1)S(1)}, u32[]{:S(2)}, u32[]{:S(2)}) %collective-permute-start.5) | collective-permute-done | bytes 1048608 | tf_op jit(solution)/shard_map/ppermute | solution.py:28
  44.1 1.4 %collective-permute-done.8.refs_5_ = bf16[1024,512]{1,0:T(8,128)(2,1)} collective-permute-done((bf16[1024,512]{1,0:T(8,128)(2,1)S(1)}, bf16[1024,512]{1,0:T(8,128)(2,1)}, u32[]{:S(2)}, u32[]{:S(2)}) %collective-permute-start.8) | collective-permute-done | bytes 1048608 | tf_op jit(solution)/shard_map/ppermute | solution.py:28
  45.5 3.5 %collective-permute-start.10 = (bf16[1024,512]{1,0:T(8,128)(2,1)}, bf16[1024,512]{1,0:T(8,128)(2,1)}, u32[]{:S(2)}, u32[]{:S(2)}) collective-permute-start(bf16[1024,512]{1,0:T(8,128)(2,1)} %collective-permute-done.8.refs_5_), channel_id=1, source_target_pairs={{0,24},{1,7},{2,26},{3,1},{4,28},{5,3},{6,30},{7,5},{16,0},{17,23}... | collective-permute-start | bytes 3145736 | tf_op jit(solution)/shard_map/ppermute | solution.py:28
  49.0 0.1 select_add_fusion.1
  49.1 0.1 add.223
  49.2 0.1 add.219
  49.2 0.1 fusion.10
  49.3 0.1 reshape.312
  49.4 0.7 gather_fusion
  50.1 0.1 pad_add_fusion.meta
  50.2 6.5 %collective-permute-done.7.refs_4_ = bf16[1024,512]{1,0:T(8,128)(2,1)} collective-permute-done((bf16[1024,512]{1,0:T(8,128)(2,1)S(1)}, bf16[1024,512]{1,0:T(8,128)(2,1)}, u32[]{:S(2)}, u32[]{:S(2)}) %collective-permute-start.7) | collective-permute-done | bytes 1048608 | tf_op jit(solution)/shard_map/ppermute | solution.py:28
  56.7 9.8 %collective-permute-done.9.refs_6_ = bf16[1024,512]{1,0:T(8,128)(2,1)} collective-permute-done((bf16[1024,512]{1,0:T(8,128)(2,1)S(1)}, bf16[1024,512]{1,0:T(8,128)(2,1)}, u32[]{:S(2)}, u32[]{:S(2)}) %collective-permute-start.9) | collective-permute-done | bytes 1048608 | tf_op jit(solution)/shard_map/ppermute | solution.py:28
  66.6 1.5 %collective-permute-done.10.refs_7_ = bf16[1024,512]{1,0:T(8,128)(2,1)} collective-permute-done((bf16[1024,512]{1,0:T(8,128)(2,1)}, bf16[1024,512]{1,0:T(8,128)(2,1)}, u32[]{:S(2)}, u32[]{:S(2)}) %collective-permute-start.10) | collective-permute-done | bytes 1048608 | tf_op jit(solution)/shard_map/ppermute | solution.py:28
  68.1 13.4 %all-gather.3.cloned.1.call-done = bf16[4096,512]{1,0:T(8,128)(2,1)} async-done(((bf16[512,512]{1,0:T(8,128)(2,1)}), bf16[4096,512]{1,0:T(8,128)(2,1)}) %all-gather.3.cloned.1.call-update) | async-done | bytes 4194320 | tf_op jit(solution)/shard_map/all_gather | solution.py:105
  81.4 2.2 %copy-done = bf16[4096,512]{1,0:T(8,128)(2,1)S(1)} copy-done((bf16[4096,512]{1,0:T(8,128)(2,1)S(1)}, bf16[4096,512]{1,0:T(8,128)(2,1)}, u32[]{:S(2)}) %copy-start) | copy-done | bytes 4194328
  83.6 3.2 %products.3 = (f32[256,512]{1,0:T(8,128)S(1)}, f32[256,512]{1,0:T(8,128)S(1)}) custom-call(s32[49]{0:T(128)S(1)} %pad_add_fusion.meta, bf16[8,512,512]{2,1,0:T(8,128)(2,1)S(1)} %bitcast.7, bf16[1024,512]{1,0:T(8,128)(2,1)S(1)} %pad_maximum_fusion.refs_0_, bf16[1024,512]{1,0:T(8,128)(2,1)S(1)} %constant_dynamic-update-slice_fusion.refs_1_, ...), custom_call_target="tpu_custom_call" | custom-call | tf_op jit(solution)/shard_map/products/pallas_call | solution.py:60
  86.8 0.9 collective-permute-start.13
  87.8 3.2 %products.2 = (f32[256,512]{1,0:T(8,128)S(1)}, f32[256,512]{1,0:T(8,128)S(1)}) custom-call(s32[49]{0:T(128)S(1)} %pad_add_fusion.meta, bf16[8,512,512]{2,1,0:T(8,128)(2,1)S(1)} %bitcast.8, bf16[1024,512]{1,0:T(8,128)(2,1)S(1)} %pad_maximum_fusion.refs_0_, bf16[1024,512]{1,0:T(8,128)(2,1)S(1)} %constant_dynamic-update-slice_fusion.refs_1_, ...), custom_call_target="tpu_custom_call" | custom-call | tf_op jit(solution)/shard_map/products/pallas_call | solution.py:60
  90.9 0.1 collective-permute-start.11
  91.1 0.1 add_convert_fusion
  91.2 3.5 %collective-permute-start.14 = (bf16[256,512]{1,0:T(8,128)(2,1)S(1)}, bf16[256,512]{1,0:T(8,128)(2,1)S(1)}, u32[]{:S(2)}, u32[]{:S(2)}) collective-permute-start(bf16[256,512]{1,0:T(8,128)(2,1)S(1)} %add_convert_fusion), channel_id=1, source_target_pairs={{0,0},{1,16},{16,1},{17,17},{2,2},{3,18},{18,3},{19,19},{4,4},{5,2... | collective-permute-start | bytes 786440 | tf_op jit(solution)/shard_map/ppermute | solution.py:118
  94.7 0.0 collective-permute-done.11
  94.7 0.1 add_convert_fusion.1
  94.8 2.1 %collective-permute-start.12 = (bf16[256,512]{1,0:T(8,128)(2,1)S(1)}, bf16[256,512]{1,0:T(8,128)(2,1)S(1)}, u32[]{:S(2)}, u32[]{:S(2)}) collective-permute-start(bf16[256,512]{1,0:T(8,128)(2,1)S(1)} %add_convert_fusion.1), channel_id=1, source_target_pairs={{0,0},{1,16},{16,1},{17,17},{2,2},{3,18},{18,3},{19,19},{4,4},{5,2... | collective-permute-start | bytes 786440 | tf_op jit(solution)/shard_map/ppermute | solution.py:118
  96.8 2.0 %collective-permute-done.14 = bf16[256,512]{1,0:T(8,128)(2,1)S(1)} collective-permute-done((bf16[256,512]{1,0:T(8,128)(2,1)S(1)}, bf16[256,512]{1,0:T(8,128)(2,1)S(1)}, u32[]{:S(2)}, u32[]{:S(2)}) %collective-permute-start.14) | collective-permute-done | bytes 262176 | tf_op jit(solution)/shard_map/ppermute | solution.py:118
  98.9 3.6 %collective-permute-done.12 = bf16[256,512]{1,0:T(8,128)(2,1)S(1)} collective-permute-done((bf16[256,512]{1,0:T(8,128)(2,1)S(1)}, bf16[256,512]{1,0:T(8,128)(2,1)S(1)}, u32[]{:S(2)}, u32[]{:S(2)}) %collective-permute-start.12) | collective-permute-done | bytes 262176 | tf_op jit(solution)/shard_map/ppermute | solution.py:118
  102.5 0.8 pad_maximum_fusion.1
  (22 shorter events, 0.2 us)
Async XLA Ops:
  6.5 74.9 %all-gather.3.cloned.1.call-start = ((), (), s32[]{:S(2)}) async-start(), calls=%async_computation | async-start | bytes 4718592 | tf_op jit(solution)/shard_map/all_gather | solution.py:105
  6.5 12.1 %collective-permute-start = (bf16[512,512]{1,0:T(8,128)(2,1)}, bf16[512,512]{1,0:T(8,128)(2,1)S(1)}, u32[]{:S(2)}, u32[]{:S(2)}) collective-permute-start(bf16[512,512]{1,0:T(8,128)(2,1)} %param.4), channel_id=1, source_target_pairs={{0,0},{1,16},{16,1},{17,17},{2,2},{3,18},{18,3},{19,19},{4,4},{5,2... | collective-permute-start | bytes 1572872 | tf_op jit(solution)/shard_map/ppermute | solution.py:101
  14.6 9.6 %collective-permute-start.1 = (bf16[512,512]{1,0:T(8,128)(2,1)S(1)}, bf16[512,512]{1,0:T(8,128)(2,1)S(1)}, u32[]{:S(2)}, u32[]{:S(2)}) collective-permute-start(bf16[512,512]{1,0:T(8,128)(2,1)S(1)} %fusion), channel_id=1, source_target_pairs={{0,2},{1,17},{2,4},{3,19},{4,6},{5,21},{6,0},{7,23},{16,18},{17,9}... | collective-permute-start | bytes 1572872 | tf_op jit(solution)/shard_map/ppermute | solution.py:28
  14.7 9.5 %collective-permute-start.2 = (bf16[512,512]{1,0:T(8,128)(2,1)S(1)}, bf16[512,512]{1,0:T(8,128)(2,1)S(1)}, u32[]{:S(2)}, u32[]{:S(2)}) collective-permute-start(bf16[512,512]{1,0:T(8,128)(2,1)S(1)} %fusion), channel_id=1, source_target_pairs={{0,6},{1,25},{2,0},{3,27},{4,2},{5,29},{6,4},{7,31},{16,22},{17,1}... | collective-permute-start | bytes 1572872 | tf_op jit(solution)/shard_map/ppermute | solution.py:28
  18.6 5.6 %copy-start.4 = (bf16[512,512]{1,0:T(8,128)(2,1)}, bf16[512,512]{1,0:T(8,128)(2,1)S(1)}, u32[]{:S(2)}) copy-start(bf16[512,512]{1,0:T(8,128)(2,1)S(1)} %collective-permute-done) | copy-start | bytes 1572868
  24.3 1.0 copy-start.2
  24.3 6.8 %collective-permute-start.3 = (bf16[256,512]{1,0:T(8,128)(2,1)S(1)}, bf16[256,512]{1,0:T(8,128)(2,1)S(1)}, u32[]{:S(2)}, u32[]{:S(2)}) collective-permute-start(bf16[256,512]{1,0:T(8,128)(2,1)S(1)} %slice.6), channel_id=1, source_target_pairs={{0,2},{1,17},{2,4},{3,19},{4,6},{5,21},{6,0},{7,23},{16,18},{17,9}... | collective-permute-start | bytes 786440 | tf_op jit(solution)/shard_map/ppermute | solution.py:28
  25.3 23.7 %copy-start.5 = (s32[4]{0:T(128)S(1)}, s32[4]{0:T(128)}, u32[]{:S(2)}) copy-start(s32[4]{0:T(128)} %constant.87.clone) | copy-start | bytes 52
  25.3 24.1 %copy-start.1 = (s32[16,16]{1,0:T(8,128)S(1)}, s32[16,16]{1,0:T(8,128)}, u32[]{:S(2)}) copy-start(s32[16,16]{1,0:T(8,128)} %param.6) | copy-start | bytes 3076
  25.3 5.8 %collective-permute-start.4 = (bf16[256,512]{1,0:T(8,128)(2,1)S(1)}, bf16[256,512]{1,0:T(8,128)(2,1)S(1)}, u32[]{:S(2)}, u32[]{:S(2)}) collective-permute-start(bf16[256,512]{1,0:T(8,128)(2,1)S(1)} %slice.7), channel_id=1, source_target_pairs={{0,6},{1,25},{2,0},{3,27},{4,2},{5,29},{6,4},{7,31},{16,22},{17,1}... | collective-permute-start | bytes 786440 | tf_op jit(solution)/shard_map/ppermute | solution.py:28
  27.5 1.4 %copy-start.3 = (bf16[512,512]{1,0:T(8,128)(2,1)S(1)}, bf16[512,512]{1,0:T(8,128)(2,1)}, u32[]{:S(2)}) copy-start(bf16[512,512]{1,0:T(8,128)(2,1)} %copy-done.2) | copy-start | bytes 1572868
  27.6 16.5 %collective-permute-start.5 = (bf16[1024,512]{1,0:T(8,128)(2,1)S(1)}, bf16[1024,512]{1,0:T(8,128)(2,1)S(1)}, u32[]{:S(2)}, u32[]{:S(2)}) collective-permute-start(bf16[1024,512]{1,0:T(8,128)(2,1)S(1)} %pad_maximum_fusion.refs_0_), channel_id=1, source_target_pairs={{0,16},{1,3},{2,18},{3,5},{4,20},{5,7},{6,22},{7,1},{16,8},{17,19}... | collective-permute-start | bytes 3145736 | tf_op jit(solution)/shard_map/ppermute | solution.py:28
  31.2 14.3 %collective-permute-start.8 = (bf16[1024,512]{1,0:T(8,128)(2,1)S(1)}, bf16[1024,512]{1,0:T(8,128)(2,1)}, u32[]{:S(2)}, u32[]{:S(2)}) collective-permute-start(bf16[1024,512]{1,0:T(8,128)(2,1)S(1)} %constant_dynamic-update-slice_fusion.refs_1_), channel_id=1, source_target_pairs={{0,24},{1,7},{2,26},{3,1},{4,28},{5,3},{6,30},{7,5},{16,0},{17,23}... | collective-permute-start | bytes 3145736 | tf_op jit(solution)/shard_map/ppermute | solution.py:28
  33.7 23.0 %collective-permute-start.7 = (bf16[1024,512]{1,0:T(8,128)(2,1)S(1)}, bf16[1024,512]{1,0:T(8,128)(2,1)}, u32[]{:S(2)}, u32[]{:S(2)}) collective-permute-start(bf16[1024,512]{1,0:T(8,128)(2,1)S(1)} %pad_maximum_fusion.refs_0_), channel_id=1, source_target_pairs={{0,24},{1,7},{2,26},{3,1},{4,28},{5,3},{6,30},{7,5},{16,0},{17,23}... | collective-permute-start | bytes 3145736 | tf_op jit(solution)/shard_map/ppermute | solution.py:28
  34.0 22.8 %collective-permute-start.6 = (bf16[1024,512]{1,0:T(8,128)(2,1)S(1)}, bf16[1024,512]{1,0:T(8,128)(2,1)}, u32[]{:S(2)}, u32[]{:S(2)}) collective-permute-start(bf16[1024,512]{1,0:T(8,128)(2,1)S(1)} %constant_dynamic-update-slice_fusion.refs_1_), channel_id=1, source_target_pairs={{0,16},{1,3},{2,18},{3,5},{4,20},{5,7},{6,22},{7,1},{16,8},{17,19}... | collective-permute-start | bytes 3145736 | tf_op jit(solution)/shard_map/ppermute | solution.py:28
  44.1 22.5 %collective-permute-start.9 = (bf16[1024,512]{1,0:T(8,128)(2,1)S(1)}, bf16[1024,512]{1,0:T(8,128)(2,1)}, u32[]{:S(2)}, u32[]{:S(2)}) collective-permute-start(bf16[1024,512]{1,0:T(8,128)(2,1)S(1)} %collective-permute-done.5.refs_2_), channel_id=1, source_target_pairs={{0,16},{1,3},{2,18},{3,5},{4,20},{5,7},{6,22},{7,1},{16,8},{17,19}... | collective-permute-start | bytes 3145736 | tf_op jit(solution)/shard_map/ppermute | solution.py:28
  45.5 22.6 %collective-permute-start.10 = (bf16[1024,512]{1,0:T(8,128)(2,1)}, bf16[1024,512]{1,0:T(8,128)(2,1)}, u32[]{:S(2)}, u32[]{:S(2)}) collective-permute-start(bf16[1024,512]{1,0:T(8,128)(2,1)} %collective-permute-done.8.refs_5_), channel_id=1, source_target_pairs={{0,24},{1,7},{2,26},{3,1},{4,28},{5,3},{6,30},{7,5},{16,0},{17,23}... | collective-permute-start | bytes 3145736 | tf_op jit(solution)/shard_map/ppermute | solution.py:28
  81.4 2.2 %copy-start = (bf16[4096,512]{1,0:T(8,128)(2,1)S(1)}, bf16[4096,512]{1,0:T(8,128)(2,1)}, u32[]{:S(2)}) copy-start(bf16[4096,512]{1,0:T(8,128)(2,1)} %all-gather.3.cloned.1.call-done) | copy-start | bytes 12582916
  86.8 4.2 %collective-permute-start.13 = (f32[256,512]{1,0:T(8,128)S(1)}, f32[256,512]{1,0:T(8,128)S(1)}, u32[]{:S(2)}, u32[]{:S(2)}) collective-permute-start(f32[256,512]{1,0:T(8,128)S(1)} %get-tuple-element.18), channel_id=1, source_target_pairs={{0,1},{1,0},{2,3},{3,2},{4,5},{5,4},{6,7},{7,6},{8,9},{9,8},{10,11... | collective-permute-start | bytes 1572872 | tf_op jit(solution)/shard_map/ppermute | solution.py:117
  90.9 3.7 %collective-permute-start.11 = (f32[256,512]{1,0:T(8,128)S(1)}, f32[256,512]{1,0:T(8,128)S(1)}, u32[]{:S(2)}, u32[]{:S(2)}) collective-permute-start(f32[256,512]{1,0:T(8,128)S(1)} %get-tuple-element.16), channel_id=1, source_target_pairs={{0,1},{1,0},{2,3},{3,2},{4,5},{5,4},{6,7},{7,6},{8,9},{9,8},{10,11... | collective-permute-start | bytes 1572872 | tf_op jit(solution)/shard_map/ppermute | solution.py:117
  91.2 7.7 %collective-permute-start.14 = (bf16[256,512]{1,0:T(8,128)(2,1)S(1)}, bf16[256,512]{1,0:T(8,128)(2,1)S(1)}, u32[]{:S(2)}, u32[]{:S(2)}) collective-permute-start(bf16[256,512]{1,0:T(8,128)(2,1)S(1)} %add_convert_fusion), channel_id=1, source_target_pairs={{0,0},{1,16},{16,1},{17,17},{2,2},{3,18},{18,3},{19,19},{4,4},{5,2... | collective-permute-start | bytes 786440 | tf_op jit(solution)/shard_map/ppermute | solution.py:118
  94.8 7.7 %collective-permute-start.12 = (bf16[256,512]{1,0:T(8,128)(2,1)S(1)}, bf16[256,512]{1,0:T(8,128)(2,1)S(1)}, u32[]{:S(2)}, u32[]{:S(2)}) collective-permute-start(bf16[256,512]{1,0:T(8,128)(2,1)S(1)} %add_convert_fusion.1), channel_id=1, source_target_pairs={{0,0},{1,16},{16,1},{17,17},{2,2},{3,18},{18,3},{19,19},{4,4},{5,2... | collective-permute-start | bytes 786440 | tf_op jit(solution)/shard_map/ppermute | solution.py:118
Sparse Core Ops, SparseCore 0:
  24.4 56.9 all-gather.2

commit v3 on v0

v3 whole, which is shorter than its diff:
```python
import functools

import jax
import jax.numpy as jnp
from jax import lax
from jax.experimental import pallas as pl
from jax.experimental.pallas import tpu as pltpu
from jax.sharding import Mesh
from jax.sharding import PartitionSpec as P

TILE = 512
CODED = True
PARTS = 2
EXTRA = 16
LARGEST = 32000.0
COLUMN = ("yl", "yh", "c")


def column_id(yl, yh, c):
    return (yl * 2 + yh) * 2 + c


def to_parity(tile, across):
    pairs = []
    for yl in range(2):
        for yh in range(2):
            for c in range(2):
                to = yl if c == yl else 1 - yl
                pairs.append((column_id(yl, yh, c), column_id(to, yh ^ across, c if c == yl else yl)))
    return lax.ppermute(tile, COLUMN, pairs)


def shift(name, count, piece, by):
    return lax.ppermute(piece, name, [(i, (i + by) % count) for i in range(count)])


along_x = functools.partial(shift, "x", 4)
along_z = functools.partial(shift, "z", 8)


def other_core(piece):
    return shift("c", 2, piece, 1)


def other_chip(piece):
    return shift("yl", 2, piece, 1)


def add_up(meta, draws, own, other, total, first, begin, size):
    total[...] = jnp.zeros_like(total)
    for n in range(8):
        for which, ref in ((1, own[n]), (2, other[n])):

            @pl.when(meta[first + n] == which)
            def _(n=n, ref=ref):
                total[...] += jnp.dot(
                    draws[meta[16 + n], begin : begin + size, :],
                    ref[...],
                    preferred_element_type=jnp.float32,
                )


def give_kernel(begin, size, meta, draws, *refs):
    own, other, (out, total) = refs[:8], refs[8:16], refs[16:]
    add_up(meta, draws, own, other, total, 0, begin, size)
    if not CODED:
        out[...] = total[...]
        return
    sums = total[...]
    most = jnp.max(jnp.max(jnp.abs(sums), axis=1, keepdims=True), axis=0, keepdims=True)
    power = jnp.floor(jnp.log(LARGEST / jnp.maximum(most, 1e-30)) * 1.4426950)
    out[:size, :] = jnp.round(sums * jnp.exp2(power)).astype(jnp.int32).astype(jnp.int16)
    out[size:, :] = jnp.broadcast_to(power, (EXTRA, TILE)).astype(jnp.int32).astype(jnp.int16)


def keep_kernel(begin, size, meta, draws, *refs):
    own, other, (out, total) = refs[:8], refs[8:16], refs[16:]
    add_up(meta, draws, own, other, total, 8, begin, size)
    out[...] = total[...]


def products(kernel, meta, draws, own, other, begin, size, out):
    whole = pl.BlockSpec(memory_space=pltpu.VMEM)
    return pl.pallas_call(
        functools.partial(kernel, begin, size),
        out_shape=out,
        in_specs=[pl.BlockSpec(memory_space=pltpu.SMEM)] + [whole] * 17,
        out_specs=whole,
        scratch_shapes=[pltpu.VMEM((size, TILE), jnp.float32)],
        compiler_params=pltpu.CompilerParams(vmem_limit_bytes=40 * 1024 * 1024),
        name=kernel.__name__,
    )(meta, draws, *own, *other)


def describe(occupancy):
    z, yl, yh, x, c = (lax.axis_index(n) for n in ("z", "yl", "yh", "x", "c"))
    off = jnp.array((0, 0, -1, -1, 1, 1, 2, 2), jnp.int32)
    flip = jnp.array((0, 1, 0, 1, 0, 1, 0, 1), jnp.int32)
    block = (yh ^ flip) * 4 + (x + off) % 4

    def held(row):
        where = jnp.where(row == c, 1, 2)
        return jnp.where(occupancy[2 * z + row, 2 * block + yl] == 1, where, 0)

    return jnp.concatenate([held(1 - yl), held(yl), (z - block) % 8]).astype(jnp.int32)


def masked(factor, occupancy):
    z, yl, yh, x, c = (lax.axis_index(n) for n in ("z", "yl", "yh", "x", "c"))
    row, column = 2 * z + yl, 8 * yh + 2 * x + c
    i = row * TILE + lax.broadcasted_iota(jnp.int32, factor.shape, 0)
    j = column * TILE + lax.broadcasted_iota(jnp.int32, factor.shape, 1)
    keep = (occupancy[row, column] == 1) & (j <= i)
    return jnp.where(keep, factor, jnp.zeros((), factor.dtype)).T


def local(draws, factor, occupancy):
    meta = describe(occupancy)
    tile = masked(factor, occupancy)
    near, far = to_parity(tile, 0), to_parity(tile, 1)
    up, down = [draws], [draws]
    for step in range(4):
        up.append(along_z(up[-1], 1))
        if step < 3:
            down.append(along_z(down[-1], -1))
    every = jnp.stack(up + down[:0:-1])
    near_b, far_a = along_x(near, 1), along_x(far, -1)
    far_b, near_a = along_x(far, 1), along_x(near, -1)
    near_o, far_o = along_x(near_b, 1), along_x(far_a, -1)
    own = [near, far, near_b, far_b, near_a, far_a, near_o, far_o]
    other = [other_core(piece) for piece in own]
    size = TILE // PARTS
    crossed = []
    for part in range(PARTS):
        if CODED:
            out = jax.ShapeDtypeStruct((size + EXTRA, TILE), jnp.int16)
        else:
            out = jax.ShapeDtypeStruct((size, TILE), jnp.float32)
        give = products(give_kernel, meta, every, own, other, part * size, size, out)
        crossed.append(other_chip(give))
    out = jax.ShapeDtypeStruct((TILE, TILE), jnp.float32)
    keep = products(keep_kernel, meta, every, own, other, 0, TILE, out)
    sums = []
    for part, sent in enumerate(crossed):
        if CODED:
            power = sent[size, 0].astype(jnp.float32)
            sent = sent[:size].astype(jnp.float32) * jnp.exp2(-power)
        sums.append((keep[part * size : (part + 1) * size] + sent).astype(jnp.bfloat16))
    return jnp.concatenate(sums, axis=0)


def solution(mesh):
    fine = Mesh(mesh.devices.reshape(8, 2, 2, 4, 2), ("z", "yl", "yh", "x", "c"))
    scen, blk = ("z", "yl"), ("yh", "x", "c")
    return jax.shard_map(
        local,
        mesh=fine,
        in_specs=(P(blk, scen), P(scen, blk), P()),
        out_specs=P(blk, scen),
        check_vma=False,
    )
```

time: 305 us -> 99.3 us (0.33)
  waiting for transfers between devices: 277 us -> 36.8 us
  starting transfers between devices: 0.04 us -> 43.4 us
  matrix products: 13.4 us -> 0 us
  between operations: 13.4 us -> 2.25 us
  local copies, waits for them, and re-layouts: 1.01 us -> 9.74 us
    all_gather x2 -> x0, waiting for transfers between devices: 276 us -> none  [the longest x1 186 us: local(): whole = lax.all_gather(draws, 'scen', axis=1, tiled=True)]
    ppermute x0 -> x25, starting transfers between devices: none -> 43.4 us  [the longest x23 35.5 us: shift(): lax.ppermute(piece, name, [(i, (i + by) % count) for i in range(count)])]
    ppermute x0 -> x25, waiting for transfers between devices: none -> 36.8 us  [the longest x23 36.8 us: shift(): lax.ppermute(piece, name, [(i, (i + by) % count) for i in range(count)])]
    dot_general x2 -> x0, matrix products: 13.4 us -> none  [the longest x1 12.5 us: times_transposed(): lax.dot_general(left, right, (((1,), (1,)), ((), ())), preferred_element_...]
    unnamed x0 -> x8, local copies, waits for them, and re-layouts: none -> 4.63 us
  transfers between devices with their start and end apart: 2 -> 25, of which waited for: 2 -> 11; matrix products, arithmetic and copies ran while one was open for 0% -> 11% of each run, Pallas kernels for 0% -> 2%
where the time goes in v3:
time: 99.3 us; the launch traced here: 98.2 us
  starting transfers between devices  43.4 us (44%)
  waiting for transfers between devices  36.8 us (37%)
  local copies, waits for them, and re-layouts  9.74 us (10%)
  Pallas kernels  3 us (3%)
  other arithmetic  2.94 us (3%)
  between operations  2.25 us (2%)
    ppermute x23, waiting for transfers between devices, shift(): lax.ppermute(piece, name, [(i, (i + by) % count) for i in range(count)])  36.8 us
    ppermute x23, starting transfers between devices, shift(): lax.ppermute(piece, name, [(i, (i + by) % count) for i in range(count)])  35.5 us
    ppermute x2, starting transfers between devices, to_parity(): return lax.ppermute(tile, COLUMN, pairs)  7.88 us
    unnamed x8, local copies, waits for them, and re-layouts  4.63 us
    pallas_call x3, Pallas kernels, products(): pl.pallas_call(functools.partial(kernel, begin, size), out_shape=out, in_...  3 us
    gather x2, local copies, waits for them, and re-layouts, held(): return jnp.where(occupancy[2 * z + row, 2 * block + yl] == 1, where, 0)  2.69 us
  transfers between devices with their start and end apart: 25, of which 11 were waited for; matrix products, arithmetic and copies ran while one was open for 11% of the time, Pallas kernels for 2%

profile of v3, /device:TPU:1, one launch (start us, length us, event | category | flops | bytes accessed | tf_op | source)
XLA Modules:
  0.0 98.2 jit_solution(9004968518565585600)
XLA Ops:
  0.0 2.5 %collective-permute-start = (bf16[512,512]{1,0:T(8,128)(2,1)}, bf16[512,512]{1,0:T(8,128)(2,1)S(1)}, u32[]{:S(2)}, u32[]{:S(2)}) collective-permute-start(bf16[512,512]{1,0:T(8,128)(2,1)} %param.5), channel_id=1, source_target_pairs={{0,32},{32,64},{64,96},{96,128},{128,160},{160,192},{192,224},{224... | collective-permute-start | bytes 1572872 | tf_op jit(solution)/shard_map/ppermute | solution.py:34
  2.5 3.9 %collective-permute-start.4 = (bf16[512,512]{1,0:T(8,128)(2,1)}, bf16[512,512]{1,0:T(8,128)(2,1)S(1)}, u32[]{:S(2)}, u32[]{:S(2)}) collective-permute-start(bf16[512,512]{1,0:T(8,128)(2,1)} %param.5), channel_id=1, source_target_pairs={{0,224},{32,0},{64,32},{96,64},{128,96},{160,128},{192,160},{224,1... | collective-permute-start | bytes 1572872 | tf_op jit(solution)/shard_map/ppermute | solution.py:34
  6.4 1.3 %copy.7 = bf16[512,512]{0,1:T(8,128)(2,1)S(1)} copy(bf16[512,512]{1,0:T(8,128)(2,1)} %param.6) | data formatting | bytes 1048576 | tf_op args[1]
  7.7 1.3 %dynamic_slice.3 = s32[1,1]{1,0:T(1,128)} dynamic-slice(s32[16,16]{1,0:T(8,128)} %param.7, s32[]{:T(128)S(6)} %select_n.48, s32[]{:T(128)S(6)} %select_n.52), dynamic_slice_sizes={1,1} | dynamic-slice | bytes 12 | tf_op jit(solution)/shard_map/dynamic_slice | solution.py:113
  9.6 1.1 %fusion = bf16[512,512]{1,0:T(8,128)(2,1)} fusion(bf16[512,512]{0,1:T(8,128)(2,1)S(1)} %copy.7, s32[512]{0:T(512)S(1)} %get-tuple-element.12, s32[512]{0:T(512)S(1)} %get-tuple-element.13, pred[]{:T(512)} %bitcast.8), kind=kLoop, calls=%fused_computation.3 | loop fusion | flops 786432 | bytes 1052673 | tf_op jit(solution)/shard_map/transpose | solution.py:114
  10.7 4.0 %collective-permute-start.7 = (bf16[512,512]{1,0:T(8,128)(2,1)}, bf16[512,512]{1,0:T(8,128)(2,1)S(1)}, u32[]{:S(2)}, u32[]{:S(2)}) collective-permute-start(bf16[512,512]{1,0:T(8,128)(2,1)} %fusion), channel_id=1, source_target_pairs={{0,0},{1,16},{8,8},{9,24},{16,1},{17,17},{24,9},{25,25},{2,2},{3,1... | collective-permute-start | bytes 1572872 | tf_op jit(solution)/shard_map/ppermute | solution.py:30
  14.7 3.5 %collective-permute-done = bf16[512,512]{1,0:T(8,128)(2,1)S(1)} collective-permute-done((bf16[512,512]{1,0:T(8,128)(2,1)}, bf16[512,512]{1,0:T(8,128)(2,1)S(1)}, u32[]{:S(2)}, u32[]{:S(2)}) %collective-permute-start) | collective-permute-done | bytes 524320 | tf_op jit(solution)/shard_map/ppermute | solution.py:34
  18.3 3.8 %collective-permute-start.8 = (bf16[512,512]{1,0:T(8,128)(2,1)}, bf16[512,512]{1,0:T(8,128)(2,1)S(1)}, u32[]{:S(2)}, u32[]{:S(2)}) collective-permute-start(bf16[512,512]{1,0:T(8,128)(2,1)} %fusion), channel_id=1, source_target_pairs={{0,8},{1,24},{8,0},{9,16},{16,9},{17,25},{24,1},{25,17},{2,10},{3,... | collective-permute-start | bytes 1572872 | tf_op jit(solution)/shard_map/ppermute | solution.py:30
  22.1 0.7 broadcast_or_fusion.1
  22.8 3.0 %collective-permute-start.5 = (bf16[512,512]{1,0:T(8,128)(2,1)S(1)}, bf16[512,512]{1,0:T(8,128)(2,1)S(1)}, u32[]{:S(2)}, u32[]{:S(2)}) collective-permute-start(bf16[512,512]{1,0:T(8,128)(2,1)S(1)} %collective-permute-done.4), channel_id=1, source_target_pairs={{0,224},{32,0},{64,32},{96,64},{128,96},{160,128},{192,160},{224,1... | collective-permute-start | bytes 1572872 | tf_op jit(solution)/shard_map/ppermute | solution.py:34
  25.8 1.2 %collective-permute-start.9 = (bf16[512,512]{1,0:T(8,128)(2,1)S(1)}, bf16[512,512]{1,0:T(8,128)(2,1)S(1)}, u32[]{:S(2)}, u32[]{:S(2)}) collective-permute-start(bf16[512,512]{1,0:T(8,128)(2,1)S(1)} %collective-permute-done.7.refs_0_), channel_id=1, source_target_pairs={{0,2},{2,4},{4,6},{6,0},{1,3},{3,5},{5,7},{7,1},{8,10},{10,12},{12... | collective-permute-start | bytes 1572872 | tf_op jit(solution)/shard_map/ppermute | solution.py:34
  27.1 4.7 %collective-permute-done.1 = bf16[512,512]{1,0:T(8,128)(2,1)} collective-permute-done((bf16[512,512]{1,0:T(8,128)(2,1)S(1)}, bf16[512,512]{1,0:T(8,128)(2,1)}, u32[]{:S(2)}, u32[]{:S(2)}) %collective-permute-start.1) | collective-permute-done | bytes 524320 | tf_op jit(solution)/shard_map/ppermute | solution.py:34
  31.8 1.3 %gather_fusion.1 = s32[8]{0:T(128)S(1)} fusion(s32[16,16]{1,0:T(8,128)} %param.7, s32[8]{0:T(128)S(1)} %broadcast_or_fusion), kind=kCustom, calls=%fused_computation.1 | custom fusion | bytes 128 | tf_op jit(solution)/shard_map/gather | solution.py:103
  33.1 1.4 %gather_fusion = s32[8]{0:T(128)S(1)} fusion(s32[16,16]{1,0:T(8,128)} %param.7, s32[8]{0:T(128)S(1)} %get-tuple-element.5), kind=kCustom, calls=%fused_computation | custom fusion | bytes 128 | tf_op jit(solution)/shard_map/gather | solution.py:103
  34.5 2.6 %collective-permute-start.11 = (bf16[512,512]{1,0:T(8,128)(2,1)S(1)}, bf16[512,512]{1,0:T(8,128)(2,1)S(1)}, u32[]{:S(2)}, u32[]{:S(2)}) collective-permute-start(bf16[512,512]{1,0:T(8,128)(2,1)S(1)} %collective-permute-done.7.refs_0_), channel_id=1, source_target_pairs={{0,6},{2,0},{4,2},{6,4},{1,7},{3,1},{5,3},{7,5},{8,14},{10,8},{12,... | collective-permute-start | bytes 1572872 | tf_op jit(solution)/shard_map/ppermute | solution.py:34
  37.1 2.7 %collective-permute-start.12 = (bf16[512,512]{1,0:T(8,128)(2,1)S(1)}, bf16[512,512]{1,0:T(8,128)(2,1)S(1)}, u32[]{:S(2)}, u32[]{:S(2)}) collective-permute-start(bf16[512,512]{1,0:T(8,128)(2,1)S(1)} %collective-permute-done.8.refs_1_), channel_id=1, source_target_pairs={{0,6},{2,0},{4,2},{6,4},{1,7},{3,1},{5,3},{7,5},{8,14},{10,8},{12,... | collective-permute-start | bytes 1572872 | tf_op jit(solution)/shard_map/ppermute | solution.py:34
  39.7 0.0 collective-permute-done.9.refs_2_
  39.8 3.0 %collective-permute-start.15 = (bf16[512,512]{1,0:T(8,128)(2,1)S(1)}, bf16[512,512]{1,0:T(8,128)(2,1)S(1)}, u32[]{:S(2)}, u32[]{:S(2)}) collective-permute-start(bf16[512,512]{1,0:T(8,128)(2,1)S(1)} %collective-permute-done.7.refs_0_), channel_id=1, source_target_pairs={{0,1},{1,0},{2,3},{3,2},{4,5},{5,4},{6,7},{7,6},{8,9},{9,8},{10,11... | collective-permute-start | bytes 1572872 | tf_op jit(solution)/shard_map/ppermute | solution.py:34
  42.7 1.8 %collective-permute-done.2 = bf16[512,512]{1,0:T(8,128)(2,1)} collective-permute-done((bf16[512,512]{1,0:T(8,128)(2,1)}, bf16[512,512]{1,0:T(8,128)(2,1)}, u32[]{:S(2)}, u32[]{:S(2)}) %collective-permute-start.2) | collective-permute-done | bytes 524320 | tf_op jit(solution)/shard_map/ppermute | solution.py:34
  44.6 0.1 pad_add_fusion.meta
  44.6 1.1 %bitcast_dynamic-update-slice_fusion.7 = bf16[8,512,512]{2,1,0:T(8,128)(2,1)S(1)} fusion(bf16[512,512]{1,0:T(8,128)(2,1)} %param.5), kind=kLoop, calls=%fused_computation.16 | loop fusion | bytes 1048576
  45.8 3.5 %collective-permute-done.10.refs_3_ = bf16[512,512]{1,0:T(8,128)(2,1)S(1)} collective-permute-done((bf16[512,512]{1,0:T(8,128)(2,1)S(1)}, bf16[512,512]{1,0:T(8,128)(2,1)S(1)}, u32[]{:S(2)}, u32[]{:S(2)}) %collective-permute-start.10) | collective-permute-done | bytes 524320 | tf_op jit(solution)/shard_map/ppermute | solution.py:34
  49.3 3.3 %collective-permute-start.16 = (bf16[512,512]{1,0:T(8,128)(2,1)S(1)}, bf16[512,512]{1,0:T(8,128)(2,1)S(1)}, u32[]{:S(2)}, u32[]{:S(2)}) collective-permute-start(bf16[512,512]{1,0:T(8,128)(2,1)S(1)} %collective-permute-done.8.refs_1_), channel_id=1, source_target_pairs={{0,1},{1,0},{2,3},{3,2},{4,5},{5,4},{6,7},{7,6},{8,9},{9,8},{10,11... | collective-permute-start | bytes 1572872 | tf_op jit(solution)/shard_map/ppermute | solution.py:34
  52.6 4.7 %collective-permute-done.12.refs_5_ = bf16[512,512]{1,0:T(8,128)(2,1)S(1)} collective-permute-done((bf16[512,512]{1,0:T(8,128)(2,1)S(1)}, bf16[512,512]{1,0:T(8,128)(2,1)S(1)}, u32[]{:S(2)}, u32[]{:S(2)}) %collective-permute-start.12) | collective-permute-done | bytes 524320 | tf_op jit(solution)/shard_map/ppermute | solution.py:34
  57.4 3.1 %collective-permute-start.17 = (bf16[512,512]{1,0:T(8,128)(2,1)S(1)}, bf16[512,512]{1,0:T(8,128)(2,1)S(1)}, u32[]{:S(2)}, u32[]{:S(2)}) collective-permute-start(bf16[512,512]{1,0:T(8,128)(2,1)S(1)} %collective-permute-done.9.refs_2_), channel_id=1, source_target_pairs={{0,1},{1,0},{2,3},{3,2},{4,5},{5,4},{6,7},{7,6},{8,9},{9,8},{10,11... | collective-permute-start | bytes 1572872 | tf_op jit(solution)/shard_map/ppermute | solution.py:34
  60.4 2.7 %collective-permute-start.6 = (bf16[512,512]{1,0:T(8,128)(2,1)S(1)}, bf16[512,512]{1,0:T(8,128)(2,1)S(1)}, u32[]{:S(2)}, u32[]{:S(2)}) collective-permute-start(bf16[512,512]{1,0:T(8,128)(2,1)S(1)} %collective-permute-done.5), channel_id=1, source_target_pairs={{0,224},{32,0},{64,32},{96,64},{128,96},{160,128},{192,160},{224,1... | collective-permute-start | bytes 1572872 | tf_op jit(solution)/shard_map/ppermute | solution.py:34
  63.1 3.4 %collective-permute-start.14 = (bf16[512,512]{1,0:T(8,128)(2,1)S(1)}, bf16[512,512]{1,0:T(8,128)(2,1)S(1)}, u32[]{:S(2)}, u32[]{:S(2)}) collective-permute-start(bf16[512,512]{1,0:T(8,128)(2,1)S(1)} %collective-permute-done.12.refs_5_), channel_id=1, source_target_pairs={{0,6},{2,0},{4,2},{6,4},{1,7},{3,1},{5,3},{7,5},{8,14},{10,8},{12,... | collective-permute-start | bytes 1572872 | tf_op jit(solution)/shard_map/ppermute | solution.py:34
  66.5 1.1 %bitcast_dynamic-update-slice_fusion.5 = bf16[8,512,512]{2,1,0:T(8,128)(2,1)S(1)} fusion(bf16[8,512,512]{2,1,0:T(8,128)(2,1)S(1)} %bitcast_dynamic-update-slice_fusion.6, bf16[512,512]{1,0:T(8,128)(2,1)} %collective-permute-done.1), kind=kLoop, calls=%fused_computation.14 | loop fusion | bytes 1048576
  67.6 1.1 %bitcast_dynamic-update-slice_fusion.4 = bf16[8,512,512]{2,1,0:T(8,128)(2,1)S(1)} fusion(bf16[8,512,512]{2,1,0:T(8,128)(2,1)S(1)} %bitcast_dynamic-update-slice_fusion.5, bf16[512,512]{1,0:T(8,128)(2,1)} %collective-permute-done.2), kind=kLoop, calls=%fused_computation.13 | loop fusion | bytes 1048576
  68.7 0.7 collective-permute-start.20
  69.4 5.1 %collective-permute-done.6 = bf16[512,512]{1,0:T(8,128)(2,1)S(1)} collective-permute-done((bf16[512,512]{1,0:T(8,128)(2,1)S(1)}, bf16[512,512]{1,0:T(8,128)(2,1)S(1)}, u32[]{:S(2)}, u32[]{:S(2)}) %collective-permute-start.6) | collective-permute-done | bytes 524320 | tf_op jit(solution)/shard_map/ppermute | solution.py:34
  74.5 0.8 collective-permute-start.18
  75.2 0.0 collective-permute-start.19
  75.3 2.3 %collective-permute-done.14.refs_7_ = bf16[512,512]{1,0:T(8,128)(2,1)S(1)} collective-permute-done((bf16[512,512]{1,0:T(8,128)(2,1)S(1)}, bf16[512,512]{1,0:T(8,128)(2,1)S(1)}, u32[]{:S(2)}, u32[]{:S(2)}) %collective-permute-start.14) | collective-permute-done | bytes 524320 | tf_op jit(solution)/shard_map/ppermute | solution.py:34
  77.6 1.1 %collective-permute-start.21 = (bf16[512,512]{1,0:T(8,128)(2,1)S(1)}, bf16[512,512]{1,0:T(8,128)(2,1)S(1)}, u32[]{:S(2)}, u32[]{:S(2)}) collective-permute-start(bf16[512,512]{1,0:T(8,128)(2,1)S(1)} %collective-permute-done.13.refs_6_), channel_id=1, source_target_pairs={{0,1},{1,0},{2,3},{3,2},{4,5},{5,4},{6,7},{7,6},{8,9},{9,8},{10,11... | collective-permute-start | bytes 1572872 | tf_op jit(solution)/shard_map/ppermute | solution.py:34
  78.8 1.4 %collective-permute-done.21.refs_14_ = bf16[512,512]{1,0:T(8,128)(2,1)S(1)} collective-permute-done((bf16[512,512]{1,0:T(8,128)(2,1)S(1)}, bf16[512,512]{1,0:T(8,128)(2,1)S(1)}, u32[]{:S(2)}, u32[]{:S(2)}) %collective-permute-start.21) | collective-permute-done | bytes 524320 | tf_op jit(solution)/shard_map/ppermute | solution.py:34
  80.2 0.7 collective-permute-done.22.refs_15_
  80.9 0.9 give_kernel.2
  81.8 1.4 %collective-permute-start.23 = (s16[272,512]{1,0:T(8,128)(2,1)S(1)}, s16[272,512]{1,0:T(8,128)(2,1)S(1)}, u32[]{:S(2)}, u32[]{:S(2)}) collective-permute-start(s16[272,512]{1,0:T(8,128)(2,1)S(1)} %give_kernel.2), channel_id=1, source_target_pairs={{0,16},{16,0},{1,17},{17,1},{2,18},{18,2},{3,19},{19,3},{4,20},{20... | collective-permute-start | bytes 835592 | tf_op jit(solution)/shard_map/ppermute | solution.py:34
  83.2 0.9 give_kernel.3
  84.1 0.3 collective-permute-start.24
  84.4 1.2 %keep_kernel.1 = f32[512,512]{1,0:T(8,128)S(1)} custom-call(s32[24]{0:T(128)S(1)} %pad_add_fusion.meta, bf16[8,512,512]{2,1,0:T(8,128)(2,1)S(1)} %bitcast_dynamic-update-slice_fusion.draws, bf16[512,512]{1,0:T(8,128)(2,1)S(1)} %collective-permute-done.7.refs_0_, bf16[512,512]{1,0:T(8,128)(2,1)S(1)} %collective-permute-done.8.refs_1_, ...), custom_call_target="tpu_custom_call" | custom-call | tf_op jit(solution)/shard_map/keep_kernel/pallas_call | solution.py:84
  85.6 4.2 %collective-permute-done.23 = s16[272,512]{1,0:T(8,128)(2,1)S(1)} collective-permute-done((s16[272,512]{1,0:T(8,128)(2,1)S(1)}, s16[272,512]{1,0:T(8,128)(2,1)S(1)}, u32[]{:S(2)}, u32[]{:S(2)}) %collective-permute-start.23) | collective-permute-done | bytes 278560 | tf_op jit(solution)/shard_map/ppermute | solution.py:34
  89.8 0.5 slice.30
  91.0 4.8 %collective-permute-done.24 = s16[272,512]{1,0:T(8,128)(2,1)S(1)} collective-permute-done((s16[272,512]{1,0:T(8,128)(2,1)S(1)}, s16[272,512]{1,0:T(8,128)(2,1)S(1)}, u32[]{:S(2)}, u32[]{:S(2)}) %collective-permute-start.24) | collective-permute-done | bytes 278560 | tf_op jit(solution)/shard_map/ppermute | solution.py:34
  95.8 0.6 slice.33
  97.1 0.2 fusion.2
  97.3 0.8 pad_maximum_fusion
  (28 shorter events, 0.3 us)
Async XLA Ops:
  0.0 18.3 %collective-permute-start = (bf16[512,512]{1,0:T(8,128)(2,1)}, bf16[512,512]{1,0:T(8,128)(2,1)S(1)}, u32[]{:S(2)}, u32[]{:S(2)}) collective-permute-start(bf16[512,512]{1,0:T(8,128)(2,1)} %param.5), channel_id=1, source_target_pairs={{0,32},{32,64},{64,96},{96,128},{128,160},{160,192},{192,224},{224... | collective-permute-start | bytes 1572872 | tf_op jit(solution)/shard_map/ppermute | solution.py:34
  2.5 20.3 %collective-permute-start.4 = (bf16[512,512]{1,0:T(8,128)(2,1)}, bf16[512,512]{1,0:T(8,128)(2,1)S(1)}, u32[]{:S(2)}, u32[]{:S(2)}) collective-permute-start(bf16[512,512]{1,0:T(8,128)(2,1)} %param.5), channel_id=1, source_target_pairs={{0,224},{32,0},{64,32},{96,64},{128,96},{160,128},{192,160},{224,1... | collective-permute-start | bytes 1572872 | tf_op jit(solution)/shard_map/ppermute | solution.py:34
  10.7 15.2 %collective-permute-start.7 = (bf16[512,512]{1,0:T(8,128)(2,1)}, bf16[512,512]{1,0:T(8,128)(2,1)S(1)}, u32[]{:S(2)}, u32[]{:S(2)}) collective-permute-start(bf16[512,512]{1,0:T(8,128)(2,1)} %fusion), channel_id=1, source_target_pairs={{0,0},{1,16},{8,8},{9,24},{16,1},{17,17},{24,9},{25,25},{2,2},{3,1... | collective-permute-start | bytes 1572872 | tf_op jit(solution)/shard_map/ppermute | solution.py:30
  18.3 13.5 %collective-permute-start.1 = (bf16[512,512]{1,0:T(8,128)(2,1)S(1)}, bf16[512,512]{1,0:T(8,128)(2,1)}, u32[]{:S(2)}, u32[]{:S(2)}) collective-permute-start(bf16[512,512]{1,0:T(8,128)(2,1)S(1)} %collective-permute-done), channel_id=1, source_target_pairs={{0,32},{32,64},{64,96},{96,128},{128,160},{160,192},{192,224},{224... | collective-permute-start | bytes 1572872 | tf_op jit(solution)/shard_map/ppermute | solution.py:34
  18.3 18.8 %collective-permute-start.8 = (bf16[512,512]{1,0:T(8,128)(2,1)}, bf16[512,512]{1,0:T(8,128)(2,1)S(1)}, u32[]{:S(2)}, u32[]{:S(2)}) collective-permute-start(bf16[512,512]{1,0:T(8,128)(2,1)} %fusion), channel_id=1, source_target_pairs={{0,8},{1,24},{8,0},{9,16},{16,9},{17,25},{24,1},{25,17},{2,10},{3,... | collective-permute-start | bytes 1572872 | tf_op jit(solution)/shard_map/ppermute | solution.py:30
  22.8 14.2 %collective-permute-start.5 = (bf16[512,512]{1,0:T(8,128)(2,1)S(1)}, bf16[512,512]{1,0:T(8,128)(2,1)S(1)}, u32[]{:S(2)}, u32[]{:S(2)}) collective-permute-start(bf16[512,512]{1,0:T(8,128)(2,1)S(1)} %collective-permute-done.4), channel_id=1, source_target_pairs={{0,224},{32,0},{64,32},{96,64},{128,96},{160,128},{192,160},{224,1... | collective-permute-start | bytes 1572872 | tf_op jit(solution)/shard_map/ppermute | solution.py:34
  25.8 13.9 %collective-permute-start.9 = (bf16[512,512]{1,0:T(8,128)(2,1)S(1)}, bf16[512,512]{1,0:T(8,128)(2,1)S(1)}, u32[]{:S(2)}, u32[]{:S(2)}) collective-permute-start(bf16[512,512]{1,0:T(8,128)(2,1)S(1)} %collective-permute-done.7.refs_0_), channel_id=1, source_target_pairs={{0,2},{2,4},{4,6},{6,0},{1,3},{3,5},{5,7},{7,1},{8,10},{10,12},{12... | collective-permute-start | bytes 1572872 | tf_op jit(solution)/shard_map/ppermute | solution.py:34
  31.8 12.8 %collective-permute-start.2 = (bf16[512,512]{1,0:T(8,128)(2,1)}, bf16[512,512]{1,0:T(8,128)(2,1)}, u32[]{:S(2)}, u32[]{:S(2)}) collective-permute-start(bf16[512,512]{1,0:T(8,128)(2,1)} %collective-permute-done.1), channel_id=1, source_target_pairs={{0,32},{32,64},{64,96},{96,128},{128,160},{160,192},{192,224},{224... | collective-permute-start | bytes 1572872 | tf_op jit(solution)/shard_map/ppermute | solution.py:34
  34.5 18.1 %collective-permute-start.11 = (bf16[512,512]{1,0:T(8,128)(2,1)S(1)}, bf16[512,512]{1,0:T(8,128)(2,1)S(1)}, u32[]{:S(2)}, u32[]{:S(2)}) collective-permute-start(bf16[512,512]{1,0:T(8,128)(2,1)S(1)} %collective-permute-done.7.refs_0_), channel_id=1, source_target_pairs={{0,6},{2,0},{4,2},{6,4},{1,7},{3,1},{5,3},{7,5},{8,14},{10,8},{12,... | collective-permute-start | bytes 1572872 | tf_op jit(solution)/shard_map/ppermute | solution.py:34
  37.1 12.2 %collective-permute-start.10 = (bf16[512,512]{1,0:T(8,128)(2,1)S(1)}, bf16[512,512]{1,0:T(8,128)(2,1)S(1)}, u32[]{:S(2)}, u32[]{:S(2)}) collective-permute-start(bf16[512,512]{1,0:T(8,128)(2,1)S(1)} %collective-permute-done.8.refs_1_), channel_id=1, source_target_pairs={{0,2},{2,4},{4,6},{6,0},{1,3},{3,5},{5,7},{7,1},{8,10},{10,12},{12... | collective-permute-start | bytes 1572872 | tf_op jit(solution)/shard_map/ppermute | solution.py:34
  37.1 20.3 %collective-permute-start.12 = (bf16[512,512]{1,0:T(8,128)(2,1)S(1)}, bf16[512,512]{1,0:T(8,128)(2,1)S(1)}, u32[]{:S(2)}, u32[]{:S(2)}) collective-permute-start(bf16[512,512]{1,0:T(8,128)(2,1)S(1)} %collective-permute-done.8.refs_1_), channel_id=1, source_target_pairs={{0,6},{2,0},{4,2},{6,4},{1,7},{3,1},{5,3},{7,5},{8,14},{10,8},{12,... | collective-permute-start | bytes 1572872 | tf_op jit(solution)/shard_map/ppermute | solution.py:34
  39.8 20.7 %collective-permute-start.15 = (bf16[512,512]{1,0:T(8,128)(2,1)S(1)}, bf16[512,512]{1,0:T(8,128)(2,1)S(1)}, u32[]{:S(2)}, u32[]{:S(2)}) collective-permute-start(bf16[512,512]{1,0:T(8,128)(2,1)S(1)} %collective-permute-done.7.refs_0_), channel_id=1, source_target_pairs={{0,1},{1,0},{2,3},{3,2},{4,5},{5,4},{6,7},{7,6},{8,9},{9,8},{10,11... | collective-permute-start | bytes 1572872 | tf_op jit(solution)/shard_map/ppermute | solution.py:34
  44.6 18.5 %collective-permute-start.3 = (bf16[512,512]{1,0:T(8,128)(2,1)}, bf16[512,512]{1,0:T(8,128)(2,1)S(1)}, u32[]{:S(2)}, u32[]{:S(2)}) collective-permute-start(bf16[512,512]{1,0:T(8,128)(2,1)} %collective-permute-done.2), channel_id=1, source_target_pairs={{0,32},{32,64},{64,96},{96,128},{128,160},{160,192},{192,224},{224... | collective-permute-start | bytes 1572872 | tf_op jit(solution)/shard_map/ppermute | solution.py:34
  49.3 19.4 %collective-permute-start.16 = (bf16[512,512]{1,0:T(8,128)(2,1)S(1)}, bf16[512,512]{1,0:T(8,128)(2,1)S(1)}, u32[]{:S(2)}, u32[]{:S(2)}) collective-permute-start(bf16[512,512]{1,0:T(8,128)(2,1)S(1)} %collective-permute-done.8.refs_1_), channel_id=1, source_target_pairs={{0,1},{1,0},{2,3},{3,2},{4,5},{5,4},{6,7},{7,6},{8,9},{9,8},{10,11... | collective-permute-start | bytes 1572872 | tf_op jit(solution)/shard_map/ppermute | solution.py:34
  52.6 22.6 %collective-permute-start.13 = (bf16[512,512]{1,0:T(8,128)(2,1)S(1)}, bf16[512,512]{1,0:T(8,128)(2,1)S(1)}, u32[]{:S(2)}, u32[]{:S(2)}) collective-permute-start(bf16[512,512]{1,0:T(8,128)(2,1)S(1)} %collective-permute-done.9.refs_2_), channel_id=1, source_target_pairs={{0,2},{2,4},{4,6},{6,0},{1,3},{3,5},{5,7},{7,1},{8,10},{10,12},{12... | collective-permute-start | bytes 1572872 | tf_op jit(solution)/shard_map/ppermute | solution.py:34
  57.4 21.3 %collective-permute-start.17 = (bf16[512,512]{1,0:T(8,128)(2,1)S(1)}, bf16[512,512]{1,0:T(8,128)(2,1)S(1)}, u32[]{:S(2)}, u32[]{:S(2)}) collective-permute-start(bf16[512,512]{1,0:T(8,128)(2,1)S(1)} %collective-permute-done.9.refs_2_), channel_id=1, source_target_pairs={{0,1},{1,0},{2,3},{3,2},{4,5},{5,4},{6,7},{7,6},{8,9},{9,8},{10,11... | collective-permute-start | bytes 1572872 | tf_op jit(solution)/shard_map/ppermute | solution.py:34
  60.4 14.0 %collective-permute-start.6 = (bf16[512,512]{1,0:T(8,128)(2,1)S(1)}, bf16[512,512]{1,0:T(8,128)(2,1)S(1)}, u32[]{:S(2)}, u32[]{:S(2)}) collective-permute-start(bf16[512,512]{1,0:T(8,128)(2,1)S(1)} %collective-permute-done.5), channel_id=1, source_target_pairs={{0,224},{32,0},{64,32},{96,64},{128,96},{160,128},{192,160},{224,1... | collective-permute-start | bytes 1572872 | tf_op jit(solution)/shard_map/ppermute | solution.py:34
  63.1 14.4 %collective-permute-start.14 = (bf16[512,512]{1,0:T(8,128)(2,1)S(1)}, bf16[512,512]{1,0:T(8,128)(2,1)S(1)}, u32[]{:S(2)}, u32[]{:S(2)}) collective-permute-start(bf16[512,512]{1,0:T(8,128)(2,1)S(1)} %collective-permute-done.12.refs_5_), channel_id=1, source_target_pairs={{0,6},{2,0},{4,2},{6,4},{1,7},{3,1},{5,3},{7,5},{8,14},{10,8},{12,... | collective-permute-start | bytes 1572872 | tf_op jit(solution)/shard_map/ppermute | solution.py:34
  68.7 10.1 %collective-permute-start.20 = (bf16[512,512]{1,0:T(8,128)(2,1)S(1)}, bf16[512,512]{1,0:T(8,128)(2,1)S(1)}, u32[]{:S(2)}, u32[]{:S(2)}) collective-permute-start(bf16[512,512]{1,0:T(8,128)(2,1)S(1)} %collective-permute-done.12.refs_5_), channel_id=1, source_target_pairs={{0,1},{1,0},{2,3},{3,2},{4,5},{5,4},{6,7},{7,6},{8,9},{9,8},{10,11... | collective-permute-start | bytes 1572872 | tf_op jit(solution)/shard_map/ppermute | solution.py:34
  74.5 4.3 %collective-permute-start.18 = (bf16[512,512]{1,0:T(8,128)(2,1)S(1)}, bf16[512,512]{1,0:T(8,128)(2,1)S(1)}, u32[]{:S(2)}, u32[]{:S(2)}) collective-permute-start(bf16[512,512]{1,0:T(8,128)(2,1)S(1)} %collective-permute-done.10.refs_3_), channel_id=1, source_target_pairs={{0,1},{1,0},{2,3},{3,2},{4,5},{5,4},{6,7},{7,6},{8,9},{9,8},{10,11... | collective-permute-start | bytes 1572872 | tf_op jit(solution)/shard_map/ppermute | solution.py:34
  75.2 3.6 %collective-permute-start.19 = (bf16[512,512]{1,0:T(8,128)(2,1)S(1)}, bf16[512,512]{1,0:T(8,128)(2,1)S(1)}, u32[]{:S(2)}, u32[]{:S(2)}) collective-permute-start(bf16[512,512]{1,0:T(8,128)(2,1)S(1)} %collective-permute-done.11.refs_4_), channel_id=1, source_target_pairs={{0,1},{1,0},{2,3},{3,2},{4,5},{5,4},{6,7},{7,6},{8,9},{9,8},{10,11... | collective-permute-start | bytes 1572872 | tf_op jit(solution)/shard_map/ppermute | solution.py:34
  77.6 2.6 %collective-permute-start.21 = (bf16[512,512]{1,0:T(8,128)(2,1)S(1)}, bf16[512,512]{1,0:T(8,128)(2,1)S(1)}, u32[]{:S(2)}, u32[]{:S(2)}) collective-permute-start(bf16[512,512]{1,0:T(8,128)(2,1)S(1)} %collective-permute-done.13.refs_6_), channel_id=1, source_target_pairs={{0,1},{1,0},{2,3},{3,2},{4,5},{5,4},{6,7},{7,6},{8,9},{9,8},{10,11... | collective-permute-start | bytes 1572872 | tf_op jit(solution)/shard_map/ppermute | solution.py:34
  78.7 2.3 %collective-permute-start.22 = (bf16[512,512]{1,0:T(8,128)(2,1)S(1)}, bf16[512,512]{1,0:T(8,128)(2,1)S(1)}, u32[]{:S(2)}, u32[]{:S(2)}) collective-permute-start(bf16[512,512]{1,0:T(8,128)(2,1)S(1)} %collective-permute-done.14.refs_7_), channel_id=1, source_target_pairs={{0,1},{1,0},{2,3},{3,2},{4,5},{5,4},{6,7},{7,6},{8,9},{9,8},{10,11... | collective-permute-start | bytes 1572872 | tf_op jit(solution)/shard_map/ppermute | solution.py:34
  81.8 8.0 %collective-permute-start.23 = (s16[272,512]{1,0:T(8,128)(2,1)S(1)}, s16[272,512]{1,0:T(8,128)(2,1)S(1)}, u32[]{:S(2)}, u32[]{:S(2)}) collective-permute-start(s16[272,512]{1,0:T(8,128)(2,1)S(1)} %give_kernel.2), channel_id=1, source_target_pairs={{0,16},{16,0},{1,17},{17,1},{2,18},{18,2},{3,19},{19,3},{4,20},{20... | collective-permute-start | bytes 835592 | tf_op jit(solution)/shard_map/ppermute | solution.py:34
  84.1 11.6 %collective-permute-start.24 = (s16[272,512]{1,0:T(8,128)(2,1)S(1)}, s16[272,512]{1,0:T(8,128)(2,1)S(1)}, u32[]{:S(2)}, u32[]{:S(2)}) collective-permute-start(s16[272,512]{1,0:T(8,128)(2,1)S(1)} %give_kernel.3), channel_id=1, source_target_pairs={{0,16},{16,0},{1,17},{17,1},{2,18},{18,2},{3,19},{19,3},{4,20},{20... | collective-permute-start | bytes 835592 | tf_op jit(solution)/shard_map/ppermute | solution.py:34

commit v4 on v0

v4 whole, which is shorter than its diff:
```python
import functools

import jax
import jax.numpy as jnp
from jax import lax
from jax.experimental import pallas as pl
from jax.experimental.pallas import tpu as pltpu
from jax.sharding import Mesh
from jax.sharding import PartitionSpec as P

TILE = 512
PARTS = 2
SIZE = TILE // PARTS
EXTRA = 16
LARGEST = 32000.0
COLUMN = ("yl", "yh", "c")
SMEM = pl.BlockSpec(memory_space=pltpu.SMEM)
VMEM = pl.BlockSpec(memory_space=pltpu.VMEM)
PIECES = ((0, 0), (1, 0), (0, -1), (1, -1), (0, 1), (1, 1), (0, 2), (1, 2))


def column_id(yl, yh, c):
    return (yl * 2 + yh) * 2 + c


def to_parity(tile, across):
    pairs = []
    for yl in range(2):
        for yh in range(2):
            for c in range(2):
                to = yl if c == yl else 1 - yl
                pairs.append((column_id(yl, yh, c), column_id(to, yh ^ across, c if c == yl else yl)))
    return lax.ppermute(tile, COLUMN, pairs)


def shift(name, count, piece, by):
    return lax.ppermute(piece, name, [(i, (i + by) % count) for i in range(count)])


along_x = functools.partial(shift, "x", 4)
along_z = functools.partial(shift, "z", 8)


def other_core(piece):
    return shift("c", 2, piece, 1)


def other_chip(piece):
    return shift("yl", 2, piece, 1)


def call(kernel, out, scratch, specs, name):
    return pl.pallas_call(
        kernel,
        out_shape=out,
        in_specs=specs,
        out_specs=VMEM,
        scratch_shapes=scratch,
        compiler_params=pltpu.CompilerParams(vmem_limit_bytes=40 * 1024 * 1024),
        name=name,
    )


def masked_kernel(place, factor, out):
    z, yl, yh, x, c = (place[n] for n in range(5))
    ahead = (2 * z + yl - (8 * yh + 2 * x + c)) * TILE
    tile = factor[...].T
    j = lax.broadcasted_iota(jnp.int32, tile.shape, 0)
    i = lax.broadcasted_iota(jnp.int32, tile.shape, 1)
    out[...] = jnp.where(j <= i + ahead, tile, jnp.zeros_like(tile))


def masked(place, factor):
    out = jax.ShapeDtypeStruct((TILE, TILE), factor.dtype)
    return call(masked_kernel, out, [], [SMEM, VMEM], "masked")(place, factor)


def pack_kernel(*refs):
    for n, ref in enumerate(refs[:-1]):
        refs[-1][n * TILE : (n + 1) * TILE, :] = ref[...]


def pack(*tiles):
    out = jax.ShapeDtypeStruct((len(tiles) * TILE, TILE), tiles[0].dtype)
    return call(pack_kernel, out, [], [VMEM] * len(tiles), "pack")(*tiles)


def sums_kernel(given, begin, size, packs, place, occupancy, *refs):
    refs, (out, total, slots) = refs[:-3], refs[-3:]
    draws, halves, packed = refs[:7], refs[7:9], refs[9:]
    own, other = {}, {}
    for tiles, refs in ((own, packed[: len(packs[0])]), (other, packed[len(packs[0]) :])):
        for ref, pack in zip(refs, packs[tiles is other]):
            for n, piece in enumerate(pack):
                tiles[piece] = ref.at[n * TILE : (n + 1) * TILE, :]
    z, yl, yh, x, c = (place[n] for n in range(5))
    row = 1 - yl if given else yl
    for n, slot in enumerate((0, 1, 2, 3, 5, 6, 7)):
        slots[slot] = draws[n][begin : begin + size, :]
    for part in range(size // SIZE):
        slots[4, part * SIZE : (part + 1) * SIZE, :] = halves[begin // SIZE + part][...]
    total[...] = jnp.zeros_like(total)
    for n, (across, by) in enumerate(PIECES):
        block = (1 - yh if across else yh) * 4 + ((x + by) & 3)
        column = 2 * block + yl
        held = (occupancy[2 * z + row, column] == 1) & (column <= 2 * z + row)
        slot = (z - block) & 7
        for where, ref in ((row == c, own[n]), (row != c, other[n])):

            @pl.when(held & where)
            def _(slot=slot, ref=ref):
                total[...] += jnp.dot(slots[slot], ref[...], preferred_element_type=jnp.float32)

    if not given:
        out[...] = total[...]
        return
    sums = total[...].reshape(EXTRA, size // EXTRA, TILE)
    most = jnp.max(jnp.max(jnp.abs(sums), axis=1, keepdims=True), axis=2, keepdims=True)
    power = jnp.floor(jnp.log(LARGEST / jnp.maximum(most, 1e-30)) * 1.4426950)
    codes = jnp.round(sums * jnp.exp2(power)).reshape(size, TILE)
    out[:size, :] = codes.astype(jnp.int32).astype(jnp.int16)
    powers = jnp.broadcast_to(power, (EXTRA, 1, TILE)).reshape(EXTRA, TILE)
    out[size:, :] = powers.astype(jnp.int32).astype(jnp.int16)


def sums(given, begin, size, packs, out, *args):
    scratch = [pltpu.VMEM((size, TILE), jnp.float32), pltpu.VMEM((8, size, TILE), jnp.bfloat16)]
    kernel = functools.partial(sums_kernel, given, begin, size, packs)
    specs = [SMEM] * 2 + [VMEM] * (len(args) - 2)
    return call(kernel, out, scratch, specs, "give" if given else "keep")(*args)


def join_kernel(keep, *refs):
    out = refs[-1]
    for part, sent in enumerate(refs[:-1]):
        rows = slice(part * SIZE, (part + 1) * SIZE)
        power = sent[SIZE:, :].astype(jnp.int32).astype(jnp.float32).reshape(EXTRA, 1, TILE)
        codes = sent[:SIZE, :].astype(jnp.int32).astype(jnp.float32).reshape(EXTRA, SIZE // EXTRA, TILE)
        crossed = (codes * jnp.exp2(-power)).reshape(SIZE, TILE)
        out[rows, :] = (keep[rows, :] + crossed).astype(out.dtype)


def join(keep, crossed):
    out = jax.ShapeDtypeStruct((TILE, TILE), jnp.bfloat16)
    return call(join_kernel, out, [], [VMEM] * (1 + PARTS), "join")(keep, *crossed)


def local(draws, factor, occupancy):
    place = jnp.stack([lax.axis_index(n) for n in ("z", "yl", "yh", "x", "c")]).astype(jnp.int32)
    together = lax.optimization_barrier
    tile = masked(place, factor)
    near, far = to_parity(tile, 0), to_parity(tile, 1)
    up1, down1 = along_z(draws, 1), along_z(draws, -1)
    up1, down1, near, far = together((up1, down1, near, far))
    pair = pack(near, far)
    up2, down2 = along_z(up1, 1), along_z(down1, -1)
    before, after = along_x(pair, 1), along_x(pair, -1)
    pair_c = other_core(pair)
    up2, down2, pair_c = together((up2, down2, pair_c))
    up3, down3 = along_z(up2, 1), along_z(down2, -1)
    near_o, far_o = along_x(before[:TILE], 1), along_x(after[TILE:], -1)
    up3, down3, before, after = together((up3, down3, before, after))
    up4, down4 = along_z(up3[:SIZE], 1), along_z(down3[SIZE:], -1)
    before_c, after_c = other_core(before), other_core(after)
    up4, down4, near_o, far_o = together((up4, down4, near_o, far_o))
    last_c = other_core(pack(near_o, far_o))
    packs = ((0, 1), (2, 3), (4, 5), (6,), (7,)), ((0, 1), (2, 3), (4, 5), (6, 7))
    args = (place, occupancy, draws, up1, up2, up3, down3, down2, down1, up4, down4)
    args += (pair, before, after, near_o, far_o, pair_c, before_c, after_c, last_c)
    coded = jax.ShapeDtypeStruct((SIZE + EXTRA, TILE), jnp.int16)
    crossed = [other_chip(sums(True, part * SIZE, SIZE, packs, coded, *args)) for part in range(PARTS)]
    keep = sums(False, 0, TILE, packs, jax.ShapeDtypeStruct((TILE, TILE), jnp.float32), *args)
    return join(keep, crossed)


def solution(mesh):
    fine = Mesh(mesh.devices.reshape(8, 2, 2, 4, 2), ("z", "yl", "yh", "x", "c"))
    scen, blk = ("z", "yl"), ("yh", "x", "c")
    return jax.shard_map(
        local,
        mesh=fine,
        in_specs=(P(blk, scen), P(scen, blk), P()),
        out_specs=P(blk, scen),
        check_vma=False,
    )
```

time: 305 us -> 92.5 us (0.30)
  waiting for transfers between devices: 277 us -> 50.4 us
  starting transfers between devices: 0.04 us -> 34.6 us
  matrix products: 13.4 us -> 0 us
  between operations: 13.4 us -> 0.13 us
  Pallas kernels: 0 us -> 5.97 us
    all_gather x2 -> x0, waiting for transfers between devices: 276 us -> none  [the longest x1 186 us: local(): whole = lax.all_gather(draws, 'scen', axis=1, tiled=True)]
    ppermute x0 -> x20, waiting for transfers between devices: none -> 50.4 us  [the longest x18 45.5 us: shift(): lax.ppermute(piece, name, [(i, (i + by) % count) for i in range(count)])]
    ppermute x0 -> x20, starting transfers between devices: none -> 34.6 us  [the longest x18 28.5 us: shift(): lax.ppermute(piece, name, [(i, (i + by) % count) for i in range(count)])]
    dot_general x2 -> x0, matrix products: 13.4 us -> none  [the longest x1 12.5 us: times_transposed(): lax.dot_general(left, right, (((1,), (1,)), ((), ())), preferred_element_...]
    pallas_call x0 -> x7, Pallas kernels: none -> 5.97 us  [the longest x3 4.05 us: sums(): return call(kernel, out, scratch, specs, 'give' if given else 'keep')(*args)]
  transfers between devices with their start and end apart: 2 -> 20, of which waited for: 2 -> 12; matrix products, arithmetic and copies ran while one was open for 0% -> 0% of each run, Pallas kernels for 0% -> 3%
where the time goes in v4:
time: 92.5 us; the launch traced here: 92.4 us
  waiting for transfers between devices  50.4 us (54%)
  starting transfers between devices  34.6 us (37%)
  Pallas kernels  5.97 us (6%)
  local copies, waits for them, and re-layouts  1.24 us (1%)
    ppermute x18, waiting for transfers between devices, shift(): lax.ppermute(piece, name, [(i, (i + by) % count) for i in range(count)])  45.5 us
    ppermute x18, starting transfers between devices, shift(): lax.ppermute(piece, name, [(i, (i + by) % count) for i in range(count)])  28.5 us
    ppermute x2, starting transfers between devices, to_parity(): return lax.ppermute(tile, COLUMN, pairs)  6.12 us
    ppermute x2, waiting for transfers between devices, to_parity(): return lax.ppermute(tile, COLUMN, pairs)  4.96 us
    pallas_call x3, Pallas kernels, sums(): return call(kernel, out, scratch, specs, 'give' if given else 'keep')(*args)  4.05 us
  transfers between devices with their start and end apart: 20, of which 12 were waited for; matrix products, arithmetic and copies ran while one was open for 0% of the time, Pallas kernels for 3%

profile of v4, /device:TPU:1, one launch (start us, length us, event | category | flops | bytes accessed | tf_op | source)
XLA Modules:
  0.0 92.4 jit_solution(576208177073374871)
XLA Ops:
  0.0 0.1 stack.23.place
  0.1 1.0 %copy-done.1 = bf16[512,512]{1,0:T(8,128)(2,1)S(1)} copy-done((bf16[512,512]{1,0:T(8,128)(2,1)S(1)}, bf16[512,512]{1,0:T(8,128)(2,1)}, u32[]{:S(2)}) %copy-start.1) | copy-done | bytes 524312
  1.1 0.8 masked.1
  1.9 4.2 %collective-permute-start.3 = (bf16[512,512]{1,0:T(8,128)(2,1)S(1)}, bf16[512,512]{1,0:T(8,128)(2,1)S(1)}, u32[]{:S(2)}, u32[]{:S(2)}) collective-permute-start(bf16[512,512]{1,0:T(8,128)(2,1)S(1)} %masked.1), channel_id=1, source_target_pairs={{0,8},{1,24},{8,0},{9,16},{16,9},{17,25},{24,1},{25,17},{2,10},{3,... | collective-permute-start | bytes 1572872 | tf_op jit(solution)/shard_map/ppermute | solution.py:33
  6.1 1.9 %collective-permute-start.2 = (bf16[512,512]{1,0:T(8,128)(2,1)S(1)}, bf16[512,512]{1,0:T(8,128)(2,1)S(1)}, u32[]{:S(2)}, u32[]{:S(2)}) collective-permute-start(bf16[512,512]{1,0:T(8,128)(2,1)S(1)} %masked.1), channel_id=1, source_target_pairs={{0,0},{1,16},{8,8},{9,24},{16,1},{17,17},{24,9},{25,25},{2,2},{3,1... | collective-permute-start | bytes 1572872 | tf_op jit(solution)/shard_map/ppermute | solution.py:33
  8.1 5.7 %collective-permute-start.1 = (bf16[512,512]{1,0:T(8,128)(2,1)S(1)}, bf16[512,512]{1,0:T(8,128)(2,1)S(1)}, u32[]{:S(2)}, u32[]{:S(2)}) collective-permute-start(bf16[512,512]{1,0:T(8,128)(2,1)S(1)} %copy-done), channel_id=1, source_target_pairs={{0,224},{32,0},{64,32},{96,64},{128,96},{160,128},{192,160},{224,1... | collective-permute-start | bytes 1572872 | tf_op jit(solution)/shard_map/ppermute | solution.py:37
  13.7 0.0 collective-permute-start
  13.7 3.9 %collective-permute-done.3.refs_1_ = bf16[512,512]{1,0:T(8,128)(2,1)S(1)} collective-permute-done((bf16[512,512]{1,0:T(8,128)(2,1)S(1)}, bf16[512,512]{1,0:T(8,128)(2,1)S(1)}, u32[]{:S(2)}, u32[]{:S(2)}) %collective-permute-start.3) | collective-permute-done | bytes 524320 | tf_op jit(solution)/shard_map/ppermute | solution.py:33
  17.6 1.1 %collective-permute-done.2.refs_0_ = bf16[512,512]{1,0:T(8,128)(2,1)S(1)} collective-permute-done((bf16[512,512]{1,0:T(8,128)(2,1)S(1)}, bf16[512,512]{1,0:T(8,128)(2,1)S(1)}, u32[]{:S(2)}, u32[]{:S(2)}) %collective-permute-start.2) | collective-permute-done | bytes 524320 | tf_op jit(solution)/shard_map/ppermute | solution.py:33
  18.7 6.6 %collective-permute-done.1.refs_6_ = bf16[512,512]{1,0:T(8,128)(2,1)S(1)} collective-permute-done((bf16[512,512]{1,0:T(8,128)(2,1)S(1)}, bf16[512,512]{1,0:T(8,128)(2,1)S(1)}, u32[]{:S(2)}, u32[]{:S(2)}) %collective-permute-start.1) | collective-permute-done | bytes 524320 | tf_op jit(solution)/shard_map/ppermute | solution.py:37
  25.3 3.5 %collective-permute-done.refs_1_ = bf16[512,512]{1,0:T(8,128)(2,1)S(1)} collective-permute-done((bf16[512,512]{1,0:T(8,128)(2,1)S(1)}, bf16[512,512]{1,0:T(8,128)(2,1)S(1)}, u32[]{:S(2)}, u32[]{:S(2)}) %collective-permute-start) | collective-permute-done | bytes 524320 | tf_op jit(solution)/shard_map/ppermute | solution.py:37
  28.8 0.1 pack.2.refs_9_
  28.9 0.6 collective-permute-start.6
  29.4 2.5 %collective-permute-start.10 = (bf16[1024,512]{1,0:T(8,128)(2,1)S(1)}, bf16[1024,512]{1,0:T(8,128)(2,1)S(1)}, u32[]{:S(2)}, u32[]{:S(2)}) collective-permute-start(bf16[1024,512]{1,0:T(8,128)(2,1)S(1)} %pack.2.refs_9_), channel_id=1, source_target_pairs={{0,6},{2,0},{4,2},{6,4},{1,7},{3,1},{5,3},{7,5},{8,14},{10,8},{12,... | collective-permute-start | bytes 3145736 | tf_op jit(solution)/shard_map/ppermute | solution.py:37
  31.9 0.0 collective-permute-start.9
  31.9 0.0 collective-permute-start.4
  31.9 2.7 %collective-permute-start.5 = (bf16[512,512]{1,0:T(8,128)(2,1)S(1)}, bf16[512,512]{1,0:T(8,128)(2,1)S(1)}, u32[]{:S(2)}, u32[]{:S(2)}) collective-permute-start(bf16[512,512]{1,0:T(8,128)(2,1)S(1)} %collective-permute-done.1.refs_6_), channel_id=1, source_target_pairs={{0,224},{32,0},{64,32},{96,64},{128,96},{160,128},{192,160},{224,1... | collective-permute-start | bytes 1572872 | tf_op jit(solution)/shard_map/ppermute | solution.py:37
  34.6 11.7 %collective-permute-done.4.refs_2_ = bf16[512,512]{1,0:T(8,128)(2,1)S(1)} collective-permute-done((bf16[512,512]{1,0:T(8,128)(2,1)S(1)}, bf16[512,512]{1,0:T(8,128)(2,1)S(1)}, u32[]{:S(2)}, u32[]{:S(2)}) %collective-permute-start.4) | collective-permute-done | bytes 524320 | tf_op jit(solution)/shard_map/ppermute | solution.py:37
  46.3 0.0 collective-permute-done.5.refs_5_
  46.3 0.0 collective-permute-done.6.refs_14_
  46.3 0.0 collective-permute-start.7
  46.3 2.7 %collective-permute-start.8 = (bf16[512,512]{1,0:T(8,128)(2,1)S(1)}, bf16[512,512]{1,0:T(8,128)(2,1)S(1)}, u32[]{:S(2)}, u32[]{:S(2)}) collective-permute-start(bf16[512,512]{1,0:T(8,128)(2,1)S(1)} %collective-permute-done.5.refs_5_), channel_id=1, source_target_pairs={{0,224},{32,0},{64,32},{96,64},{128,96},{160,128},{192,160},{224,1... | collective-permute-start | bytes 1572872 | tf_op jit(solution)/shard_map/ppermute | solution.py:37
  49.0 5.5 %collective-permute-done.10.refs_11_ = bf16[1024,512]{1,0:T(8,128)(2,1)S(1)} collective-permute-done((bf16[1024,512]{1,0:T(8,128)(2,1)S(1)}, bf16[1024,512]{1,0:T(8,128)(2,1)S(1)}, u32[]{:S(2)}, u32[]{:S(2)}) %collective-permute-start.10) | collective-permute-done | bytes 1048608 | tf_op jit(solution)/shard_map/ppermute | solution.py:37
  54.5 3.5 %collective-permute-start.14 = (bf16[512,512]{1,0:T(8,128)(2,1)S(1)}, bf16[512,512]{1,0:T(8,128)(2,1)S(1)}, u32[]{:S(2)}, u32[]{:S(2)}) collective-permute-start(bf16[512,512]{1,0:T(8,128)(2,1)S(1)} %slice.17), channel_id=1, source_target_pairs={{0,6},{2,0},{4,2},{6,4},{1,7},{3,1},{5,3},{7,5},{8,14},{10,8},{12,... | collective-permute-start | bytes 1572872 | tf_op jit(solution)/shard_map/ppermute | solution.py:37
  58.0 0.0 collective-permute-done.9.refs_10_
  58.0 0.1 collective-permute-start.13
  58.1 1.7 %collective-permute-done.7.refs_3_ = bf16[512,512]{1,0:T(8,128)(2,1)S(1)} collective-permute-done((bf16[512,512]{1,0:T(8,128)(2,1)S(1)}, bf16[512,512]{1,0:T(8,128)(2,1)S(1)}, u32[]{:S(2)}, u32[]{:S(2)}) %collective-permute-start.7) | collective-permute-done | bytes 524320 | tf_op jit(solution)/shard_map/ppermute | solution.py:37
  59.7 0.0 collective-permute-done.8.refs_4_
  59.8 0.0 copy-start.2
  59.8 2.5 %collective-permute-start.12 = (bf16[256,512]{1,0:T(8,128)(2,1)S(1)}, bf16[256,512]{1,0:T(8,128)(2,1)S(1)}, u32[]{:S(2)}, u32[]{:S(2)}) collective-permute-start(bf16[256,512]{1,0:T(8,128)(2,1)S(1)} %slice.13), channel_id=1, source_target_pairs={{0,224},{32,0},{64,32},{96,64},{128,96},{160,128},{192,160},{224,1... | collective-permute-start | bytes 786440 | tf_op jit(solution)/shard_map/ppermute | solution.py:37
  62.3 2.7 %collective-permute-start.15 = (bf16[1024,512]{1,0:T(8,128)(2,1)S(1)}, bf16[1024,512]{1,0:T(8,128)(2,1)S(1)}, u32[]{:S(2)}, u32[]{:S(2)}) collective-permute-start(bf16[1024,512]{1,0:T(8,128)(2,1)S(1)} %collective-permute-done.9.refs_10_), channel_id=1, source_target_pairs={{0,1},{1,0},{2,3},{3,2},{4,5},{5,4},{6,7},{7,6},{8,9},{9,8},{10,11... | collective-permute-start | bytes 3145736 | tf_op jit(solution)/shard_map/ppermute | solution.py:37
  64.9 3.4 %collective-permute-done.14.refs_1_.refs_13_ = bf16[512,512]{1,0:T(8,128)(2,1)S(1)} collective-permute-done((bf16[512,512]{1,0:T(8,128)(2,1)S(1)}, bf16[512,512]{1,0:T(8,128)(2,1)S(1)}, u32[]{:S(2)}, u32[]{:S(2)}) %collective-permute-start.14) | collective-permute-done | bytes 524320 | tf_op jit(solution)/shard_map/ppermute | solution.py:37
  68.3 1.8 %collective-permute-start.16 = (bf16[1024,512]{1,0:T(8,128)(2,1)S(1)}, bf16[1024,512]{1,0:T(8,128)(2,1)S(1)}, u32[]{:S(2)}, u32[]{:S(2)}) collective-permute-start(bf16[1024,512]{1,0:T(8,128)(2,1)S(1)} %collective-permute-done.10.refs_11_), channel_id=1, source_target_pairs={{0,1},{1,0},{2,3},{3,2},{4,5},{5,4},{6,7},{7,6},{8,9},{9,8},{10,11... | collective-permute-start | bytes 3145736 | tf_op jit(solution)/shard_map/ppermute | solution.py:37
  70.1 1.5 %collective-permute-done.13.refs_0_.refs_12_ = bf16[512,512]{1,0:T(8,128)(2,1)S(1)} collective-permute-done((bf16[512,512]{1,0:T(8,128)(2,1)S(1)}, bf16[512,512]{1,0:T(8,128)(2,1)S(1)}, u32[]{:S(2)}, u32[]{:S(2)}) %collective-permute-start.13) | collective-permute-done | bytes 524320 | tf_op jit(solution)/shard_map/ppermute | solution.py:37
  71.6 0.0 collective-permute-done.11.refs_7_
  71.6 0.1 pack.3
  71.6 2.3 %collective-permute-start.17 = (bf16[1024,512]{1,0:T(8,128)(2,1)S(1)}, bf16[1024,512]{1,0:T(8,128)(2,1)S(1)}, u32[]{:S(2)}, u32[]{:S(2)}) collective-permute-start(bf16[1024,512]{1,0:T(8,128)(2,1)S(1)} %pack.3), channel_id=1, source_target_pairs={{0,1},{1,0},{2,3},{3,2},{4,5},{5,4},{6,7},{7,6},{8,9},{9,8},{10,11... | collective-permute-start | bytes 3145736 | tf_op jit(solution)/shard_map/ppermute | solution.py:37
  74.0 0.0 collective-permute-done.15.refs_15_
  74.0 0.0 collective-permute-done.16.refs_16_
  74.0 2.3 %collective-permute-done.17.refs_17_ = bf16[1024,512]{1,0:T(8,128)(2,1)S(1)} collective-permute-done((bf16[1024,512]{1,0:T(8,128)(2,1)S(1)}, bf16[1024,512]{1,0:T(8,128)(2,1)S(1)}, u32[]{:S(2)}, u32[]{:S(2)}) %collective-permute-start.17) | collective-permute-done | bytes 1048608 | tf_op jit(solution)/shard_map/ppermute | solution.py:37
  76.3 1.2 %give.2 = s16[272,512]{1,0:T(8,128)(2,1)S(1)} custom-call(s32[5]{0:T(128)S(1)} %stack.23.place, s32[16,16]{1,0:T(8,128)S(1)} %copy-done.2, bf16[512,512]{1,0:T(8,128)(2,1)S(1)} %copy-done, bf16[512,512]{1,0:T(8,128)(2,1)S(1)} %collective-permute-done.refs_1_, bf16[512,512]{1,0:T(8,128)(2,1)S(1)} %collective-permute-done.4.refs_2_, ...), custom_call_target="tpu_custom_call" | custom-call | tf_op jit(solution)/shard_map/give/pallas_call | solution.py:130
  77.5 0.1 collective-permute-start.18
  77.6 1.2 %give.3 = s16[272,512]{1,0:T(8,128)(2,1)S(1)} custom-call(s32[5]{0:T(128)S(1)} %stack.23.place, s32[16,16]{1,0:T(8,128)S(1)} %copy-done.2, bf16[512,512]{1,0:T(8,128)(2,1)S(1)} %copy-done, bf16[512,512]{1,0:T(8,128)(2,1)S(1)} %collective-permute-done.refs_1_, bf16[512,512]{1,0:T(8,128)(2,1)S(1)} %collective-permute-done.4.refs_2_, ...), custom_call_target="tpu_custom_call" | custom-call | tf_op jit(solution)/shard_map/give/pallas_call | solution.py:130
  78.8 1.5 %collective-permute-start.19 = (s16[272,512]{1,0:T(8,128)(2,1)S(1)}, s16[272,512]{1,0:T(8,128)(2,1)S(1)}, u32[]{:S(2)}, u32[]{:S(2)}) collective-permute-start(s16[272,512]{1,0:T(8,128)(2,1)S(1)} %give.3), channel_id=1, source_target_pairs={{0,16},{16,0},{1,17},{17,1},{2,18},{18,2},{3,19},{19,3},{4,20},{20... | collective-permute-start | bytes 835592 | tf_op jit(solution)/shard_map/ppermute | solution.py:37
  80.3 1.6 %keep.1 = f32[512,512]{1,0:T(8,128)S(1)} custom-call(s32[5]{0:T(128)S(1)} %stack.23.place, s32[16,16]{1,0:T(8,128)S(1)} %copy-done.2, bf16[512,512]{1,0:T(8,128)(2,1)S(1)} %copy-done, bf16[512,512]{1,0:T(8,128)(2,1)S(1)} %collective-permute-done.refs_1_, bf16[512,512]{1,0:T(8,128)(2,1)S(1)} %collective-permute-done.4.refs_2_, ...), custom_call_target="tpu_custom_call" | custom-call | tf_op jit(solution)/shard_map/keep/pallas_call | solution.py:130
  82.0 3.5 %collective-permute-done.18.refs_0_ = s16[272,512]{1,0:T(8,128)(2,1)S(1)} collective-permute-done((s16[272,512]{1,0:T(8,128)(2,1)S(1)}, s16[272,512]{1,0:T(8,128)(2,1)S(1)}, u32[]{:S(2)}, u32[]{:S(2)}) %collective-permute-start.18) | collective-permute-done | bytes 278560 | tf_op jit(solution)/shard_map/ppermute | solution.py:37
  85.4 6.0 %collective-permute-done.19.refs_1_ = s16[272,512]{1,0:T(8,128)(2,1)S(1)} collective-permute-done((s16[272,512]{1,0:T(8,128)(2,1)S(1)}, s16[272,512]{1,0:T(8,128)(2,1)S(1)}, u32[]{:S(2)}, u32[]{:S(2)}) %collective-permute-start.19) | collective-permute-done | bytes 278560 | tf_op jit(solution)/shard_map/ppermute | solution.py:37
  91.4 1.0 %join.1 = bf16[512,512]{1,0:T(8,128)(2,1)} custom-call(f32[512,512]{1,0:T(8,128)S(1)} %keep.1, s16[272,512]{1,0:T(8,128)(2,1)S(1)} %collective-permute-done.18.refs_0_, s16[272,512]{1,0:T(8,128)(2,1)S(1)} %collective-permute-done.19.refs_1_), custom_call_target="tpu_custom_call" | custom-call | tf_op jit(solution)/shard_map/join/pallas_call | solution.py:145
  (10 shorter events, 0.1 us)
Async XLA Ops:
  0.1 1.0 %copy-start.1 = (bf16[512,512]{1,0:T(8,128)(2,1)S(1)}, bf16[512,512]{1,0:T(8,128)(2,1)}, u32[]{:S(2)}) copy-start(bf16[512,512]{1,0:T(8,128)(2,1)} %factor.1) | copy-start | bytes 1572868
  1.1 6.9 %copy-start = (bf16[512,512]{1,0:T(8,128)(2,1)S(1)}, bf16[512,512]{1,0:T(8,128)(2,1)}, u32[]{:S(2)}) copy-start(bf16[512,512]{1,0:T(8,128)(2,1)} %refs_0_.5) | copy-start | bytes 1572868
  1.9 15.7 %collective-permute-start.3 = (bf16[512,512]{1,0:T(8,128)(2,1)S(1)}, bf16[512,512]{1,0:T(8,128)(2,1)S(1)}, u32[]{:S(2)}, u32[]{:S(2)}) collective-permute-start(bf16[512,512]{1,0:T(8,128)(2,1)S(1)} %masked.1), channel_id=1, source_target_pairs={{0,8},{1,24},{8,0},{9,16},{16,9},{17,25},{24,1},{25,17},{2,10},{3,... | collective-permute-start | bytes 1572872 | tf_op jit(solution)/shard_map/ppermute | solution.py:33
  6.1 12.5 %collective-permute-start.2 = (bf16[512,512]{1,0:T(8,128)(2,1)S(1)}, bf16[512,512]{1,0:T(8,128)(2,1)S(1)}, u32[]{:S(2)}, u32[]{:S(2)}) collective-permute-start(bf16[512,512]{1,0:T(8,128)(2,1)S(1)} %masked.1), channel_id=1, source_target_pairs={{0,0},{1,16},{8,8},{9,24},{16,1},{17,17},{24,9},{25,25},{2,2},{3,1... | collective-permute-start | bytes 1572872 | tf_op jit(solution)/shard_map/ppermute | solution.py:33
  8.1 17.2 %collective-permute-start.1 = (bf16[512,512]{1,0:T(8,128)(2,1)S(1)}, bf16[512,512]{1,0:T(8,128)(2,1)S(1)}, u32[]{:S(2)}, u32[]{:S(2)}) collective-permute-start(bf16[512,512]{1,0:T(8,128)(2,1)S(1)} %copy-done), channel_id=1, source_target_pairs={{0,224},{32,0},{64,32},{96,64},{128,96},{160,128},{192,160},{224,1... | collective-permute-start | bytes 1572872 | tf_op jit(solution)/shard_map/ppermute | solution.py:37
  13.7 15.1 %collective-permute-start = (bf16[512,512]{1,0:T(8,128)(2,1)S(1)}, bf16[512,512]{1,0:T(8,128)(2,1)S(1)}, u32[]{:S(2)}, u32[]{:S(2)}) collective-permute-start(bf16[512,512]{1,0:T(8,128)(2,1)S(1)} %copy-done), channel_id=1, source_target_pairs={{0,32},{32,64},{64,96},{96,128},{128,160},{160,192},{192,224},{224... | collective-permute-start | bytes 1572872 | tf_op jit(solution)/shard_map/ppermute | solution.py:37
  28.9 17.4 %collective-permute-start.6 = (bf16[1024,512]{1,0:T(8,128)(2,1)S(1)}, bf16[1024,512]{1,0:T(8,128)(2,1)S(1)}, u32[]{:S(2)}, u32[]{:S(2)}) collective-permute-start(bf16[1024,512]{1,0:T(8,128)(2,1)S(1)} %pack.2.refs_9_), channel_id=1, source_target_pairs={{0,1},{1,0},{2,3},{3,2},{4,5},{5,4},{6,7},{7,6},{8,9},{9,8},{10,11... | collective-permute-start | bytes 3145736 | tf_op jit(solution)/shard_map/ppermute | solution.py:37
  29.4 25.0 %collective-permute-start.10 = (bf16[1024,512]{1,0:T(8,128)(2,1)S(1)}, bf16[1024,512]{1,0:T(8,128)(2,1)S(1)}, u32[]{:S(2)}, u32[]{:S(2)}) collective-permute-start(bf16[1024,512]{1,0:T(8,128)(2,1)S(1)} %pack.2.refs_9_), channel_id=1, source_target_pairs={{0,6},{2,0},{4,2},{6,4},{1,7},{3,1},{5,3},{7,5},{8,14},{10,8},{12,... | collective-permute-start | bytes 3145736 | tf_op jit(solution)/shard_map/ppermute | solution.py:37
  31.9 26.0 %collective-permute-start.9 = (bf16[1024,512]{1,0:T(8,128)(2,1)S(1)}, bf16[1024,512]{1,0:T(8,128)(2,1)S(1)}, u32[]{:S(2)}, u32[]{:S(2)}) collective-permute-start(bf16[1024,512]{1,0:T(8,128)(2,1)S(1)} %pack.2.refs_9_), channel_id=1, source_target_pairs={{0,2},{2,4},{4,6},{6,0},{1,3},{3,5},{5,7},{7,1},{8,10},{10,12},{12... | collective-permute-start | bytes 3145736 | tf_op jit(solution)/shard_map/ppermute | solution.py:37
  31.9 14.4 %collective-permute-start.4 = (bf16[512,512]{1,0:T(8,128)(2,1)S(1)}, bf16[512,512]{1,0:T(8,128)(2,1)S(1)}, u32[]{:S(2)}, u32[]{:S(2)}) collective-permute-start(bf16[512,512]{1,0:T(8,128)(2,1)S(1)} %collective-permute-done.refs_1_), channel_id=1, source_target_pairs={{0,32},{32,64},{64,96},{96,128},{128,160},{160,192},{192,224},{224... | collective-permute-start | bytes 1572872 | tf_op jit(solution)/shard_map/ppermute | solution.py:37
  31.9 14.4 %collective-permute-start.5 = (bf16[512,512]{1,0:T(8,128)(2,1)S(1)}, bf16[512,512]{1,0:T(8,128)(2,1)S(1)}, u32[]{:S(2)}, u32[]{:S(2)}) collective-permute-start(bf16[512,512]{1,0:T(8,128)(2,1)S(1)} %collective-permute-done.1.refs_6_), channel_id=1, source_target_pairs={{0,224},{32,0},{64,32},{96,64},{128,96},{160,128},{192,160},{224,1... | collective-permute-start | bytes 1572872 | tf_op jit(solution)/shard_map/ppermute | solution.py:37
  46.3 13.4 %collective-permute-start.7 = (bf16[512,512]{1,0:T(8,128)(2,1)S(1)}, bf16[512,512]{1,0:T(8,128)(2,1)S(1)}, u32[]{:S(2)}, u32[]{:S(2)}) collective-permute-start(bf16[512,512]{1,0:T(8,128)(2,1)S(1)} %collective-permute-done.4.refs_2_), channel_id=1, source_target_pairs={{0,32},{32,64},{64,96},{96,128},{128,160},{160,192},{192,224},{224... | collective-permute-start | bytes 1572872 | tf_op jit(solution)/shard_map/ppermute | solution.py:37
  46.3 13.4 %collective-permute-start.8 = (bf16[512,512]{1,0:T(8,128)(2,1)S(1)}, bf16[512,512]{1,0:T(8,128)(2,1)S(1)}, u32[]{:S(2)}, u32[]{:S(2)}) collective-permute-start(bf16[512,512]{1,0:T(8,128)(2,1)S(1)} %collective-permute-done.5.refs_5_), channel_id=1, source_target_pairs={{0,224},{32,0},{64,32},{96,64},{128,96},{160,128},{192,160},{224,1... | collective-permute-start | bytes 1572872 | tf_op jit(solution)/shard_map/ppermute | solution.py:37
  54.5 13.9 %collective-permute-start.14 = (bf16[512,512]{1,0:T(8,128)(2,1)S(1)}, bf16[512,512]{1,0:T(8,128)(2,1)S(1)}, u32[]{:S(2)}, u32[]{:S(2)}) collective-permute-start(bf16[512,512]{1,0:T(8,128)(2,1)S(1)} %slice.17), channel_id=1, source_target_pairs={{0,6},{2,0},{4,2},{6,4},{1,7},{3,1},{5,3},{7,5},{8,14},{10,8},{12,... | collective-permute-start | bytes 1572872 | tf_op jit(solution)/shard_map/ppermute | solution.py:37
  58.0 13.6 %collective-permute-start.13 = (bf16[512,512]{1,0:T(8,128)(2,1)S(1)}, bf16[512,512]{1,0:T(8,128)(2,1)S(1)}, u32[]{:S(2)}, u32[]{:S(2)}) collective-permute-start(bf16[512,512]{1,0:T(8,128)(2,1)S(1)} %slice.16), channel_id=1, source_target_pairs={{0,2},{2,4},{4,6},{6,0},{1,3},{3,5},{5,7},{7,1},{8,10},{10,12},{12... | collective-permute-start | bytes 1572872 | tf_op jit(solution)/shard_map/ppermute | solution.py:37
  59.8 16.5 %copy-start.2 = (s32[16,16]{1,0:T(8,128)S(1)}, s32[16,16]{1,0:T(8,128)}, u32[]{:S(2)}) copy-start(s32[16,16]{1,0:T(8,128)} %occupancy.5) | copy-start | bytes 3076
  59.8 11.8 %collective-permute-start.12 = (bf16[256,512]{1,0:T(8,128)(2,1)S(1)}, bf16[256,512]{1,0:T(8,128)(2,1)S(1)}, u32[]{:S(2)}, u32[]{:S(2)}) collective-permute-start(bf16[256,512]{1,0:T(8,128)(2,1)S(1)} %slice.13), channel_id=1, source_target_pairs={{0,224},{32,0},{64,32},{96,64},{128,96},{160,128},{192,160},{224,1... | collective-permute-start | bytes 786440 | tf_op jit(solution)/shard_map/ppermute | solution.py:37
  62.3 9.3 %collective-permute-start.11 = (bf16[256,512]{1,0:T(8,128)(2,1)S(1)}, bf16[256,512]{1,0:T(8,128)(2,1)S(1)}, u32[]{:S(2)}, u32[]{:S(2)}) collective-permute-start(bf16[256,512]{1,0:T(8,128)(2,1)S(1)} %slice.12), channel_id=1, source_target_pairs={{0,32},{32,64},{64,96},{96,128},{128,160},{160,192},{192,224},{224... | collective-permute-start | bytes 786440 | tf_op jit(solution)/shard_map/ppermute | solution.py:37
  62.3 11.7 %collective-permute-start.15 = (bf16[1024,512]{1,0:T(8,128)(2,1)S(1)}, bf16[1024,512]{1,0:T(8,128)(2,1)S(1)}, u32[]{:S(2)}, u32[]{:S(2)}) collective-permute-start(bf16[1024,512]{1,0:T(8,128)(2,1)S(1)} %collective-permute-done.9.refs_10_), channel_id=1, source_target_pairs={{0,1},{1,0},{2,3},{3,2},{4,5},{5,4},{6,7},{7,6},{8,9},{9,8},{10,11... | collective-permute-start | bytes 3145736 | tf_op jit(solution)/shard_map/ppermute | solution.py:37
  68.3 5.7 %collective-permute-start.16 = (bf16[1024,512]{1,0:T(8,128)(2,1)S(1)}, bf16[1024,512]{1,0:T(8,128)(2,1)S(1)}, u32[]{:S(2)}, u32[]{:S(2)}) collective-permute-start(bf16[1024,512]{1,0:T(8,128)(2,1)S(1)} %collective-permute-done.10.refs_11_), channel_id=1, source_target_pairs={{0,1},{1,0},{2,3},{3,2},{4,5},{5,4},{6,7},{7,6},{8,9},{9,8},{10,11... | collective-permute-start | bytes 3145736 | tf_op jit(solution)/shard_map/ppermute | solution.py:37
  71.6 4.6 %collective-permute-start.17 = (bf16[1024,512]{1,0:T(8,128)(2,1)S(1)}, bf16[1024,512]{1,0:T(8,128)(2,1)S(1)}, u32[]{:S(2)}, u32[]{:S(2)}) collective-permute-start(bf16[1024,512]{1,0:T(8,128)(2,1)S(1)} %pack.3), channel_id=1, source_target_pairs={{0,1},{1,0},{2,3},{3,2},{4,5},{5,4},{6,7},{7,6},{8,9},{9,8},{10,11... | collective-permute-start | bytes 3145736 | tf_op jit(solution)/shard_map/ppermute | solution.py:37
  77.5 8.0 %collective-permute-start.18 = (s16[272,512]{1,0:T(8,128)(2,1)S(1)}, s16[272,512]{1,0:T(8,128)(2,1)S(1)}, u32[]{:S(2)}, u32[]{:S(2)}) collective-permute-start(s16[272,512]{1,0:T(8,128)(2,1)S(1)} %give.2), channel_id=1, source_target_pairs={{0,16},{16,0},{1,17},{17,1},{2,18},{18,2},{3,19},{19,3},{4,20},{20... | collective-permute-start | bytes 835592 | tf_op jit(solution)/shard_map/ppermute | solution.py:37
  78.8 12.6 %collective-permute-start.19 = (s16[272,512]{1,0:T(8,128)(2,1)S(1)}, s16[272,512]{1,0:T(8,128)(2,1)S(1)}, u32[]{:S(2)}, u32[]{:S(2)}) collective-permute-start(s16[272,512]{1,0:T(8,128)(2,1)S(1)} %give.3), channel_id=1, source_target_pairs={{0,16},{16,0},{1,17},{17,1},{2,18},{18,2},{3,19},{19,3},{4,20},{20... | collective-permute-start | bytes 835592 | tf_op jit(solution)/shard_map/ppermute | solution.py:37

commit v5 on v4

--- a/solution.py
+++ b/solution.py
@@ -9,8 +9,8 @@
 from jax.sharding import PartitionSpec as P
 
 TILE = 512
-PARTS = 2
-SIZE = TILE // PARTS
+HALF = TILE // 2
+PARTS = ((0, 128), (128, 384))
 EXTRA = 16
 LARGEST = 32000.0
 COLUMN = ("yl", "yh", "c")
@@ -49,12 +49,12 @@
     return shift("yl", 2, piece, 1)
 
 
-def call(kernel, out, scratch, specs, name):
+def call(kernel, out, scratch, specs, name, out_specs=VMEM):
     return pl.pallas_call(
         kernel,
         out_shape=out,
         in_specs=specs,
-        out_specs=VMEM,
+        out_specs=out_specs,
         scratch_shapes=scratch,
         compiler_params=pltpu.CompilerParams(vmem_limit_bytes=40 * 1024 * 1024),
         name=name,
@@ -76,41 +76,66 @@
 
 
 def pack_kernel(*refs):
-    for n, ref in enumerate(refs[:-1]):
-        refs[-1][n * TILE : (n + 1) * TILE, :] = ref[...]
+    at = 0
+    for ref in refs[:-1]:
+        refs[-1][at : at + ref.shape[0], :] = ref[...]
+        at += ref.shape[0]
 
 
 def pack(*tiles):
-    out = jax.ShapeDtypeStruct((len(tiles) * TILE, TILE), tiles[0].dtype)
+    out = jax.ShapeDtypeStruct((sum(tile.shape[0] for tile in tiles), TILE), tiles[0].dtype)
     return call(pack_kernel, out, [], [VMEM] * len(tiles), "pack")(*tiles)
 
 
-def sums_kernel(given, begin, size, packs, place, occupancy, *refs):
-    refs, (out, total, slots) = refs[:-3], refs[-3:]
-    draws, halves, packed = refs[:7], refs[7:9], refs[9:]
+def add_up(row, ready, begin, size, packs, place, occupancy, draws, halves, packed, total, slots):
     own, other = {}, {}
     for tiles, refs in ((own, packed[: len(packs[0])]), (other, packed[len(packs[0]) :])):
         for ref, pack in zip(refs, packs[tiles is other]):
             for n, piece in enumerate(pack):
                 tiles[piece] = ref.at[n * TILE : (n + 1) * TILE, :]
     z, yl, yh, x, c = (place[n] for n in range(5))
-    row = 1 - yl if given else yl
     for n, slot in enumerate((0, 1, 2, 3, 5, 6, 7)):
         slots[slot] = draws[n][begin : begin + size, :]
-    for part in range(size // SIZE):
-        slots[4, part * SIZE : (part + 1) * SIZE, :] = halves[begin // SIZE + part][...]
-    total[...] = jnp.zeros_like(total)
-    for n, (across, by) in enumerate(PIECES):
+    for n, half in enumerate(halves):
+        low, high = max(begin, n * HALF), min(begin + size, (n + 1) * HALF)
+        if low < high:
+            slots[4, low - begin : high - begin, :] = half[low - n * HALF : high - n * HALF, :]
+    for n, (across, by) in enumerate(PIECES[:6] if ready else PIECES):
         block = (1 - yh if across else yh) * 4 + ((x + by) & 3)
         column = 2 * block + yl
+        slot = (z - block) & 7
         held = (occupancy[2 * z + row, column] == 1) & (column <= 2 * z + row)
-        slot = (z - block) & 7
+        if ready:
+            held &= slot != 4
+        elif n < 6:
+            held &= slot == 4
         for where, ref in ((row == c, own[n]), (row != c, other[n])):
 
             @pl.when(held & where)
             def _(slot=slot, ref=ref):
                 total[...] += jnp.dot(slots[slot], ref[...], preferred_element_type=jnp.float32)
 
+
+def early_kernel(packs, place, occupancy, *refs):
+    draws, packed, (give, keep, slots) = refs[:7], refs[7:-3], refs[-3:]
+    for row, total in ((1 - place[1], give), (place[1], keep)):
+        total[...] = jnp.zeros_like(total)
+        add_up(row, True, 0, TILE, packs, place, occupancy, draws, (), packed, total, slots)
+
+
+def early(packs, *args):
+    out = jax.ShapeDtypeStruct((TILE, TILE), jnp.float32)
+    specs = [SMEM] * 2 + [VMEM] * (len(args) - 2)
+    scratch = [pltpu.VMEM((8, TILE, TILE), jnp.bfloat16)]
+    kernel = functools.partial(early_kernel, packs)
+    return call(kernel, (out, out), scratch, specs, "early", (VMEM, VMEM))(*args)
+
+
+def late_kernel(given, begin, size, packs, place, occupancy, so_far, *refs):
+    draws, halves, packed, (out, total, slots) = refs[:7], refs[7:9], refs[9:-3], refs[-3:]
+    total[...] = so_far[begin : begin + size, :]
+    row = 1 - place[1] if given else place[1]
+    add_up(row, False, begin, size, packs, place, occupancy, draws, halves, packed, total, slots)
     if not given:
         out[...] = total[...]
         return
@@ -123,26 +148,26 @@
     out[size:, :] = powers.astype(jnp.int32).astype(jnp.int16)
 
 
-def sums(given, begin, size, packs, out, *args):
+def late(given, begin, size, packs, out, *args):
     scratch = [pltpu.VMEM((size, TILE), jnp.float32), pltpu.VMEM((8, size, TILE), jnp.bfloat16)]
-    kernel = functools.partial(sums_kernel, given, begin, size, packs)
+    kernel = functools.partial(late_kernel, given, begin, size, packs)
     specs = [SMEM] * 2 + [VMEM] * (len(args) - 2)
     return call(kernel, out, scratch, specs, "give" if given else "keep")(*args)
 
 
 def join_kernel(keep, *refs):
     out = refs[-1]
-    for part, sent in enumerate(refs[:-1]):
-        rows = slice(part * SIZE, (part + 1) * SIZE)
-        power = sent[SIZE:, :].astype(jnp.int32).astype(jnp.float32).reshape(EXTRA, 1, TILE)
-        codes = sent[:SIZE, :].astype(jnp.int32).astype(jnp.float32).reshape(EXTRA, SIZE // EXTRA, TILE)
-        crossed = (codes * jnp.exp2(-power)).reshape(SIZE, TILE)
+    for sent, (begin, size) in zip(refs, PARTS):
+        rows = slice(begin, begin + size)
+        power = sent[size:, :].astype(jnp.int32).astype(jnp.float32).reshape(EXTRA, 1, TILE)
+        codes = sent[:size, :].astype(jnp.int32).astype(jnp.float32).reshape(EXTRA, size // EXTRA, TILE)
+        crossed = (codes * jnp.exp2(-power)).reshape(size, TILE)
         out[rows, :] = (keep[rows, :] + crossed).astype(out.dtype)
 
 
 def join(keep, crossed):
     out = jax.ShapeDtypeStruct((TILE, TILE), jnp.bfloat16)
-    return call(join_kernel, out, [], [VMEM] * (1 + PARTS), "join")(keep, *crossed)
+    return call(join_kernel, out, [], [VMEM] * (1 + len(crossed)), "join")(keep, *crossed)
 
 
 def local(draws, factor, occupancy):
@@ -155,21 +180,24 @@
     pair = pack(near, far)
     up2, down2 = along_z(up1, 1), along_z(down1, -1)
     before, after = along_x(pair, 1), along_x(pair, -1)
-    pair_c = other_core(pair)
-    up2, down2, pair_c = together((up2, down2, pair_c))
+    up2, down2 = together((up2, down2))
     up3, down3 = along_z(up2, 1), along_z(down2, -1)
     near_o, far_o = along_x(before[:TILE], 1), along_x(after[TILE:], -1)
     up3, down3, before, after = together((up3, down3, before, after))
-    up4, down4 = along_z(up3[:SIZE], 1), along_z(down3[SIZE:], -1)
-    before_c, after_c = other_core(before), other_core(after)
+    up4, down4 = along_z(up3[:HALF], 1), along_z(down3[HALF:], -1)
+    pair_c, before_c, after_c = other_core(pair), other_core(before), other_core(after)
     up4, down4, near_o, far_o = together((up4, down4, near_o, far_o))
     last_c = other_core(pack(near_o, far_o))
-    packs = ((0, 1), (2, 3), (4, 5), (6,), (7,)), ((0, 1), (2, 3), (4, 5), (6, 7))
-    args = (place, occupancy, draws, up1, up2, up3, down3, down2, down1, up4, down4)
-    args += (pair, before, after, near_o, far_o, pair_c, before_c, after_c, last_c)
-    coded = jax.ShapeDtypeStruct((SIZE + EXTRA, TILE), jnp.int16)
-    crossed = [other_chip(sums(True, part * SIZE, SIZE, packs, coded, *args)) for part in range(PARTS)]
-    keep = sums(False, 0, TILE, packs, jax.ShapeDtypeStruct((TILE, TILE), jnp.float32), *args)
+    circled = (draws, up1, up2, up3, down3, down2, down1)
+    ready = ((0, 1), (2, 3), (4, 5))
+    give, keep = early((ready, ready), place, occupancy, *circled, pair, before, after, pair_c, before_c, after_c)
+    packs = ready + ((6,), (7,)), ready + ((6, 7),)
+    args = (*circled, up4, down4, pair, before, after, near_o, far_o, pair_c, before_c, after_c, last_c)
+    crossed = []
+    for begin, size in PARTS:
+        coded = jax.ShapeDtypeStruct((size + EXTRA, TILE), jnp.int16)
+        crossed.append(other_chip(late(True, begin, size, packs, coded, place, occupancy, give, *args)))
+    keep = late(False, 0, TILE, packs, jax.ShapeDtypeStruct((TILE, TILE), jnp.float32), place, occupancy, keep, *args)
     return join(keep, crossed)
 
 

time: 92.5 us -> 89.3 us (0.965)
  waiting for transfers between devices: 50.4 us -> 43.3 us
  Pallas kernels: 5.97 us -> 8.71 us
  starting transfers between devices: 34.6 us -> 35.9 us
    ppermute x18, waiting for transfers between devices: 45.5 us -> 35 us  [shift(): lax.ppermute(piece, name, [(i, (i + by) % count) for i in range(count)])]
    ppermute x2, waiting for transfers between devices: 4.96 us -> 8.28 us  [to_parity(): return lax.ppermute(tile, COLUMN, pairs)]
    pallas_call x4 -> x5, Pallas kernels: 5.05 us -> 7.78 us  [the longest x3 4.43 us: late(): return call(kernel, out, scratch, specs, 'give' if given else 'keep')(*args)]
    ppermute x18, starting transfers between devices: 28.5 us -> 29.6 us  [shift(): lax.ppermute(piece, name, [(i, (i + by) % count) for i in range(count)])]
  transfers between devices with their start and end apart: 20 -> 20, of which waited for: 12 -> 11; matrix products, arithmetic and copies ran while one was open for 0% -> 0% of each run, Pallas kernels for 3% -> 6%
where the time goes in v5:
time: 89.3 us
  waiting for transfers between devices  43.3 us (48%)
  starting transfers between devices  35.9 us (40%)
  Pallas kernels  8.71 us (10%)
  local copies, waits for them, and re-layouts  1.25 us (1%)
    ppermute x18, waiting for transfers between devices, shift(): lax.ppermute(piece, name, [(i, (i + by) % count) for i in range(count)])  35 us
    ppermute x18, starting transfers between devices, shift(): lax.ppermute(piece, name, [(i, (i + by) % count) for i in range(count)])  29.6 us
    ppermute x2, waiting for transfers between devices, to_parity(): return lax.ppermute(tile, COLUMN, pairs)  8.28 us
    ppermute x2, starting transfers between devices, to_parity(): return lax.ppermute(tile, COLUMN, pairs)  6.3 us
    pallas_call x3, Pallas kernels, late(): return call(kernel, out, scratch, specs, 'give' if given else 'keep')(*args)  4.43 us
    pallas_call x1, Pallas kernels, early(): call(kernel, (out, out), scratch, specs, 'early', (VMEM, VMEM))(*args)  2.36 us
  transfers between devices with their start and end apart: 20, of which 11 were waited for; matrix products, arithmetic and copies ran while one was open for 0% of the time, Pallas kernels for 6%

profile of v5, /device:TPU:1, one launch (start us, length us, event | category | flops | bytes accessed | tf_op | source)
XLA Modules:
  0.0 89.3 jit_solution(4813147728282158619)
XLA Ops:
  0.0 0.1 stack.23.place
  0.1 1.0 %copy-done.2 = bf16[512,512]{1,0:T(8,128)(2,1)S(1)} copy-done((bf16[512,512]{1,0:T(8,128)(2,1)S(1)}, bf16[512,512]{1,0:T(8,128)(2,1)}, u32[]{:S(2)}) %copy-start.2) | copy-done | bytes 524312
  1.1 0.8 masked.1
  1.9 4.6 %collective-permute-start.2 = (bf16[512,512]{1,0:T(8,128)(2,1)S(1)}, bf16[512,512]{1,0:T(8,128)(2,1)S(1)}, u32[]{:S(2)}, u32[]{:S(2)}) collective-permute-start(bf16[512,512]{1,0:T(8,128)(2,1)S(1)} %masked.1), channel_id=1, source_target_pairs={{0,0},{1,16},{8,8},{9,24},{16,1},{17,17},{24,9},{25,25},{2,2},{3,1... | collective-permute-start | bytes 1572872 | tf_op jit(solution)/shard_map/ppermute | solution.py:33
  6.5 1.7 %collective-permute-start.3 = (bf16[512,512]{1,0:T(8,128)(2,1)S(1)}, bf16[512,512]{1,0:T(8,128)(2,1)S(1)}, u32[]{:S(2)}, u32[]{:S(2)}) collective-permute-start(bf16[512,512]{1,0:T(8,128)(2,1)S(1)} %masked.1), channel_id=1, source_target_pairs={{0,8},{1,24},{8,0},{9,16},{16,9},{17,25},{24,1},{25,17},{2,10},{3,... | collective-permute-start | bytes 1572872 | tf_op jit(solution)/shard_map/ppermute | solution.py:33
  8.2 1.6 %collective-permute-start = (bf16[512,512]{1,0:T(8,128)(2,1)S(1)}, bf16[512,512]{1,0:T(8,128)(2,1)S(1)}, u32[]{:S(2)}, u32[]{:S(2)}) collective-permute-start(bf16[512,512]{1,0:T(8,128)(2,1)S(1)} %copy-done.1), channel_id=1, source_target_pairs={{0,32},{32,64},{64,96},{96,128},{128,160},{160,192},{192,224},{224... | collective-permute-start | bytes 1572872 | tf_op jit(solution)/shard_map/ppermute | solution.py:37
  9.9 3.9 %collective-permute-start.1 = (bf16[512,512]{1,0:T(8,128)(2,1)S(1)}, bf16[512,512]{1,0:T(8,128)(2,1)S(1)}, u32[]{:S(2)}, u32[]{:S(2)}) collective-permute-start(bf16[512,512]{1,0:T(8,128)(2,1)S(1)} %copy-done.1), channel_id=1, source_target_pairs={{0,224},{32,0},{64,32},{96,64},{128,96},{160,128},{192,160},{224,1... | collective-permute-start | bytes 1572872 | tf_op jit(solution)/shard_map/ppermute | solution.py:37
  13.8 5.4 %collective-permute-done.2.refs_0_ = bf16[512,512]{1,0:T(8,128)(2,1)S(1)} collective-permute-done((bf16[512,512]{1,0:T(8,128)(2,1)S(1)}, bf16[512,512]{1,0:T(8,128)(2,1)S(1)}, u32[]{:S(2)}, u32[]{:S(2)}) %collective-permute-start.2) | collective-permute-done | bytes 524320 | tf_op jit(solution)/shard_map/ppermute | solution.py:33
  19.3 2.9 %collective-permute-done.3.refs_1_ = bf16[512,512]{1,0:T(8,128)(2,1)S(1)} collective-permute-done((bf16[512,512]{1,0:T(8,128)(2,1)S(1)}, bf16[512,512]{1,0:T(8,128)(2,1)S(1)}, u32[]{:S(2)}, u32[]{:S(2)}) %collective-permute-start.3) | collective-permute-done | bytes 524320 | tf_op jit(solution)/shard_map/ppermute | solution.py:33
  22.1 3.3 %collective-permute-done.refs_1_ = bf16[512,512]{1,0:T(8,128)(2,1)S(1)} collective-permute-done((bf16[512,512]{1,0:T(8,128)(2,1)S(1)}, bf16[512,512]{1,0:T(8,128)(2,1)S(1)}, u32[]{:S(2)}, u32[]{:S(2)}) %collective-permute-start) | collective-permute-done | bytes 524320 | tf_op jit(solution)/shard_map/ppermute | solution.py:37
  25.4 0.0 collective-permute-done.1.refs_6_
  25.4 0.1 pack.2.refs_7_.refs_9_
  25.4 1.3 %collective-permute-start.8 = (bf16[1024,512]{1,0:T(8,128)(2,1)S(1)}, bf16[1024,512]{1,0:T(8,128)(2,1)S(1)}, u32[]{:S(2)}, u32[]{:S(2)}) collective-permute-start(bf16[1024,512]{1,0:T(8,128)(2,1)S(1)} %pack.2.refs_7_.refs_9_), channel_id=1, source_target_pairs={{0,2},{2,4},{4,6},{6,0},{1,3},{3,5},{5,7},{7,1},{8,10},{10,12},{12... | collective-permute-start | bytes 3145736 | tf_op jit(solution)/shard_map/ppermute | solution.py:37
  26.7 1.5 %collective-permute-start.9 = (bf16[1024,512]{1,0:T(8,128)(2,1)S(1)}, bf16[1024,512]{1,0:T(8,128)(2,1)S(1)}, u32[]{:S(2)}, u32[]{:S(2)}) collective-permute-start(bf16[1024,512]{1,0:T(8,128)(2,1)S(1)} %pack.2.refs_7_.refs_9_), channel_id=1, source_target_pairs={{0,6},{2,0},{4,2},{6,4},{1,7},{3,1},{5,3},{7,5},{8,14},{10,8},{12,... | collective-permute-start | bytes 3145736 | tf_op jit(solution)/shard_map/ppermute | solution.py:37
  28.2 0.0 collective-permute-start.4
  28.2 3.0 %collective-permute-start.5 = (bf16[512,512]{1,0:T(8,128)(2,1)S(1)}, bf16[512,512]{1,0:T(8,128)(2,1)S(1)}, u32[]{:S(2)}, u32[]{:S(2)}) collective-permute-start(bf16[512,512]{1,0:T(8,128)(2,1)S(1)} %collective-permute-done.1.refs_6_), channel_id=1, source_target_pairs={{0,224},{32,0},{64,32},{96,64},{128,96},{160,128},{192,160},{224,1... | collective-permute-start | bytes 1572872 | tf_op jit(solution)/shard_map/ppermute | solution.py:37
  31.2 11.3 %collective-permute-done.4.refs_2_ = bf16[512,512]{1,0:T(8,128)(2,1)S(1)} collective-permute-done((bf16[512,512]{1,0:T(8,128)(2,1)S(1)}, bf16[512,512]{1,0:T(8,128)(2,1)S(1)}, u32[]{:S(2)}, u32[]{:S(2)}) %collective-permute-start.4) | collective-permute-done | bytes 524320 | tf_op jit(solution)/shard_map/ppermute | solution.py:37
  42.5 0.0 collective-permute-done.5.refs_5_
  42.5 2.3 %collective-permute-start.6 = (bf16[512,512]{1,0:T(8,128)(2,1)S(1)}, bf16[512,512]{1,0:T(8,128)(2,1)S(1)}, u32[]{:S(2)}, u32[]{:S(2)}) collective-permute-start(bf16[512,512]{1,0:T(8,128)(2,1)S(1)} %collective-permute-done.4.refs_2_), channel_id=1, source_target_pairs={{0,32},{32,64},{64,96},{96,128},{128,160},{160,192},{192,224},{224... | collective-permute-start | bytes 1572872 | tf_op jit(solution)/shard_map/ppermute | solution.py:37
  44.8 0.3 collective-permute-start.7
  45.2 6.3 %collective-permute-done.8.refs_8_.refs_10_ = bf16[1024,512]{1,0:T(8,128)(2,1)S(1)} collective-permute-done((bf16[1024,512]{1,0:T(8,128)(2,1)S(1)}, bf16[1024,512]{1,0:T(8,128)(2,1)S(1)}, u32[]{:S(2)}, u32[]{:S(2)}) %collective-permute-start.8) | collective-permute-done | bytes 1048608 | tf_op jit(solution)/shard_map/ppermute | solution.py:37
  51.5 0.1 collective-permute-start.15
  51.6 2.7 %collective-permute-start.16 = (bf16[512,512]{1,0:T(8,128)(2,1)S(1)}, bf16[512,512]{1,0:T(8,128)(2,1)S(1)}, u32[]{:S(2)}, u32[]{:S(2)}) collective-permute-start(bf16[512,512]{1,0:T(8,128)(2,1)S(1)} %slice.17), channel_id=1, source_target_pairs={{0,6},{2,0},{4,2},{6,4},{1,7},{3,1},{5,3},{7,5},{8,14},{10,8},{12,... | collective-permute-start | bytes 1572872 | tf_op jit(solution)/shard_map/ppermute | solution.py:37
  54.4 1.2 %collective-permute-done.6.refs_3_ = bf16[512,512]{1,0:T(8,128)(2,1)S(1)} collective-permute-done((bf16[512,512]{1,0:T(8,128)(2,1)S(1)}, bf16[512,512]{1,0:T(8,128)(2,1)S(1)}, u32[]{:S(2)}, u32[]{:S(2)}) %collective-permute-start.6) | collective-permute-done | bytes 524320 | tf_op jit(solution)/shard_map/ppermute | solution.py:37
  55.6 0.5 collective-permute-done.7.refs_4_
  56.1 1.0 %collective-permute-start.13 = (bf16[256,512]{1,0:T(8,128)(2,1)S(1)}, bf16[256,512]{1,0:T(8,128)(2,1)S(1)}, u32[]{:S(2)}, u32[]{:S(2)}) collective-permute-start(bf16[256,512]{1,0:T(8,128)(2,1)S(1)} %slice.12), channel_id=1, source_target_pairs={{0,32},{32,64},{64,96},{96,128},{128,160},{160,192},{192,224},{224... | collective-permute-start | bytes 786440 | tf_op jit(solution)/shard_map/ppermute | solution.py:37
  57.2 0.0 copy-start.3
  57.2 1.8 %collective-permute-start.14 = (bf16[256,512]{1,0:T(8,128)(2,1)S(1)}, bf16[256,512]{1,0:T(8,128)(2,1)S(1)}, u32[]{:S(2)}, u32[]{:S(2)}) collective-permute-start(bf16[256,512]{1,0:T(8,128)(2,1)S(1)} %slice.13), channel_id=1, source_target_pairs={{0,224},{32,0},{64,32},{96,64},{128,96},{160,128},{192,160},{224,1... | collective-permute-start | bytes 786440 | tf_op jit(solution)/shard_map/ppermute | solution.py:37
  59.0 3.6 %collective-permute-start.10 = (bf16[1024,512]{1,0:T(8,128)(2,1)S(1)}, bf16[1024,512]{1,0:T(8,128)(2,1)S(1)}, u32[]{:S(2)}, u32[]{:S(2)}) collective-permute-start(bf16[1024,512]{1,0:T(8,128)(2,1)S(1)} %pack.2.refs_7_.refs_9_), channel_id=1, source_target_pairs={{0,1},{1,0},{2,3},{3,2},{4,5},{5,4},{6,7},{7,6},{8,9},{9,8},{10,11... | collective-permute-start | bytes 3145736 | tf_op jit(solution)/shard_map/ppermute | solution.py:37
  62.6 0.3 collective-permute-done.13.refs_7_
  62.9 3.9 %collective-permute-start.11 = (bf16[1024,512]{1,0:T(8,128)(2,1)S(1)}, bf16[1024,512]{1,0:T(8,128)(2,1)S(1)}, u32[]{:S(2)}, u32[]{:S(2)}) collective-permute-start(bf16[1024,512]{1,0:T(8,128)(2,1)S(1)} %collective-permute-done.8.refs_8_.refs_10_), channel_id=1, source_target_pairs={{0,1},{1,0},{2,3},{3,2},{4,5},{5,4},{6,7},{7,6},{8,9},{9,8},{10,11... | collective-permute-start | bytes 3145736 | tf_op jit(solution)/shard_map/ppermute | solution.py:37
  66.9 0.0 collective-permute-done.14.refs_8_
  66.9 0.4 collective-permute-start.12
  67.2 0.0 collective-permute-done.15.refs_0_.refs_12_
  67.3 0.0 collective-permute-done.16.refs_1_.refs_13_
  67.3 0.1 pack.3
  67.3 0.4 collective-permute-start.17
  67.7 0.0 collective-permute-done.10.refs_10_.refs_14_
  67.7 1.4 %collective-permute-done.11.refs_11_.refs_15_ = bf16[1024,512]{1,0:T(8,128)(2,1)S(1)} collective-permute-done((bf16[1024,512]{1,0:T(8,128)(2,1)S(1)}, bf16[1024,512]{1,0:T(8,128)(2,1)S(1)}, u32[]{:S(2)}, u32[]{:S(2)}) %collective-permute-start.11) | collective-permute-done | bytes 1048608 | tf_op jit(solution)/shard_map/ppermute | solution.py:37
  69.1 1.5 %collective-permute-done.12.refs_12_.refs_16_ = bf16[1024,512]{1,0:T(8,128)(2,1)S(1)} collective-permute-done((bf16[1024,512]{1,0:T(8,128)(2,1)S(1)}, bf16[1024,512]{1,0:T(8,128)(2,1)S(1)}, u32[]{:S(2)}, u32[]{:S(2)}) %collective-permute-start.12) | collective-permute-done | bytes 1048608 | tf_op jit(solution)/shard_map/ppermute | solution.py:37
  70.6 2.4 %early.1 = (f32[512,512]{1,0:T(8,128)S(1)}, f32[512,512]{1,0:T(8,128)S(1)}) custom-call(s32[5]{0:T(128)S(1)} %stack.23.place, s32[16,16]{1,0:T(8,128)S(1)} %copy-done.3, bf16[512,512]{1,0:T(8,128)(2,1)S(1)} %copy-done.1, bf16[512,512]{1,0:T(8,128)(2,1)S(1)} %collective-permute-done.refs_1_, bf16[512,512]{1,0:T(8,128)(2,1)S(1)} %collective-permute-done.4.refs_2_, ...), custom_call_target="tpu_custom_call" | custom-call | tf_op jit(solution)/shard_map/early/pallas_call | solution.py:131
  73.0 1.3 %give.3 = s16[400,512]{1,0:T(8,128)(2,1)S(1)} custom-call(s32[5]{0:T(128)S(1)} %stack.23.place, s32[16,16]{1,0:T(8,128)S(1)} %copy-done.3, f32[512,512]{1,0:T(8,128)S(1)} %get-tuple-element.36.so_far, bf16[512,512]{1,0:T(8,128)(2,1)S(1)} %copy-done.1, bf16[512,512]{1,0:T(8,128)(2,1)S(1)} %collective-permute-done.refs_1_, ...), custom_call_target="tpu_custom_call" | custom-call | tf_op jit(solution)/shard_map/give/pallas_call | solution.py:155
  74.4 0.1 collective-permute-start.19
  74.5 1.3 %give.2 = s16[144,512]{1,0:T(8,128)(2,1)S(1)} custom-call(s32[5]{0:T(128)S(1)} %stack.23.place, s32[16,16]{1,0:T(8,128)S(1)} %copy-done.3, f32[512,512]{1,0:T(8,128)S(1)} %get-tuple-element.36.so_far, bf16[512,512]{1,0:T(8,128)(2,1)S(1)} %copy-done.1, bf16[512,512]{1,0:T(8,128)(2,1)S(1)} %collective-permute-done.refs_1_, ...), custom_call_target="tpu_custom_call" | custom-call | tf_op jit(solution)/shard_map/give/pallas_call | solution.py:155
  75.8 1.5 %collective-permute-start.18 = (s16[144,512]{1,0:T(8,128)(2,1)S(1)}, s16[144,512]{1,0:T(8,128)(2,1)S(1)}, u32[]{:S(2)}, u32[]{:S(2)}) collective-permute-start(s16[144,512]{1,0:T(8,128)(2,1)S(1)} %give.2), channel_id=1, source_target_pairs={{0,16},{16,0},{1,17},{17,1},{2,18},{18,2},{3,19},{19,3},{4,20},{20... | collective-permute-start | bytes 442376 | tf_op jit(solution)/shard_map/ppermute | solution.py:37
  77.3 1.8 %keep.1 = f32[512,512]{1,0:T(8,128)S(1)} custom-call(s32[5]{0:T(128)S(1)} %stack.23.place, s32[16,16]{1,0:T(8,128)S(1)} %copy-done.3, f32[512,512]{1,0:T(8,128)S(1)} %get-tuple-element.31.so_far, bf16[512,512]{1,0:T(8,128)(2,1)S(1)} %copy-done.1, bf16[512,512]{1,0:T(8,128)(2,1)S(1)} %collective-permute-done.refs_1_, ...), custom_call_target="tpu_custom_call" | custom-call | tf_op jit(solution)/shard_map/keep/pallas_call | solution.py:155
  79.1 9.2 %collective-permute-done.18.refs_0_ = s16[144,512]{1,0:T(8,128)(2,1)S(1)} collective-permute-done((s16[144,512]{1,0:T(8,128)(2,1)S(1)}, s16[144,512]{1,0:T(8,128)(2,1)S(1)}, u32[]{:S(2)}, u32[]{:S(2)}) %collective-permute-start.18) | collective-permute-done | bytes 147488 | tf_op jit(solution)/shard_map/ppermute | solution.py:37
  88.3 1.0 %join.1 = bf16[512,512]{1,0:T(8,128)(2,1)} custom-call(f32[512,512]{1,0:T(8,128)S(1)} %keep.1, s16[144,512]{1,0:T(8,128)(2,1)S(1)} %collective-permute-done.18.refs_0_, s16[400,512]{1,0:T(8,128)(2,1)S(1)} %collective-permute-done.19.refs_1_), custom_call_target="tpu_custom_call" | custom-call | tf_op jit(solution)/shard_map/join/pallas_call | solution.py:170
  (13 shorter events, 0.1 us)
Async XLA Ops:
  0.1 1.0 %copy-start.2 = (bf16[512,512]{1,0:T(8,128)(2,1)S(1)}, bf16[512,512]{1,0:T(8,128)(2,1)}, u32[]{:S(2)}) copy-start(bf16[512,512]{1,0:T(8,128)(2,1)} %factor.1) | copy-start | bytes 1572868
  1.1 7.1 %copy-start.1 = (bf16[512,512]{1,0:T(8,128)(2,1)S(1)}, bf16[512,512]{1,0:T(8,128)(2,1)}, u32[]{:S(2)}) copy-start(bf16[512,512]{1,0:T(8,128)(2,1)} %refs_0_.7) | copy-start | bytes 1572868
  1.9 17.3 %collective-permute-start.2 = (bf16[512,512]{1,0:T(8,128)(2,1)S(1)}, bf16[512,512]{1,0:T(8,128)(2,1)S(1)}, u32[]{:S(2)}, u32[]{:S(2)}) collective-permute-start(bf16[512,512]{1,0:T(8,128)(2,1)S(1)} %masked.1), channel_id=1, source_target_pairs={{0,0},{1,16},{8,8},{9,24},{16,1},{17,17},{24,9},{25,25},{2,2},{3,1... | collective-permute-start | bytes 1572872 | tf_op jit(solution)/shard_map/ppermute | solution.py:33
  6.5 15.6 %collective-permute-start.3 = (bf16[512,512]{1,0:T(8,128)(2,1)S(1)}, bf16[512,512]{1,0:T(8,128)(2,1)S(1)}, u32[]{:S(2)}, u32[]{:S(2)}) collective-permute-start(bf16[512,512]{1,0:T(8,128)(2,1)S(1)} %masked.1), channel_id=1, source_target_pairs={{0,8},{1,24},{8,0},{9,16},{16,9},{17,25},{24,1},{25,17},{2,10},{3,... | collective-permute-start | bytes 1572872 | tf_op jit(solution)/shard_map/ppermute | solution.py:33
  8.2 17.1 %collective-permute-start = (bf16[512,512]{1,0:T(8,128)(2,1)S(1)}, bf16[512,512]{1,0:T(8,128)(2,1)S(1)}, u32[]{:S(2)}, u32[]{:S(2)}) collective-permute-start(bf16[512,512]{1,0:T(8,128)(2,1)S(1)} %copy-done.1), channel_id=1, source_target_pairs={{0,32},{32,64},{64,96},{96,128},{128,160},{160,192},{192,224},{224... | collective-permute-start | bytes 1572872 | tf_op jit(solution)/shard_map/ppermute | solution.py:37
  9.9 15.5 %collective-permute-start.1 = (bf16[512,512]{1,0:T(8,128)(2,1)S(1)}, bf16[512,512]{1,0:T(8,128)(2,1)S(1)}, u32[]{:S(2)}, u32[]{:S(2)}) collective-permute-start(bf16[512,512]{1,0:T(8,128)(2,1)S(1)} %copy-done.1), channel_id=1, source_target_pairs={{0,224},{32,0},{64,32},{96,64},{128,96},{160,128},{192,160},{224,1... | collective-permute-start | bytes 1572872 | tf_op jit(solution)/shard_map/ppermute | solution.py:37
  25.4 26.0 %collective-permute-start.8 = (bf16[1024,512]{1,0:T(8,128)(2,1)S(1)}, bf16[1024,512]{1,0:T(8,128)(2,1)S(1)}, u32[]{:S(2)}, u32[]{:S(2)}) collective-permute-start(bf16[1024,512]{1,0:T(8,128)(2,1)S(1)} %pack.2.refs_7_.refs_9_), channel_id=1, source_target_pairs={{0,2},{2,4},{4,6},{6,0},{1,3},{3,5},{5,7},{7,1},{8,10},{10,12},{12... | collective-permute-start | bytes 3145736 | tf_op jit(solution)/shard_map/ppermute | solution.py:37
  26.7 24.8 %collective-permute-start.9 = (bf16[1024,512]{1,0:T(8,128)(2,1)S(1)}, bf16[1024,512]{1,0:T(8,128)(2,1)S(1)}, u32[]{:S(2)}, u32[]{:S(2)}) collective-permute-start(bf16[1024,512]{1,0:T(8,128)(2,1)S(1)} %pack.2.refs_7_.refs_9_), channel_id=1, source_target_pairs={{0,6},{2,0},{4,2},{6,4},{1,7},{3,1},{5,3},{7,5},{8,14},{10,8},{12,... | collective-permute-start | bytes 3145736 | tf_op jit(solution)/shard_map/ppermute | solution.py:37
  28.2 14.3 %collective-permute-start.4 = (bf16[512,512]{1,0:T(8,128)(2,1)S(1)}, bf16[512,512]{1,0:T(8,128)(2,1)S(1)}, u32[]{:S(2)}, u32[]{:S(2)}) collective-permute-start(bf16[512,512]{1,0:T(8,128)(2,1)S(1)} %collective-permute-done.refs_1_), channel_id=1, source_target_pairs={{0,32},{32,64},{64,96},{96,128},{128,160},{160,192},{192,224},{224... | collective-permute-start | bytes 1572872 | tf_op jit(solution)/shard_map/ppermute | solution.py:37
  28.2 14.3 %collective-permute-start.5 = (bf16[512,512]{1,0:T(8,128)(2,1)S(1)}, bf16[512,512]{1,0:T(8,128)(2,1)S(1)}, u32[]{:S(2)}, u32[]{:S(2)}) collective-permute-start(bf16[512,512]{1,0:T(8,128)(2,1)S(1)} %collective-permute-done.1.refs_6_), channel_id=1, source_target_pairs={{0,224},{32,0},{64,32},{96,64},{128,96},{160,128},{192,160},{224,1... | collective-permute-start | bytes 1572872 | tf_op jit(solution)/shard_map/ppermute | solution.py:37
  42.5 13.1 %collective-permute-start.6 = (bf16[512,512]{1,0:T(8,128)(2,1)S(1)}, bf16[512,512]{1,0:T(8,128)(2,1)S(1)}, u32[]{:S(2)}, u32[]{:S(2)}) collective-permute-start(bf16[512,512]{1,0:T(8,128)(2,1)S(1)} %collective-permute-done.4.refs_2_), channel_id=1, source_target_pairs={{0,32},{32,64},{64,96},{96,128},{128,160},{160,192},{192,224},{224... | collective-permute-start | bytes 1572872 | tf_op jit(solution)/shard_map/ppermute | solution.py:37
  44.8 11.3 %collective-permute-start.7 = (bf16[512,512]{1,0:T(8,128)(2,1)S(1)}, bf16[512,512]{1,0:T(8,128)(2,1)S(1)}, u32[]{:S(2)}, u32[]{:S(2)}) collective-permute-start(bf16[512,512]{1,0:T(8,128)(2,1)S(1)} %collective-permute-done.5.refs_5_), channel_id=1, source_target_pairs={{0,224},{32,0},{64,32},{96,64},{128,96},{160,128},{192,160},{224,1... | collective-permute-start | bytes 1572872 | tf_op jit(solution)/shard_map/ppermute | solution.py:37
  51.5 15.8 %collective-permute-start.15 = (bf16[512,512]{1,0:T(8,128)(2,1)S(1)}, bf16[512,512]{1,0:T(8,128)(2,1)S(1)}, u32[]{:S(2)}, u32[]{:S(2)}) collective-permute-start(bf16[512,512]{1,0:T(8,128)(2,1)S(1)} %slice.16), channel_id=1, source_target_pairs={{0,2},{2,4},{4,6},{6,0},{1,3},{3,5},{5,7},{7,1},{8,10},{10,12},{12... | collective-permute-start | bytes 1572872 | tf_op jit(solution)/shard_map/ppermute | solution.py:37
  51.6 15.6 %collective-permute-start.16 = (bf16[512,512]{1,0:T(8,128)(2,1)S(1)}, bf16[512,512]{1,0:T(8,128)(2,1)S(1)}, u32[]{:S(2)}, u32[]{:S(2)}) collective-permute-start(bf16[512,512]{1,0:T(8,128)(2,1)S(1)} %slice.17), channel_id=1, source_target_pairs={{0,6},{2,0},{4,2},{6,4},{1,7},{3,1},{5,3},{7,5},{8,14},{10,8},{12,... | collective-permute-start | bytes 1572872 | tf_op jit(solution)/shard_map/ppermute | solution.py:37
  56.1 6.8 %collective-permute-start.13 = (bf16[256,512]{1,0:T(8,128)(2,1)S(1)}, bf16[256,512]{1,0:T(8,128)(2,1)S(1)}, u32[]{:S(2)}, u32[]{:S(2)}) collective-permute-start(bf16[256,512]{1,0:T(8,128)(2,1)S(1)} %slice.12), channel_id=1, source_target_pairs={{0,32},{32,64},{64,96},{96,128},{128,160},{160,192},{192,224},{224... | collective-permute-start | bytes 786440 | tf_op jit(solution)/shard_map/ppermute | solution.py:37
  57.2 13.5 %copy-start.3 = (s32[16,16]{1,0:T(8,128)S(1)}, s32[16,16]{1,0:T(8,128)}, u32[]{:S(2)}) copy-start(s32[16,16]{1,0:T(8,128)} %occupancy.7) | copy-start | bytes 3076
  57.2 9.7 %collective-permute-start.14 = (bf16[256,512]{1,0:T(8,128)(2,1)S(1)}, bf16[256,512]{1,0:T(8,128)(2,1)S(1)}, u32[]{:S(2)}, u32[]{:S(2)}) collective-permute-start(bf16[256,512]{1,0:T(8,128)(2,1)S(1)} %slice.13), channel_id=1, source_target_pairs={{0,224},{32,0},{64,32},{96,64},{128,96},{160,128},{192,160},{224,1... | collective-permute-start | bytes 786440 | tf_op jit(solution)/shard_map/ppermute | solution.py:37
  59.0 8.7 %collective-permute-start.10 = (bf16[1024,512]{1,0:T(8,128)(2,1)S(1)}, bf16[1024,512]{1,0:T(8,128)(2,1)S(1)}, u32[]{:S(2)}, u32[]{:S(2)}) collective-permute-start(bf16[1024,512]{1,0:T(8,128)(2,1)S(1)} %pack.2.refs_7_.refs_9_), channel_id=1, source_target_pairs={{0,1},{1,0},{2,3},{3,2},{4,5},{5,4},{6,7},{7,6},{8,9},{9,8},{10,11... | collective-permute-start | bytes 3145736 | tf_op jit(solution)/shard_map/ppermute | solution.py:37
  62.9 6.2 %collective-permute-start.11 = (bf16[1024,512]{1,0:T(8,128)(2,1)S(1)}, bf16[1024,512]{1,0:T(8,128)(2,1)S(1)}, u32[]{:S(2)}, u32[]{:S(2)}) collective-permute-start(bf16[1024,512]{1,0:T(8,128)(2,1)S(1)} %collective-permute-done.8.refs_8_.refs_10_), channel_id=1, source_target_pairs={{0,1},{1,0},{2,3},{3,2},{4,5},{5,4},{6,7},{7,6},{8,9},{9,8},{10,11... | collective-permute-start | bytes 3145736 | tf_op jit(solution)/shard_map/ppermute | solution.py:37
  66.9 3.8 %collective-permute-start.12 = (bf16[1024,512]{1,0:T(8,128)(2,1)S(1)}, bf16[1024,512]{1,0:T(8,128)(2,1)S(1)}, u32[]{:S(2)}, u32[]{:S(2)}) collective-permute-start(bf16[1024,512]{1,0:T(8,128)(2,1)S(1)} %collective-permute-done.9.refs_9_.refs_11_), channel_id=1, source_target_pairs={{0,1},{1,0},{2,3},{3,2},{4,5},{5,4},{6,7},{7,6},{8,9},{9,8},{10,11... | collective-permute-start | bytes 3145736 | tf_op jit(solution)/shard_map/ppermute | solution.py:37
  67.3 5.7 %collective-permute-start.17 = (bf16[1024,512]{1,0:T(8,128)(2,1)S(1)}, bf16[1024,512]{1,0:T(8,128)(2,1)S(1)}, u32[]{:S(2)}, u32[]{:S(2)}) collective-permute-start(bf16[1024,512]{1,0:T(8,128)(2,1)S(1)} %pack.3), channel_id=1, source_target_pairs={{0,1},{1,0},{2,3},{3,2},{4,5},{5,4},{6,7},{7,6},{8,9},{9,8},{10,11... | collective-permute-start | bytes 3145736 | tf_op jit(solution)/shard_map/ppermute | solution.py:37
  73.0 1.4 %copy-start = (bf16[1024,512]{1,0:T(8,128)(2,1)}, bf16[1024,512]{1,0:T(8,128)(2,1)S(1)}, u32[]{:S(2)}) copy-start(bf16[1024,512]{1,0:T(8,128)(2,1)S(1)} %collective-permute-done.17.refs_17_) | copy-start | bytes 3145732
  74.4 13.9 %collective-permute-start.19 = (s16[400,512]{1,0:T(8,128)(2,1)S(1)}, s16[400,512]{1,0:T(8,128)(2,1)S(1)}, u32[]{:S(2)}, u32[]{:S(2)}) collective-permute-start(s16[400,512]{1,0:T(8,128)(2,1)S(1)} %give.3), channel_id=1, source_target_pairs={{0,16},{16,0},{1,17},{17,1},{2,18},{18,2},{3,19},{19,3},{4,20},{20... | collective-permute-start | bytes 1228808 | tf_op jit(solution)/shard_map/ppermute | solution.py:37
  75.8 12.5 %collective-permute-start.18 = (s16[144,512]{1,0:T(8,128)(2,1)S(1)}, s16[144,512]{1,0:T(8,128)(2,1)S(1)}, u32[]{:S(2)}, u32[]{:S(2)}) collective-permute-start(s16[144,512]{1,0:T(8,128)(2,1)S(1)} %give.2), channel_id=1, source_target_pairs={{0,16},{16,0},{1,17},{17,1},{2,18},{18,2},{3,19},{19,3},{4,20},{20... | collective-permute-start | bytes 442376 | tf_op jit(solution)/shard_map/ppermute | solution.py:37

commit v6 on v5

--- a/solution.py
+++ b/solution.py
@@ -173,10 +173,10 @@
 def local(draws, factor, occupancy):
     place = jnp.stack([lax.axis_index(n) for n in ("z", "yl", "yh", "x", "c")]).astype(jnp.int32)
     together = lax.optimization_barrier
+    up1, down1 = along_z(draws, 1), along_z(draws, -1)
+    up1, down1 = together((up1, down1))
     tile = masked(place, factor)
-    near, far = to_parity(tile, 0), to_parity(tile, 1)
-    up1, down1 = along_z(draws, 1), along_z(draws, -1)
-    up1, down1, near, far = together((up1, down1, near, far))
+    far, near = to_parity(tile, 1), to_parity(tile, 0)
     pair = pack(near, far)
     up2, down2 = along_z(up1, 1), along_z(down1, -1)
     before, after = along_x(pair, 1), along_x(pair, -1)

time: 89.3 us -> 88 us (0.985)
  starting transfers between devices: 35.9 us -> 33.5 us
  waiting for transfers between devices: 43.3 us -> 44.4 us
    ppermute x18, starting transfers between devices: 29.6 us -> 27.2 us  [shift(): lax.ppermute(piece, name, [(i, (i + by) % count) for i in range(count)])]
    ppermute x18, waiting for transfers between devices: 35 us -> 36.1 us  [shift(): lax.ppermute(piece, name, [(i, (i + by) % count) for i in range(count)])]
  transfers between devices with their start and end apart: 20 -> 20, of which waited for: 11 -> 10; matrix products, arithmetic and copies ran while one was open for 0% -> 0% of each run, Pallas kernels for 6% -> 6%
where the time goes in v6:
time: 88 us; the launch traced here: 87.6 us
  waiting for transfers between devices  44.4 us (50%)
  starting transfers between devices  33.5 us (38%)
  Pallas kernels  8.29 us (9%)
  local copies, waits for them, and re-layouts  1.25 us (1%)
    ppermute x18, waiting for transfers between devices, shift(): lax.ppermute(piece, name, [(i, (i + by) % count) for i in range(count)])  36.1 us
    ppermute x18, starting transfers between devices, shift(): lax.ppermute(piece, name, [(i, (i + by) % count) for i in range(count)])  27.2 us
    ppermute x2, waiting for transfers between devices, to_parity(): return lax.ppermute(tile, COLUMN, pairs)  8.28 us
    ppermute x2, starting transfers between devices, to_parity(): return lax.ppermute(tile, COLUMN, pairs)  6.3 us
    pallas_call x3, Pallas kernels, late(): return call(kernel, out, scratch, specs, 'give' if given else 'keep')(*args)  4.43 us
    pallas_call x1, Pallas kernels, early(): call(kernel, (out, out), scratch, specs, 'early', (VMEM, VMEM))(*args)  1.93 us
  transfers between devices with their start and end apart: 20, of which 10 were waited for; matrix products, arithmetic and copies ran while one was open for 0% of the time, Pallas kernels for 6%

profile of v6, /device:TPU:1, one launch (start us, length us, event | category | flops | bytes accessed | tf_op | source)
XLA Modules:
  0.0 87.6 jit_solution(6454232813610058531)
XLA Ops:
  0.0 0.1 stack.23.place
  0.1 1.0 %copy-done.2 = bf16[512,512]{1,0:T(8,128)(2,1)S(1)} copy-done((bf16[512,512]{1,0:T(8,128)(2,1)S(1)}, bf16[512,512]{1,0:T(8,128)(2,1)}, u32[]{:S(2)}) %copy-start.2) | copy-done | bytes 524312
  1.1 0.8 masked.1
  1.9 4.6 %collective-permute-start.6 = (bf16[512,512]{1,0:T(8,128)(2,1)S(1)}, bf16[512,512]{1,0:T(8,128)(2,1)S(1)}, u32[]{:S(2)}, u32[]{:S(2)}) collective-permute-start(bf16[512,512]{1,0:T(8,128)(2,1)S(1)} %masked.1), channel_id=1, source_target_pairs={{0,0},{1,16},{8,8},{9,24},{16,1},{17,17},{24,9},{25,25},{2,2},{3,1... | collective-permute-start | bytes 1572872 | tf_op jit(solution)/shard_map/ppermute | solution.py:33
  6.5 1.7 %collective-permute-start.7 = (bf16[512,512]{1,0:T(8,128)(2,1)S(1)}, bf16[512,512]{1,0:T(8,128)(2,1)S(1)}, u32[]{:S(2)}, u32[]{:S(2)}) collective-permute-start(bf16[512,512]{1,0:T(8,128)(2,1)S(1)} %masked.1), channel_id=1, source_target_pairs={{0,8},{1,24},{8,0},{9,16},{16,9},{17,25},{24,1},{25,17},{2,10},{3,... | collective-permute-start | bytes 1572872 | tf_op jit(solution)/shard_map/ppermute | solution.py:33
  8.2 1.6 %collective-permute-start = (bf16[512,512]{1,0:T(8,128)(2,1)S(1)}, bf16[512,512]{1,0:T(8,128)(2,1)S(1)}, u32[]{:S(2)}, u32[]{:S(2)}) collective-permute-start(bf16[512,512]{1,0:T(8,128)(2,1)S(1)} %copy-done.1), channel_id=1, source_target_pairs={{0,32},{32,64},{64,96},{96,128},{128,160},{160,192},{192,224},{224... | collective-permute-start | bytes 1572872 | tf_op jit(solution)/shard_map/ppermute | solution.py:37
  9.9 3.9 %collective-permute-start.1 = (bf16[512,512]{1,0:T(8,128)(2,1)S(1)}, bf16[512,512]{1,0:T(8,128)(2,1)S(1)}, u32[]{:S(2)}, u32[]{:S(2)}) collective-permute-start(bf16[512,512]{1,0:T(8,128)(2,1)S(1)} %copy-done.1), channel_id=1, source_target_pairs={{0,224},{32,0},{64,32},{96,64},{128,96},{160,128},{192,160},{224,1... | collective-permute-start | bytes 1572872 | tf_op jit(solution)/shard_map/ppermute | solution.py:37
  13.8 5.4 %collective-permute-done.6.refs_0_ = bf16[512,512]{1,0:T(8,128)(2,1)S(1)} collective-permute-done((bf16[512,512]{1,0:T(8,128)(2,1)S(1)}, bf16[512,512]{1,0:T(8,128)(2,1)S(1)}, u32[]{:S(2)}, u32[]{:S(2)}) %collective-permute-start.6) | collective-permute-done | bytes 524320 | tf_op jit(solution)/shard_map/ppermute | solution.py:33
  19.3 2.9 %collective-permute-done.7.refs_1_ = bf16[512,512]{1,0:T(8,128)(2,1)S(1)} collective-permute-done((bf16[512,512]{1,0:T(8,128)(2,1)S(1)}, bf16[512,512]{1,0:T(8,128)(2,1)S(1)}, u32[]{:S(2)}, u32[]{:S(2)}) %collective-permute-start.7) | collective-permute-done | bytes 524320 | tf_op jit(solution)/shard_map/ppermute | solution.py:33
  22.1 0.1 pack.2.refs_7_.refs_9_
  22.2 0.1 collective-permute-start.8
  22.3 2.7 %collective-permute-start.9 = (bf16[1024,512]{1,0:T(8,128)(2,1)S(1)}, bf16[1024,512]{1,0:T(8,128)(2,1)S(1)}, u32[]{:S(2)}, u32[]{:S(2)}) collective-permute-start(bf16[1024,512]{1,0:T(8,128)(2,1)S(1)} %pack.2.refs_7_.refs_9_), channel_id=1, source_target_pairs={{0,6},{2,0},{4,2},{6,4},{1,7},{3,1},{5,3},{7,5},{8,14},{10,8},{12,... | collective-permute-start | bytes 3145736 | tf_op jit(solution)/shard_map/ppermute | solution.py:37
  24.9 0.4 collective-permute-done.refs_1_
  25.4 0.0 collective-permute-done.1.refs_6_
  25.4 0.0 collective-permute-start.2
  25.4 3.6 %collective-permute-start.3 = (bf16[512,512]{1,0:T(8,128)(2,1)S(1)}, bf16[512,512]{1,0:T(8,128)(2,1)S(1)}, u32[]{:S(2)}, u32[]{:S(2)}) collective-permute-start(bf16[512,512]{1,0:T(8,128)(2,1)S(1)} %collective-permute-done.1.refs_6_), channel_id=1, source_target_pairs={{0,224},{32,0},{64,32},{96,64},{128,96},{160,128},{192,160},{224,1... | collective-permute-start | bytes 1572872 | tf_op jit(solution)/shard_map/ppermute | solution.py:37
  29.0 12.4 %collective-permute-done.2.refs_2_ = bf16[512,512]{1,0:T(8,128)(2,1)S(1)} collective-permute-done((bf16[512,512]{1,0:T(8,128)(2,1)S(1)}, bf16[512,512]{1,0:T(8,128)(2,1)S(1)}, u32[]{:S(2)}, u32[]{:S(2)}) %collective-permute-start.2) | collective-permute-done | bytes 524320 | tf_op jit(solution)/shard_map/ppermute | solution.py:37
  41.3 0.0 collective-permute-done.3.refs_5_
  41.3 1.5 %collective-permute-start.4 = (bf16[512,512]{1,0:T(8,128)(2,1)S(1)}, bf16[512,512]{1,0:T(8,128)(2,1)S(1)}, u32[]{:S(2)}, u32[]{:S(2)}) collective-permute-start(bf16[512,512]{1,0:T(8,128)(2,1)S(1)} %collective-permute-done.2.refs_2_), channel_id=1, source_target_pairs={{0,32},{32,64},{64,96},{96,128},{128,160},{160,192},{192,224},{224... | collective-permute-start | bytes 1572872 | tf_op jit(solution)/shard_map/ppermute | solution.py:37
  42.8 1.2 %collective-permute-start.5 = (bf16[512,512]{1,0:T(8,128)(2,1)S(1)}, bf16[512,512]{1,0:T(8,128)(2,1)S(1)}, u32[]{:S(2)}, u32[]{:S(2)}) collective-permute-start(bf16[512,512]{1,0:T(8,128)(2,1)S(1)} %collective-permute-done.3.refs_5_), channel_id=1, source_target_pairs={{0,224},{32,0},{64,32},{96,64},{128,96},{160,128},{192,160},{224,1... | collective-permute-start | bytes 1572872 | tf_op jit(solution)/shard_map/ppermute | solution.py:37
  44.0 4.3 %collective-permute-done.8.refs_8_.refs_10_ = bf16[1024,512]{1,0:T(8,128)(2,1)S(1)} collective-permute-done((bf16[1024,512]{1,0:T(8,128)(2,1)S(1)}, bf16[1024,512]{1,0:T(8,128)(2,1)S(1)}, u32[]{:S(2)}, u32[]{:S(2)}) %collective-permute-start.8) | collective-permute-done | bytes 1048608 | tf_op jit(solution)/shard_map/ppermute | solution.py:37
  48.3 0.1 collective-permute-start.15
  48.4 0.0 collective-permute-done.9.refs_9_.refs_11_
  48.4 2.7 %collective-permute-start.16 = (bf16[512,512]{1,0:T(8,128)(2,1)S(1)}, bf16[512,512]{1,0:T(8,128)(2,1)S(1)}, u32[]{:S(2)}, u32[]{:S(2)}) collective-permute-start(bf16[512,512]{1,0:T(8,128)(2,1)S(1)} %slice.17), channel_id=1, source_target_pairs={{0,6},{2,0},{4,2},{6,4},{1,7},{3,1},{5,3},{7,5},{8,14},{10,8},{12,... | collective-permute-start | bytes 1572872 | tf_op jit(solution)/shard_map/ppermute | solution.py:37
  51.2 4.4 %collective-permute-done.4.refs_3_ = bf16[512,512]{1,0:T(8,128)(2,1)S(1)} collective-permute-done((bf16[512,512]{1,0:T(8,128)(2,1)S(1)}, bf16[512,512]{1,0:T(8,128)(2,1)S(1)}, u32[]{:S(2)}, u32[]{:S(2)}) %collective-permute-start.4) | collective-permute-done | bytes 524320 | tf_op jit(solution)/shard_map/ppermute | solution.py:37
  55.6 0.0 collective-permute-done.5.refs_4_
  55.6 0.3 collective-permute-start.13
  55.9 0.0 copy-start.3
  55.9 2.6 %collective-permute-start.14 = (bf16[256,512]{1,0:T(8,128)(2,1)S(1)}, bf16[256,512]{1,0:T(8,128)(2,1)S(1)}, u32[]{:S(2)}, u32[]{:S(2)}) collective-permute-start(bf16[256,512]{1,0:T(8,128)(2,1)S(1)} %slice.13), channel_id=1, source_target_pairs={{0,224},{32,0},{64,32},{96,64},{128,96},{160,128},{192,160},{224,1... | collective-permute-start | bytes 786440 | tf_op jit(solution)/shard_map/ppermute | solution.py:37
  58.5 2.1 %collective-permute-start.10 = (bf16[1024,512]{1,0:T(8,128)(2,1)S(1)}, bf16[1024,512]{1,0:T(8,128)(2,1)S(1)}, u32[]{:S(2)}, u32[]{:S(2)}) collective-permute-start(bf16[1024,512]{1,0:T(8,128)(2,1)S(1)} %pack.2.refs_7_.refs_9_), channel_id=1, source_target_pairs={{0,1},{1,0},{2,3},{3,2},{4,5},{5,4},{6,7},{7,6},{8,9},{9,8},{10,11... | collective-permute-start | bytes 3145736 | tf_op jit(solution)/shard_map/ppermute | solution.py:37
  60.6 2.5 %collective-permute-done.13.refs_7_ = bf16[256,512]{1,0:T(8,128)(2,1)S(1)} collective-permute-done((bf16[256,512]{1,0:T(8,128)(2,1)S(1)}, bf16[256,512]{1,0:T(8,128)(2,1)S(1)}, u32[]{:S(2)}, u32[]{:S(2)}) %collective-permute-start.13) | collective-permute-done | bytes 262176 | tf_op jit(solution)/shard_map/ppermute | solution.py:37
  63.1 2.5 %collective-permute-start.11 = (bf16[1024,512]{1,0:T(8,128)(2,1)S(1)}, bf16[1024,512]{1,0:T(8,128)(2,1)S(1)}, u32[]{:S(2)}, u32[]{:S(2)}) collective-permute-start(bf16[1024,512]{1,0:T(8,128)(2,1)S(1)} %collective-permute-done.8.refs_8_.refs_10_), channel_id=1, source_target_pairs={{0,1},{1,0},{2,3},{3,2},{4,5},{5,4},{6,7},{7,6},{8,9},{9,8},{10,11... | collective-permute-start | bytes 3145736 | tf_op jit(solution)/shard_map/ppermute | solution.py:37
  65.6 0.0 collective-permute-done.14.refs_8_
  65.6 0.0 collective-permute-start.12
  65.6 0.0 collective-permute-done.15.refs_0_.refs_12_
  65.7 0.1 pack.3
  65.7 0.8 collective-permute-start.17
  66.5 1.4 %collective-permute-done.11.refs_11_.refs_15_ = bf16[1024,512]{1,0:T(8,128)(2,1)S(1)} collective-permute-done((bf16[1024,512]{1,0:T(8,128)(2,1)S(1)}, bf16[1024,512]{1,0:T(8,128)(2,1)S(1)}, u32[]{:S(2)}, u32[]{:S(2)}) %collective-permute-start.11) | collective-permute-done | bytes 1048608 | tf_op jit(solution)/shard_map/ppermute | solution.py:37
  67.9 1.5 %collective-permute-done.12.refs_12_.refs_16_ = bf16[1024,512]{1,0:T(8,128)(2,1)S(1)} collective-permute-done((bf16[1024,512]{1,0:T(8,128)(2,1)S(1)}, bf16[1024,512]{1,0:T(8,128)(2,1)S(1)}, u32[]{:S(2)}, u32[]{:S(2)}) %collective-permute-start.12) | collective-permute-done | bytes 1048608 | tf_op jit(solution)/shard_map/ppermute | solution.py:37
  69.4 1.9 %early.1 = (f32[512,512]{1,0:T(8,128)S(1)}, f32[512,512]{1,0:T(8,128)S(1)}) custom-call(s32[5]{0:T(128)S(1)} %stack.23.place, s32[16,16]{1,0:T(8,128)S(1)} %copy-done.3, bf16[512,512]{1,0:T(8,128)(2,1)S(1)} %copy-done.1, bf16[512,512]{1,0:T(8,128)(2,1)S(1)} %collective-permute-done.refs_1_, bf16[512,512]{1,0:T(8,128)(2,1)S(1)} %collective-permute-done.2.refs_2_, ...), custom_call_target="tpu_custom_call" | custom-call | tf_op jit(solution)/shard_map/early/pallas_call | solution.py:131
  71.4 0.0 collective-permute-done.17.refs_17_
  71.4 1.3 %give.3 = s16[400,512]{1,0:T(8,128)(2,1)S(1)} custom-call(s32[5]{0:T(128)S(1)} %stack.23.place, s32[16,16]{1,0:T(8,128)S(1)} %copy-done.3, f32[512,512]{1,0:T(8,128)S(1)} %get-tuple-element.32.so_far, bf16[512,512]{1,0:T(8,128)(2,1)S(1)} %copy-done.1, bf16[512,512]{1,0:T(8,128)(2,1)S(1)} %collective-permute-done.refs_1_, ...), custom_call_target="tpu_custom_call" | custom-call | tf_op jit(solution)/shard_map/give/pallas_call | solution.py:155
  72.7 0.1 collective-permute-start.19
  72.8 1.3 %give.2 = s16[144,512]{1,0:T(8,128)(2,1)S(1)} custom-call(s32[5]{0:T(128)S(1)} %stack.23.place, s32[16,16]{1,0:T(8,128)S(1)} %copy-done.3, f32[512,512]{1,0:T(8,128)S(1)} %get-tuple-element.32.so_far, bf16[512,512]{1,0:T(8,128)(2,1)S(1)} %copy-done.1, bf16[512,512]{1,0:T(8,128)(2,1)S(1)} %collective-permute-done.refs_1_, ...), custom_call_target="tpu_custom_call" | custom-call | tf_op jit(solution)/shard_map/give/pallas_call | solution.py:155
  74.1 1.5 %collective-permute-start.18 = (s16[144,512]{1,0:T(8,128)(2,1)S(1)}, s16[144,512]{1,0:T(8,128)(2,1)S(1)}, u32[]{:S(2)}, u32[]{:S(2)}) collective-permute-start(s16[144,512]{1,0:T(8,128)(2,1)S(1)} %give.2), channel_id=1, source_target_pairs={{0,16},{16,0},{1,17},{17,1},{2,18},{18,2},{3,19},{19,3},{4,20},{20... | collective-permute-start | bytes 442376 | tf_op jit(solution)/shard_map/ppermute | solution.py:37
  75.7 1.8 %keep.1 = f32[512,512]{1,0:T(8,128)S(1)} custom-call(s32[5]{0:T(128)S(1)} %stack.23.place, s32[16,16]{1,0:T(8,128)S(1)} %copy-done.3, f32[512,512]{1,0:T(8,128)S(1)} %get-tuple-element.27.so_far, bf16[512,512]{1,0:T(8,128)(2,1)S(1)} %copy-done.1, bf16[512,512]{1,0:T(8,128)(2,1)S(1)} %collective-permute-done.refs_1_, ...), custom_call_target="tpu_custom_call" | custom-call | tf_op jit(solution)/shard_map/keep/pallas_call | solution.py:155
  77.4 9.2 %collective-permute-done.18.refs_0_ = s16[144,512]{1,0:T(8,128)(2,1)S(1)} collective-permute-done((s16[144,512]{1,0:T(8,128)(2,1)S(1)}, s16[144,512]{1,0:T(8,128)(2,1)S(1)}, u32[]{:S(2)}, u32[]{:S(2)}) %collective-permute-start.18) | collective-permute-done | bytes 147488 | tf_op jit(solution)/shard_map/ppermute | solution.py:37
  86.6 1.0 %join.1 = bf16[512,512]{1,0:T(8,128)(2,1)} custom-call(f32[512,512]{1,0:T(8,128)S(1)} %keep.1, s16[144,512]{1,0:T(8,128)(2,1)S(1)} %collective-permute-done.18.refs_0_, s16[400,512]{1,0:T(8,128)(2,1)S(1)} %collective-permute-done.19.refs_1_), custom_call_target="tpu_custom_call" | custom-call | tf_op jit(solution)/shard_map/join/pallas_call | solution.py:170
  (13 shorter events, 0.1 us)
Async XLA Ops:
  0.1 1.0 %copy-start.2 = (bf16[512,512]{1,0:T(8,128)(2,1)S(1)}, bf16[512,512]{1,0:T(8,128)(2,1)}, u32[]{:S(2)}) copy-start(bf16[512,512]{1,0:T(8,128)(2,1)} %factor.1) | copy-start | bytes 1572868
  1.1 7.1 %copy-start.1 = (bf16[512,512]{1,0:T(8,128)(2,1)S(1)}, bf16[512,512]{1,0:T(8,128)(2,1)}, u32[]{:S(2)}) copy-start(bf16[512,512]{1,0:T(8,128)(2,1)} %refs_0_.7) | copy-start | bytes 1572868
  1.9 17.3 %collective-permute-start.6 = (bf16[512,512]{1,0:T(8,128)(2,1)S(1)}, bf16[512,512]{1,0:T(8,128)(2,1)S(1)}, u32[]{:S(2)}, u32[]{:S(2)}) collective-permute-start(bf16[512,512]{1,0:T(8,128)(2,1)S(1)} %masked.1), channel_id=1, source_target_pairs={{0,0},{1,16},{8,8},{9,24},{16,1},{17,17},{24,9},{25,25},{2,2},{3,1... | collective-permute-start | bytes 1572872 | tf_op jit(solution)/shard_map/ppermute | solution.py:33
  6.5 15.6 %collective-permute-start.7 = (bf16[512,512]{1,0:T(8,128)(2,1)S(1)}, bf16[512,512]{1,0:T(8,128)(2,1)S(1)}, u32[]{:S(2)}, u32[]{:S(2)}) collective-permute-start(bf16[512,512]{1,0:T(8,128)(2,1)S(1)} %masked.1), channel_id=1, source_target_pairs={{0,8},{1,24},{8,0},{9,16},{16,9},{17,25},{24,1},{25,17},{2,10},{3,... | collective-permute-start | bytes 1572872 | tf_op jit(solution)/shard_map/ppermute | solution.py:33
  8.2 17.1 %collective-permute-start = (bf16[512,512]{1,0:T(8,128)(2,1)S(1)}, bf16[512,512]{1,0:T(8,128)(2,1)S(1)}, u32[]{:S(2)}, u32[]{:S(2)}) collective-permute-start(bf16[512,512]{1,0:T(8,128)(2,1)S(1)} %copy-done.1), channel_id=1, source_target_pairs={{0,32},{32,64},{64,96},{96,128},{128,160},{160,192},{192,224},{224... | collective-permute-start | bytes 1572872 | tf_op jit(solution)/shard_map/ppermute | solution.py:37
  9.9 15.5 %collective-permute-start.1 = (bf16[512,512]{1,0:T(8,128)(2,1)S(1)}, bf16[512,512]{1,0:T(8,128)(2,1)S(1)}, u32[]{:S(2)}, u32[]{:S(2)}) collective-permute-start(bf16[512,512]{1,0:T(8,128)(2,1)S(1)} %copy-done.1), channel_id=1, source_target_pairs={{0,224},{32,0},{64,32},{96,64},{128,96},{160,128},{192,160},{224,1... | collective-permute-start | bytes 1572872 | tf_op jit(solution)/shard_map/ppermute | solution.py:37
  22.2 26.1 %collective-permute-start.8 = (bf16[1024,512]{1,0:T(8,128)(2,1)S(1)}, bf16[1024,512]{1,0:T(8,128)(2,1)S(1)}, u32[]{:S(2)}, u32[]{:S(2)}) collective-permute-start(bf16[1024,512]{1,0:T(8,128)(2,1)S(1)} %pack.2.refs_7_.refs_9_), channel_id=1, source_target_pairs={{0,2},{2,4},{4,6},{6,0},{1,3},{3,5},{5,7},{7,1},{8,10},{10,12},{12... | collective-permute-start | bytes 3145736 | tf_op jit(solution)/shard_map/ppermute | solution.py:37
  22.3 26.1 %collective-permute-start.9 = (bf16[1024,512]{1,0:T(8,128)(2,1)S(1)}, bf16[1024,512]{1,0:T(8,128)(2,1)S(1)}, u32[]{:S(2)}, u32[]{:S(2)}) collective-permute-start(bf16[1024,512]{1,0:T(8,128)(2,1)S(1)} %pack.2.refs_7_.refs_9_), channel_id=1, source_target_pairs={{0,6},{2,0},{4,2},{6,4},{1,7},{3,1},{5,3},{7,5},{8,14},{10,8},{12,... | collective-permute-start | bytes 3145736 | tf_op jit(solution)/shard_map/ppermute | solution.py:37
  25.4 15.9 %collective-permute-start.2 = (bf16[512,512]{1,0:T(8,128)(2,1)S(1)}, bf16[512,512]{1,0:T(8,128)(2,1)S(1)}, u32[]{:S(2)}, u32[]{:S(2)}) collective-permute-start(bf16[512,512]{1,0:T(8,128)(2,1)S(1)} %collective-permute-done.refs_1_), channel_id=1, source_target_pairs={{0,32},{32,64},{64,96},{96,128},{128,160},{160,192},{192,224},{224... | collective-permute-start | bytes 1572872 | tf_op jit(solution)/shard_map/ppermute | solution.py:37
  25.4 15.9 %collective-permute-start.3 = (bf16[512,512]{1,0:T(8,128)(2,1)S(1)}, bf16[512,512]{1,0:T(8,128)(2,1)S(1)}, u32[]{:S(2)}, u32[]{:S(2)}) collective-permute-start(bf16[512,512]{1,0:T(8,128)(2,1)S(1)} %collective-permute-done.1.refs_6_), channel_id=1, source_target_pairs={{0,224},{32,0},{64,32},{96,64},{128,96},{160,128},{192,160},{224,1... | collective-permute-start | bytes 1572872 | tf_op jit(solution)/shard_map/ppermute | solution.py:37
  41.3 14.3 %collective-permute-start.4 = (bf16[512,512]{1,0:T(8,128)(2,1)S(1)}, bf16[512,512]{1,0:T(8,128)(2,1)S(1)}, u32[]{:S(2)}, u32[]{:S(2)}) collective-permute-start(bf16[512,512]{1,0:T(8,128)(2,1)S(1)} %collective-permute-done.2.refs_2_), channel_id=1, source_target_pairs={{0,32},{32,64},{64,96},{96,128},{128,160},{160,192},{192,224},{224... | collective-permute-start | bytes 1572872 | tf_op jit(solution)/shard_map/ppermute | solution.py:37
  42.8 12.8 %collective-permute-start.5 = (bf16[512,512]{1,0:T(8,128)(2,1)S(1)}, bf16[512,512]{1,0:T(8,128)(2,1)S(1)}, u32[]{:S(2)}, u32[]{:S(2)}) collective-permute-start(bf16[512,512]{1,0:T(8,128)(2,1)S(1)} %collective-permute-done.3.refs_5_), channel_id=1, source_target_pairs={{0,224},{32,0},{64,32},{96,64},{128,96},{160,128},{192,160},{224,1... | collective-permute-start | bytes 1572872 | tf_op jit(solution)/shard_map/ppermute | solution.py:37
  48.3 17.3 %collective-permute-start.15 = (bf16[512,512]{1,0:T(8,128)(2,1)S(1)}, bf16[512,512]{1,0:T(8,128)(2,1)S(1)}, u32[]{:S(2)}, u32[]{:S(2)}) collective-permute-start(bf16[512,512]{1,0:T(8,128)(2,1)S(1)} %slice.16), channel_id=1, source_target_pairs={{0,2},{2,4},{4,6},{6,0},{1,3},{3,5},{5,7},{7,1},{8,10},{10,12},{12... | collective-permute-start | bytes 1572872 | tf_op jit(solution)/shard_map/ppermute | solution.py:37
  48.4 17.2 %collective-permute-start.16 = (bf16[512,512]{1,0:T(8,128)(2,1)S(1)}, bf16[512,512]{1,0:T(8,128)(2,1)S(1)}, u32[]{:S(2)}, u32[]{:S(2)}) collective-permute-start(bf16[512,512]{1,0:T(8,128)(2,1)S(1)} %slice.17), channel_id=1, source_target_pairs={{0,6},{2,0},{4,2},{6,4},{1,7},{3,1},{5,3},{7,5},{8,14},{10,8},{12,... | collective-permute-start | bytes 1572872 | tf_op jit(solution)/shard_map/ppermute | solution.py:37
  55.6 7.5 %collective-permute-start.13 = (bf16[256,512]{1,0:T(8,128)(2,1)S(1)}, bf16[256,512]{1,0:T(8,128)(2,1)S(1)}, u32[]{:S(2)}, u32[]{:S(2)}) collective-permute-start(bf16[256,512]{1,0:T(8,128)(2,1)S(1)} %slice.12), channel_id=1, source_target_pairs={{0,32},{32,64},{64,96},{96,128},{128,160},{160,192},{192,224},{224... | collective-permute-start | bytes 786440 | tf_op jit(solution)/shard_map/ppermute | solution.py:37
  55.9 13.5 %copy-start.3 = (s32[16,16]{1,0:T(8,128)S(1)}, s32[16,16]{1,0:T(8,128)}, u32[]{:S(2)}) copy-start(s32[16,16]{1,0:T(8,128)} %occupancy.7) | copy-start | bytes 3076
  55.9 9.7 %collective-permute-start.14 = (bf16[256,512]{1,0:T(8,128)(2,1)S(1)}, bf16[256,512]{1,0:T(8,128)(2,1)S(1)}, u32[]{:S(2)}, u32[]{:S(2)}) collective-permute-start(bf16[256,512]{1,0:T(8,128)(2,1)S(1)} %slice.13), channel_id=1, source_target_pairs={{0,224},{32,0},{64,32},{96,64},{128,96},{160,128},{192,160},{224,1... | collective-permute-start | bytes 786440 | tf_op jit(solution)/shard_map/ppermute | solution.py:37
  58.5 8.0 %collective-permute-start.10 = (bf16[1024,512]{1,0:T(8,128)(2,1)S(1)}, bf16[1024,512]{1,0:T(8,128)(2,1)S(1)}, u32[]{:S(2)}, u32[]{:S(2)}) collective-permute-start(bf16[1024,512]{1,0:T(8,128)(2,1)S(1)} %pack.2.refs_7_.refs_9_), channel_id=1, source_target_pairs={{0,1},{1,0},{2,3},{3,2},{4,5},{5,4},{6,7},{7,6},{8,9},{9,8},{10,11... | collective-permute-start | bytes 3145736 | tf_op jit(solution)/shard_map/ppermute | solution.py:37
  63.1 4.8 %collective-permute-start.11 = (bf16[1024,512]{1,0:T(8,128)(2,1)S(1)}, bf16[1024,512]{1,0:T(8,128)(2,1)S(1)}, u32[]{:S(2)}, u32[]{:S(2)}) collective-permute-start(bf16[1024,512]{1,0:T(8,128)(2,1)S(1)} %collective-permute-done.8.refs_8_.refs_10_), channel_id=1, source_target_pairs={{0,1},{1,0},{2,3},{3,2},{4,5},{5,4},{6,7},{7,6},{8,9},{9,8},{10,11... | collective-permute-start | bytes 3145736 | tf_op jit(solution)/shard_map/ppermute | solution.py:37
  65.6 3.8 %collective-permute-start.12 = (bf16[1024,512]{1,0:T(8,128)(2,1)S(1)}, bf16[1024,512]{1,0:T(8,128)(2,1)S(1)}, u32[]{:S(2)}, u32[]{:S(2)}) collective-permute-start(bf16[1024,512]{1,0:T(8,128)(2,1)S(1)} %collective-permute-done.9.refs_9_.refs_11_), channel_id=1, source_target_pairs={{0,1},{1,0},{2,3},{3,2},{4,5},{5,4},{6,7},{7,6},{8,9},{9,8},{10,11... | collective-permute-start | bytes 3145736 | tf_op jit(solution)/shard_map/ppermute | solution.py:37
  65.7 5.6 %collective-permute-start.17 = (bf16[1024,512]{1,0:T(8,128)(2,1)S(1)}, bf16[1024,512]{1,0:T(8,128)(2,1)S(1)}, u32[]{:S(2)}, u32[]{:S(2)}) collective-permute-start(bf16[1024,512]{1,0:T(8,128)(2,1)S(1)} %pack.3), channel_id=1, source_target_pairs={{0,1},{1,0},{2,3},{3,2},{4,5},{5,4},{6,7},{7,6},{8,9},{9,8},{10,11... | collective-permute-start | bytes 3145736 | tf_op jit(solution)/shard_map/ppermute | solution.py:37
  71.4 1.4 %copy-start = (bf16[1024,512]{1,0:T(8,128)(2,1)}, bf16[1024,512]{1,0:T(8,128)(2,1)S(1)}, u32[]{:S(2)}) copy-start(bf16[1024,512]{1,0:T(8,128)(2,1)S(1)} %collective-permute-done.17.refs_17_) | copy-start | bytes 3145732
  72.7 13.9 %collective-permute-start.19 = (s16[400,512]{1,0:T(8,128)(2,1)S(1)}, s16[400,512]{1,0:T(8,128)(2,1)S(1)}, u32[]{:S(2)}, u32[]{:S(2)}) collective-permute-start(s16[400,512]{1,0:T(8,128)(2,1)S(1)} %give.3), channel_id=1, source_target_pairs={{0,16},{16,0},{1,17},{17,1},{2,18},{18,2},{3,19},{19,3},{4,20},{20... | collective-permute-start | bytes 1228808 | tf_op jit(solution)/shard_map/ppermute | solution.py:37
  74.1 12.5 %collective-permute-start.18 = (s16[144,512]{1,0:T(8,128)(2,1)S(1)}, s16[144,512]{1,0:T(8,128)(2,1)S(1)}, u32[]{:S(2)}, u32[]{:S(2)}) collective-permute-start(s16[144,512]{1,0:T(8,128)(2,1)S(1)} %give.2), channel_id=1, source_target_pairs={{0,16},{16,0},{1,17},{17,1},{2,18},{18,2},{3,19},{19,3},{4,20},{20... | collective-permute-start | bytes 442376 | tf_op jit(solution)/shard_map/ppermute | solution.py:37

commit v7 on v6

--- a/solution.py
+++ b/solution.py
@@ -107,7 +107,7 @@
         held = (occupancy[2 * z + row, column] == 1) & (column <= 2 * z + row)
         if ready:
             held &= slot != 4
-        elif n < 6:
+        elif ready is False and n < 6:
             held &= slot == 4
         for where, ref in ((row == c, own[n]), (row != c, other[n])):
 
@@ -117,10 +117,9 @@
 
 
 def early_kernel(packs, place, occupancy, *refs):
-    draws, packed, (give, keep, slots) = refs[:7], refs[7:-3], refs[-3:]
-    for row, total in ((1 - place[1], give), (place[1], keep)):
-        total[...] = jnp.zeros_like(total)
-        add_up(row, True, 0, TILE, packs, place, occupancy, draws, (), packed, total, slots)
+    draws, packed, (give, slots) = refs[:7], refs[7:-2], refs[-2:]
+    give[...] = jnp.zeros_like(give)
+    add_up(1 - place[1], True, 0, TILE, packs, place, occupancy, draws, (), packed, give, slots)
 
 
 def early(packs, *args):
@@ -128,14 +127,16 @@
     specs = [SMEM] * 2 + [VMEM] * (len(args) - 2)
     scratch = [pltpu.VMEM((8, TILE, TILE), jnp.bfloat16)]
     kernel = functools.partial(early_kernel, packs)
-    return call(kernel, (out, out), scratch, specs, "early", (VMEM, VMEM))(*args)
-
-
-def late_kernel(given, begin, size, packs, place, occupancy, so_far, *refs):
+    return call(kernel, out, scratch, specs, "early")(*args)
+
+
+def late_kernel(given, begin, size, packs, place, occupancy, *refs):
+    if given:
+        so_far, refs = refs[0], refs[1:]
     draws, halves, packed, (out, total, slots) = refs[:7], refs[7:9], refs[9:-3], refs[-3:]
-    total[...] = so_far[begin : begin + size, :]
+    total[...] = so_far[begin : begin + size, :] if given else jnp.zeros_like(total)
     row = 1 - place[1] if given else place[1]
-    add_up(row, False, begin, size, packs, place, occupancy, draws, halves, packed, total, slots)
+    add_up(row, False if given else None, begin, size, packs, place, occupancy, draws, halves, packed, total, slots)
     if not given:
         out[...] = total[...]
         return
@@ -190,14 +191,14 @@
     last_c = other_core(pack(near_o, far_o))
     circled = (draws, up1, up2, up3, down3, down2, down1)
     ready = ((0, 1), (2, 3), (4, 5))
-    give, keep = early((ready, ready), place, occupancy, *circled, pair, before, after, pair_c, before_c, after_c)
+    give = early((ready, ready), place, occupancy, *circled, pair, before, after, pair_c, before_c, after_c)
     packs = ready + ((6,), (7,)), ready + ((6, 7),)
     args = (*circled, up4, down4, pair, before, after, near_o, far_o, pair_c, before_c, after_c, last_c)
     crossed = []
     for begin, size in PARTS:
         coded = jax.ShapeDtypeStruct((size + EXTRA, TILE), jnp.int16)
         crossed.append(other_chip(late(True, begin, size, packs, coded, place, occupancy, give, *args)))
-    keep = late(False, 0, TILE, packs, jax.ShapeDtypeStruct((TILE, TILE), jnp.float32), place, occupancy, keep, *args)
+    keep = late(False, 0, TILE, packs, jax.ShapeDtypeStruct((TILE, TILE), jnp.float32), place, occupancy, *args)
     return join(keep, crossed)
 
 

time: 88 us -> 89.5 us (1.017)
  starting transfers between devices: 33.5 us -> 37.1 us
  Pallas kernels: 8.29 us -> 7.28 us
    ppermute x18, starting transfers between devices: 27.2 us -> 31 us  [shift(): lax.ppermute(piece, name, [(i, (i + by) % count) for i in range(count)])]
    ppermute x2, waiting for transfers between devices: 8.28 us -> 4.96 us  [to_parity(): return lax.ppermute(tile, COLUMN, pairs)]
    ppermute x18, waiting for transfers between devices: 36.1 us -> 38.6 us  [shift(): lax.ppermute(piece, name, [(i, (i + by) % count) for i in range(count)])]
  transfers between devices with their start and end apart: 20 -> 20, of which waited for: 10 -> 10; matrix products, arithmetic and copies ran while one was open for 0% -> 0% of each run, Pallas kernels for 6% -> 5%
where the time goes in v7:
time: 89.5 us; the launch traced here: 89.3 us
  waiting for transfers between devices  43.6 us (49%)
  starting transfers between devices  37.1 us (41%)
  Pallas kernels  7.28 us (8%)
  local copies, waits for them, and re-layouts  1.24 us (1%)
    ppermute x18, waiting for transfers between devices, shift(): lax.ppermute(piece, name, [(i, (i + by) % count) for i in range(count)])  38.6 us
    ppermute x18, starting transfers between devices, shift(): lax.ppermute(piece, name, [(i, (i + by) % count) for i in range(count)])  31 us
    ppermute x2, starting transfers between devices, to_parity(): return lax.ppermute(tile, COLUMN, pairs)  6.12 us
    ppermute x2, waiting for transfers between devices, to_parity(): return lax.ppermute(tile, COLUMN, pairs)  4.96 us
    pallas_call x3, Pallas kernels, late(): return call(kernel, out, scratch, specs, 'give' if given else 'keep')(*args)  4.27 us
  transfers between devices with their start and end apart: 20, of which 10 were waited for; matrix products, arithmetic and copies ran while one was open for 0% of the time, Pallas kernels for 5%

profile of v7, /device:TPU:1, one launch (start us, length us, event | category | flops | bytes accessed | tf_op | source)
XLA Modules:
  0.0 89.3 jit_solution(126846373867439073)
XLA Ops:
  0.0 0.1 stack.23.place
  0.1 1.0 %copy-done.1 = bf16[512,512]{1,0:T(8,128)(2,1)S(1)} copy-done((bf16[512,512]{1,0:T(8,128)(2,1)S(1)}, bf16[512,512]{1,0:T(8,128)(2,1)}, u32[]{:S(2)}) %copy-start.1) | copy-done | bytes 524312
  1.1 0.8 masked.1
  1.9 4.2 %collective-permute-start.7 = (bf16[512,512]{1,0:T(8,128)(2,1)S(1)}, bf16[512,512]{1,0:T(8,128)(2,1)S(1)}, u32[]{:S(2)}, u32[]{:S(2)}) collective-permute-start(bf16[512,512]{1,0:T(8,128)(2,1)S(1)} %masked.1), channel_id=1, source_target_pairs={{0,8},{1,24},{8,0},{9,16},{16,9},{17,25},{24,1},{25,17},{2,10},{3,... | collective-permute-start | bytes 1572872 | tf_op jit(solution)/shard_map/ppermute | solution.py:33
  6.1 1.9 %collective-permute-start.6 = (bf16[512,512]{1,0:T(8,128)(2,1)S(1)}, bf16[512,512]{1,0:T(8,128)(2,1)S(1)}, u32[]{:S(2)}, u32[]{:S(2)}) collective-permute-start(bf16[512,512]{1,0:T(8,128)(2,1)S(1)} %masked.1), channel_id=1, source_target_pairs={{0,0},{1,16},{8,8},{9,24},{16,1},{17,17},{24,9},{25,25},{2,2},{3,1... | collective-permute-start | bytes 1572872 | tf_op jit(solution)/shard_map/ppermute | solution.py:33
  8.1 5.7 %collective-permute-start.1 = (bf16[512,512]{1,0:T(8,128)(2,1)S(1)}, bf16[512,512]{1,0:T(8,128)(2,1)S(1)}, u32[]{:S(2)}, u32[]{:S(2)}) collective-permute-start(bf16[512,512]{1,0:T(8,128)(2,1)S(1)} %copy-done), channel_id=1, source_target_pairs={{0,224},{32,0},{64,32},{96,64},{128,96},{160,128},{192,160},{224,1... | collective-permute-start | bytes 1572872 | tf_op jit(solution)/shard_map/ppermute | solution.py:37
  13.7 0.0 collective-permute-start
  13.7 3.9 %collective-permute-done.7.refs_1_ = bf16[512,512]{1,0:T(8,128)(2,1)S(1)} collective-permute-done((bf16[512,512]{1,0:T(8,128)(2,1)S(1)}, bf16[512,512]{1,0:T(8,128)(2,1)S(1)}, u32[]{:S(2)}, u32[]{:S(2)}) %collective-permute-start.7) | collective-permute-done | bytes 524320 | tf_op jit(solution)/shard_map/ppermute | solution.py:33
  17.6 1.1 %collective-permute-done.6.refs_0_ = bf16[512,512]{1,0:T(8,128)(2,1)S(1)} collective-permute-done((bf16[512,512]{1,0:T(8,128)(2,1)S(1)}, bf16[512,512]{1,0:T(8,128)(2,1)S(1)}, u32[]{:S(2)}, u32[]{:S(2)}) %collective-permute-start.6) | collective-permute-done | bytes 524320 | tf_op jit(solution)/shard_map/ppermute | solution.py:33
  18.7 0.1 pack.2.refs_9_.refs_7_.refs_10_
  18.8 2.8 %collective-permute-start.9 = (bf16[1024,512]{1,0:T(8,128)(2,1)S(1)}, bf16[1024,512]{1,0:T(8,128)(2,1)S(1)}, u32[]{:S(2)}, u32[]{:S(2)}) collective-permute-start(bf16[1024,512]{1,0:T(8,128)(2,1)S(1)} %pack.2.refs_9_.refs_7_.refs_10_), channel_id=1, source_target_pairs={{0,6},{2,0},{4,2},{6,4},{1,7},{3,1},{5,3},{7,5},{8,14},{10,8},{12,... | collective-permute-start | bytes 3145736 | tf_op jit(solution)/shard_map/ppermute | solution.py:37
  21.6 0.0 collective-permute-start.8
  21.6 3.7 %collective-permute-done.1.refs_6_.refs_7_ = bf16[512,512]{1,0:T(8,128)(2,1)S(1)} collective-permute-done((bf16[512,512]{1,0:T(8,128)(2,1)S(1)}, bf16[512,512]{1,0:T(8,128)(2,1)S(1)}, u32[]{:S(2)}, u32[]{:S(2)}) %collective-permute-start.1) | collective-permute-done | bytes 524320 | tf_op jit(solution)/shard_map/ppermute | solution.py:37
  25.3 3.5 %collective-permute-done.refs_1_.refs_2_ = bf16[512,512]{1,0:T(8,128)(2,1)S(1)} collective-permute-done((bf16[512,512]{1,0:T(8,128)(2,1)S(1)}, bf16[512,512]{1,0:T(8,128)(2,1)S(1)}, u32[]{:S(2)}, u32[]{:S(2)}) %collective-permute-start) | collective-permute-done | bytes 524320 | tf_op jit(solution)/shard_map/ppermute | solution.py:37
  28.8 0.0 collective-permute-start.2
  28.8 2.7 %collective-permute-start.3 = (bf16[512,512]{1,0:T(8,128)(2,1)S(1)}, bf16[512,512]{1,0:T(8,128)(2,1)S(1)}, u32[]{:S(2)}, u32[]{:S(2)}) collective-permute-start(bf16[512,512]{1,0:T(8,128)(2,1)S(1)} %collective-permute-done.1.refs_6_.refs_7_), channel_id=1, source_target_pairs={{0,224},{32,0},{64,32},{96,64},{128,96},{160,128},{192,160},{224,1... | collective-permute-start | bytes 1572872 | tf_op jit(solution)/shard_map/ppermute | solution.py:37
  31.5 11.5 %collective-permute-done.2.refs_2_.refs_3_ = bf16[512,512]{1,0:T(8,128)(2,1)S(1)} collective-permute-done((bf16[512,512]{1,0:T(8,128)(2,1)S(1)}, bf16[512,512]{1,0:T(8,128)(2,1)S(1)}, u32[]{:S(2)}, u32[]{:S(2)}) %collective-permute-start.2) | collective-permute-done | bytes 524320 | tf_op jit(solution)/shard_map/ppermute | solution.py:37
  43.0 0.0 collective-permute-done.3.refs_5_.refs_6_
  43.0 0.0 collective-permute-start.4
  43.0 2.7 %collective-permute-start.5 = (bf16[512,512]{1,0:T(8,128)(2,1)S(1)}, bf16[512,512]{1,0:T(8,128)(2,1)S(1)}, u32[]{:S(2)}, u32[]{:S(2)}) collective-permute-start(bf16[512,512]{1,0:T(8,128)(2,1)S(1)} %collective-permute-done.3.refs_5_.refs_6_), channel_id=1, source_target_pairs={{0,224},{32,0},{64,32},{96,64},{128,96},{160,128},{192,160},{224,1... | collective-permute-start | bytes 1572872 | tf_op jit(solution)/shard_map/ppermute | solution.py:37
  45.7 0.0 collective-permute-done.9.refs_11_.refs_9_.refs_12_
  45.7 2.6 %collective-permute-start.13 = (bf16[512,512]{1,0:T(8,128)(2,1)S(1)}, bf16[512,512]{1,0:T(8,128)(2,1)S(1)}, u32[]{:S(2)}, u32[]{:S(2)}) collective-permute-start(bf16[512,512]{1,0:T(8,128)(2,1)S(1)} %slice.17), channel_id=1, source_target_pairs={{0,6},{2,0},{4,2},{6,4},{1,7},{3,1},{5,3},{7,5},{8,14},{10,8},{12,... | collective-permute-start | bytes 1572872 | tf_op jit(solution)/shard_map/ppermute | solution.py:37
  48.3 0.0 collective-permute-done.8.refs_10_.refs_8_.refs_11_
  48.3 0.1 collective-permute-start.12
  48.4 7.9 %collective-permute-done.4.refs_3_.refs_4_ = bf16[512,512]{1,0:T(8,128)(2,1)S(1)} collective-permute-done((bf16[512,512]{1,0:T(8,128)(2,1)S(1)}, bf16[512,512]{1,0:T(8,128)(2,1)S(1)}, u32[]{:S(2)}, u32[]{:S(2)}) %collective-permute-start.4) | collective-permute-done | bytes 524320 | tf_op jit(solution)/shard_map/ppermute | solution.py:37
  56.3 0.0 collective-permute-done.5.refs_4_.refs_5_
  56.3 2.5 %collective-permute-start.11 = (bf16[256,512]{1,0:T(8,128)(2,1)S(1)}, bf16[256,512]{1,0:T(8,128)(2,1)S(1)}, u32[]{:S(2)}, u32[]{:S(2)}) collective-permute-start(bf16[256,512]{1,0:T(8,128)(2,1)S(1)} %slice.13), channel_id=1, source_target_pairs={{0,224},{32,0},{64,32},{96,64},{128,96},{160,128},{192,160},{224,1... | collective-permute-start | bytes 786440 | tf_op jit(solution)/shard_map/ppermute | solution.py:37
  58.8 0.0 copy-start.2
  58.8 0.1 collective-permute-start.10
  58.9 2.9 %collective-permute-start.14 = (bf16[1024,512]{1,0:T(8,128)(2,1)S(1)}, bf16[1024,512]{1,0:T(8,128)(2,1)S(1)}, u32[]{:S(2)}, u32[]{:S(2)}) collective-permute-start(bf16[1024,512]{1,0:T(8,128)(2,1)S(1)} %pack.2.refs_9_.refs_7_.refs_10_), channel_id=1, source_target_pairs={{0,1},{1,0},{2,3},{3,2},{4,5},{5,4},{6,7},{7,6},{8,9},{9,8},{10,11... | collective-permute-start | bytes 3145736 | tf_op jit(solution)/shard_map/ppermute | solution.py:37
  61.8 0.3 collective-permute-done.11.refs_8_.refs_9_
  62.1 3.4 %collective-permute-start.15 = (bf16[1024,512]{1,0:T(8,128)(2,1)S(1)}, bf16[1024,512]{1,0:T(8,128)(2,1)S(1)}, u32[]{:S(2)}, u32[]{:S(2)}) collective-permute-start(bf16[1024,512]{1,0:T(8,128)(2,1)S(1)} %collective-permute-done.8.refs_10_.refs_8_.refs_11_), channel_id=1, source_target_pairs={{0,1},{1,0},{2,3},{3,2},{4,5},{5,4},{6,7},{7,6},{8,9},{9,8},{10,11... | collective-permute-start | bytes 3145736 | tf_op jit(solution)/shard_map/ppermute | solution.py:37
  65.5 0.0 collective-permute-done.10.refs_7_.refs_8_
  65.5 3.8 %collective-permute-start.16 = (bf16[1024,512]{1,0:T(8,128)(2,1)S(1)}, bf16[1024,512]{1,0:T(8,128)(2,1)S(1)}, u32[]{:S(2)}, u32[]{:S(2)}) collective-permute-start(bf16[1024,512]{1,0:T(8,128)(2,1)S(1)} %collective-permute-done.9.refs_11_.refs_9_.refs_12_), channel_id=1, source_target_pairs={{0,1},{1,0},{2,3},{3,2},{4,5},{5,4},{6,7},{7,6},{8,9},{9,8},{10,11... | collective-permute-start | bytes 3145736 | tf_op jit(solution)/shard_map/ppermute | solution.py:37
  69.3 0.1 pack.3
  69.4 0.3 collective-permute-start.17
  69.7 0.0 collective-permute-done.14.refs_14_.refs_10_.refs_15_
  69.7 1.9 %collective-permute-done.16.refs_16_.refs_12_.refs_17_ = bf16[1024,512]{1,0:T(8,128)(2,1)S(1)} collective-permute-done((bf16[1024,512]{1,0:T(8,128)(2,1)S(1)}, bf16[1024,512]{1,0:T(8,128)(2,1)S(1)}, u32[]{:S(2)}, u32[]{:S(2)}) %collective-permute-start.16) | collective-permute-done | bytes 1048608 | tf_op jit(solution)/shard_map/ppermute | solution.py:37
  71.6 1.1 %early.1.refs_0_ = f32[512,512]{1,0:T(8,128)S(1)} custom-call(s32[5]{0:T(128)S(1)} %stack.23.place, s32[16,16]{1,0:T(8,128)S(1)} %copy-done.2, bf16[512,512]{1,0:T(8,128)(2,1)S(1)} %copy-done, bf16[512,512]{1,0:T(8,128)(2,1)S(1)} %collective-permute-done.refs_1_.refs_2_, bf16[512,512]{1,0:T(8,128)(2,1)S(1)} %collective-permute-done.2.refs_2_.refs_3_, ...), custom_call_target="tpu_custom_call" | custom-call | tf_op jit(solution)/shard_map/early/pallas_call | solution.py:130
  72.7 0.4 collective-permute-done.17.refs_17_.refs_18_
  73.1 1.3 %give.3 = s16[400,512]{1,0:T(8,128)(2,1)S(1)} custom-call(s32[5]{0:T(128)S(1)} %stack.23.place, s32[16,16]{1,0:T(8,128)S(1)} %copy-done.2, f32[512,512]{1,0:T(8,128)S(1)} %early.1.refs_0_, bf16[512,512]{1,0:T(8,128)(2,1)S(1)} %copy-done, bf16[512,512]{1,0:T(8,128)(2,1)S(1)} %collective-permute-done.refs_1_.refs_2_, ...), custom_call_target="tpu_custom_call" | custom-call | tf_op jit(solution)/shard_map/give/pallas_call | solution.py:156
  74.4 0.1 collective-permute-start.19
  74.5 1.1 %give.2 = s16[144,512]{1,0:T(8,128)(2,1)S(1)} custom-call(s32[5]{0:T(128)S(1)} %stack.23.place, s32[16,16]{1,0:T(8,128)S(1)} %copy-done.2, f32[512,512]{1,0:T(8,128)S(1)} %early.1.refs_0_, bf16[512,512]{1,0:T(8,128)(2,1)S(1)} %copy-done, bf16[512,512]{1,0:T(8,128)(2,1)S(1)} %collective-permute-done.refs_1_.refs_2_, ...), custom_call_target="tpu_custom_call" | custom-call | tf_op jit(solution)/shard_map/give/pallas_call | solution.py:156
  75.6 1.5 %collective-permute-start.18 = (s16[144,512]{1,0:T(8,128)(2,1)S(1)}, s16[144,512]{1,0:T(8,128)(2,1)S(1)}, u32[]{:S(2)}, u32[]{:S(2)}) collective-permute-start(s16[144,512]{1,0:T(8,128)(2,1)S(1)} %give.2), channel_id=1, source_target_pairs={{0,16},{16,0},{1,17},{17,1},{2,18},{18,2},{3,19},{19,3},{4,20},{20... | collective-permute-start | bytes 442376 | tf_op jit(solution)/shard_map/ppermute | solution.py:37
  77.1 1.9 %keep.1 = f32[512,512]{1,0:T(8,128)S(1)} custom-call(s32[5]{0:T(128)S(1)} %stack.23.place, s32[16,16]{1,0:T(8,128)S(1)} %copy-done.2, bf16[512,512]{1,0:T(8,128)(2,1)S(1)} %copy-done, bf16[512,512]{1,0:T(8,128)(2,1)S(1)} %collective-permute-done.refs_1_.refs_2_, bf16[512,512]{1,0:T(8,128)(2,1)S(1)} %collective-permute-done.2.refs_2_.refs_3_, ...), custom_call_target="tpu_custom_call" | custom-call | tf_op jit(solution)/shard_map/keep/pallas_call | solution.py:156
  79.0 9.3 %collective-permute-done.18.refs_0_ = s16[144,512]{1,0:T(8,128)(2,1)S(1)} collective-permute-done((s16[144,512]{1,0:T(8,128)(2,1)S(1)}, s16[144,512]{1,0:T(8,128)(2,1)S(1)}, u32[]{:S(2)}, u32[]{:S(2)}) %collective-permute-start.18) | collective-permute-done | bytes 147488 | tf_op jit(solution)/shard_map/ppermute | solution.py:37
  88.3 0.0 collective-permute-done.19.refs_1_
  88.3 1.0 %join.1 = bf16[512,512]{1,0:T(8,128)(2,1)} custom-call(f32[512,512]{1,0:T(8,128)S(1)} %keep.1, s16[144,512]{1,0:T(8,128)(2,1)S(1)} %collective-permute-done.18.refs_0_, s16[400,512]{1,0:T(8,128)(2,1)S(1)} %collective-permute-done.19.refs_1_), custom_call_target="tpu_custom_call" | custom-call | tf_op jit(solution)/shard_map/join/pallas_call | solution.py:171
  (11 shorter events, 0.1 us)
Async XLA Ops:
  0.1 1.0 %copy-start.1 = (bf16[512,512]{1,0:T(8,128)(2,1)S(1)}, bf16[512,512]{1,0:T(8,128)(2,1)}, u32[]{:S(2)}) copy-start(bf16[512,512]{1,0:T(8,128)(2,1)} %factor.1) | copy-start | bytes 1572868
  1.1 6.9 %copy-start = (bf16[512,512]{1,0:T(8,128)(2,1)S(1)}, bf16[512,512]{1,0:T(8,128)(2,1)}, u32[]{:S(2)}) copy-start(bf16[512,512]{1,0:T(8,128)(2,1)} %refs_1_.3) | copy-start | bytes 1572868
  1.9 15.7 %collective-permute-start.7 = (bf16[512,512]{1,0:T(8,128)(2,1)S(1)}, bf16[512,512]{1,0:T(8,128)(2,1)S(1)}, u32[]{:S(2)}, u32[]{:S(2)}) collective-permute-start(bf16[512,512]{1,0:T(8,128)(2,1)S(1)} %masked.1), channel_id=1, source_target_pairs={{0,8},{1,24},{8,0},{9,16},{16,9},{17,25},{24,1},{25,17},{2,10},{3,... | collective-permute-start | bytes 1572872 | tf_op jit(solution)/shard_map/ppermute | solution.py:33
  6.1 12.5 %collective-permute-start.6 = (bf16[512,512]{1,0:T(8,128)(2,1)S(1)}, bf16[512,512]{1,0:T(8,128)(2,1)S(1)}, u32[]{:S(2)}, u32[]{:S(2)}) collective-permute-start(bf16[512,512]{1,0:T(8,128)(2,1)S(1)} %masked.1), channel_id=1, source_target_pairs={{0,0},{1,16},{8,8},{9,24},{16,1},{17,17},{24,9},{25,25},{2,2},{3,1... | collective-permute-start | bytes 1572872 | tf_op jit(solution)/shard_map/ppermute | solution.py:33
  8.1 17.2 %collective-permute-start.1 = (bf16[512,512]{1,0:T(8,128)(2,1)S(1)}, bf16[512,512]{1,0:T(8,128)(2,1)S(1)}, u32[]{:S(2)}, u32[]{:S(2)}) collective-permute-start(bf16[512,512]{1,0:T(8,128)(2,1)S(1)} %copy-done), channel_id=1, source_target_pairs={{0,224},{32,0},{64,32},{96,64},{128,96},{160,128},{192,160},{224,1... | collective-permute-start | bytes 1572872 | tf_op jit(solution)/shard_map/ppermute | solution.py:37
  13.7 15.1 %collective-permute-start = (bf16[512,512]{1,0:T(8,128)(2,1)S(1)}, bf16[512,512]{1,0:T(8,128)(2,1)S(1)}, u32[]{:S(2)}, u32[]{:S(2)}) collective-permute-start(bf16[512,512]{1,0:T(8,128)(2,1)S(1)} %copy-done), channel_id=1, source_target_pairs={{0,32},{32,64},{64,96},{96,128},{128,160},{160,192},{192,224},{224... | collective-permute-start | bytes 1572872 | tf_op jit(solution)/shard_map/ppermute | solution.py:37
  18.8 26.9 %collective-permute-start.9 = (bf16[1024,512]{1,0:T(8,128)(2,1)S(1)}, bf16[1024,512]{1,0:T(8,128)(2,1)S(1)}, u32[]{:S(2)}, u32[]{:S(2)}) collective-permute-start(bf16[1024,512]{1,0:T(8,128)(2,1)S(1)} %pack.2.refs_9_.refs_7_.refs_10_), channel_id=1, source_target_pairs={{0,6},{2,0},{4,2},{6,4},{1,7},{3,1},{5,3},{7,5},{8,14},{10,8},{12,... | collective-permute-start | bytes 3145736 | tf_op jit(solution)/shard_map/ppermute | solution.py:37
  21.6 26.7 %collective-permute-start.8 = (bf16[1024,512]{1,0:T(8,128)(2,1)S(1)}, bf16[1024,512]{1,0:T(8,128)(2,1)S(1)}, u32[]{:S(2)}, u32[]{:S(2)}) collective-permute-start(bf16[1024,512]{1,0:T(8,128)(2,1)S(1)} %pack.2.refs_9_.refs_7_.refs_10_), channel_id=1, source_target_pairs={{0,2},{2,4},{4,6},{6,0},{1,3},{3,5},{5,7},{7,1},{8,10},{10,12},{12... | collective-permute-start | bytes 3145736 | tf_op jit(solution)/shard_map/ppermute | solution.py:37
  28.8 14.2 %collective-permute-start.2 = (bf16[512,512]{1,0:T(8,128)(2,1)S(1)}, bf16[512,512]{1,0:T(8,128)(2,1)S(1)}, u32[]{:S(2)}, u32[]{:S(2)}) collective-permute-start(bf16[512,512]{1,0:T(8,128)(2,1)S(1)} %collective-permute-done.refs_1_.refs_2_), channel_id=1, source_target_pairs={{0,32},{32,64},{64,96},{96,128},{128,160},{160,192},{192,224},{224... | collective-permute-start | bytes 1572872 | tf_op jit(solution)/shard_map/ppermute | solution.py:37
  28.8 14.2 %collective-permute-start.3 = (bf16[512,512]{1,0:T(8,128)(2,1)S(1)}, bf16[512,512]{1,0:T(8,128)(2,1)S(1)}, u32[]{:S(2)}, u32[]{:S(2)}) collective-permute-start(bf16[512,512]{1,0:T(8,128)(2,1)S(1)} %collective-permute-done.1.refs_6_.refs_7_), channel_id=1, source_target_pairs={{0,224},{32,0},{64,32},{96,64},{128,96},{160,128},{192,160},{224,1... | collective-permute-start | bytes 1572872 | tf_op jit(solution)/shard_map/ppermute | solution.py:37
  43.0 13.3 %collective-permute-start.4 = (bf16[512,512]{1,0:T(8,128)(2,1)S(1)}, bf16[512,512]{1,0:T(8,128)(2,1)S(1)}, u32[]{:S(2)}, u32[]{:S(2)}) collective-permute-start(bf16[512,512]{1,0:T(8,128)(2,1)S(1)} %collective-permute-done.2.refs_2_.refs_3_), channel_id=1, source_target_pairs={{0,32},{32,64},{64,96},{96,128},{128,160},{160,192},{192,224},{224... | collective-permute-start | bytes 1572872 | tf_op jit(solution)/shard_map/ppermute | solution.py:37
  43.0 13.3 %collective-permute-start.5 = (bf16[512,512]{1,0:T(8,128)(2,1)S(1)}, bf16[512,512]{1,0:T(8,128)(2,1)S(1)}, u32[]{:S(2)}, u32[]{:S(2)}) collective-permute-start(bf16[512,512]{1,0:T(8,128)(2,1)S(1)} %collective-permute-done.3.refs_5_.refs_6_), channel_id=1, source_target_pairs={{0,224},{32,0},{64,32},{96,64},{128,96},{160,128},{192,160},{224,1... | collective-permute-start | bytes 1572872 | tf_op jit(solution)/shard_map/ppermute | solution.py:37
  45.7 23.6 %collective-permute-start.13 = (bf16[512,512]{1,0:T(8,128)(2,1)S(1)}, bf16[512,512]{1,0:T(8,128)(2,1)S(1)}, u32[]{:S(2)}, u32[]{:S(2)}) collective-permute-start(bf16[512,512]{1,0:T(8,128)(2,1)S(1)} %slice.17), channel_id=1, source_target_pairs={{0,6},{2,0},{4,2},{6,4},{1,7},{3,1},{5,3},{7,5},{8,14},{10,8},{12,... | collective-permute-start | bytes 1572872 | tf_op jit(solution)/shard_map/ppermute | solution.py:37
  48.3 21.0 %collective-permute-start.12 = (bf16[512,512]{1,0:T(8,128)(2,1)S(1)}, bf16[512,512]{1,0:T(8,128)(2,1)S(1)}, u32[]{:S(2)}, u32[]{:S(2)}) collective-permute-start(bf16[512,512]{1,0:T(8,128)(2,1)S(1)} %slice.16), channel_id=1, source_target_pairs={{0,2},{2,4},{4,6},{6,0},{1,3},{3,5},{5,7},{7,1},{8,10},{10,12},{12... | collective-permute-start | bytes 1572872 | tf_op jit(solution)/shard_map/ppermute | solution.py:37
  56.3 5.8 %collective-permute-start.11 = (bf16[256,512]{1,0:T(8,128)(2,1)S(1)}, bf16[256,512]{1,0:T(8,128)(2,1)S(1)}, u32[]{:S(2)}, u32[]{:S(2)}) collective-permute-start(bf16[256,512]{1,0:T(8,128)(2,1)S(1)} %slice.13), channel_id=1, source_target_pairs={{0,224},{32,0},{64,32},{96,64},{128,96},{160,128},{192,160},{224,1... | collective-permute-start | bytes 786440 | tf_op jit(solution)/shard_map/ppermute | solution.py:37
  58.8 12.8 %copy-start.2 = (s32[16,16]{1,0:T(8,128)S(1)}, s32[16,16]{1,0:T(8,128)}, u32[]{:S(2)}) copy-start(s32[16,16]{1,0:T(8,128)} %occupancy.7) | copy-start | bytes 3076
  58.8 6.7 %collective-permute-start.10 = (bf16[256,512]{1,0:T(8,128)(2,1)S(1)}, bf16[256,512]{1,0:T(8,128)(2,1)S(1)}, u32[]{:S(2)}, u32[]{:S(2)}) collective-permute-start(bf16[256,512]{1,0:T(8,128)(2,1)S(1)} %slice.12), channel_id=1, source_target_pairs={{0,32},{32,64},{64,96},{96,128},{128,160},{160,192},{192,224},{224... | collective-permute-start | bytes 786440 | tf_op jit(solution)/shard_map/ppermute | solution.py:37
  58.9 10.7 %collective-permute-start.14 = (bf16[1024,512]{1,0:T(8,128)(2,1)S(1)}, bf16[1024,512]{1,0:T(8,128)(2,1)S(1)}, u32[]{:S(2)}, u32[]{:S(2)}) collective-permute-start(bf16[1024,512]{1,0:T(8,128)(2,1)S(1)} %pack.2.refs_9_.refs_7_.refs_10_), channel_id=1, source_target_pairs={{0,1},{1,0},{2,3},{3,2},{4,5},{5,4},{6,7},{7,6},{8,9},{9,8},{10,11... | collective-permute-start | bytes 3145736 | tf_op jit(solution)/shard_map/ppermute | solution.py:37
  62.1 7.6 %collective-permute-start.15 = (bf16[1024,512]{1,0:T(8,128)(2,1)S(1)}, bf16[1024,512]{1,0:T(8,128)(2,1)S(1)}, u32[]{:S(2)}, u32[]{:S(2)}) collective-permute-start(bf16[1024,512]{1,0:T(8,128)(2,1)S(1)} %collective-permute-done.8.refs_10_.refs_8_.refs_11_), channel_id=1, source_target_pairs={{0,1},{1,0},{2,3},{3,2},{4,5},{5,4},{6,7},{7,6},{8,9},{9,8},{10,11... | collective-permute-start | bytes 3145736 | tf_op jit(solution)/shard_map/ppermute | solution.py:37
  65.5 6.1 %collective-permute-start.16 = (bf16[1024,512]{1,0:T(8,128)(2,1)S(1)}, bf16[1024,512]{1,0:T(8,128)(2,1)S(1)}, u32[]{:S(2)}, u32[]{:S(2)}) collective-permute-start(bf16[1024,512]{1,0:T(8,128)(2,1)S(1)} %collective-permute-done.9.refs_11_.refs_9_.refs_12_), channel_id=1, source_target_pairs={{0,1},{1,0},{2,3},{3,2},{4,5},{5,4},{6,7},{7,6},{8,9},{9,8},{10,11... | collective-permute-start | bytes 3145736 | tf_op jit(solution)/shard_map/ppermute | solution.py:37
  69.4 3.7 %collective-permute-start.17 = (bf16[1024,512]{1,0:T(8,128)(2,1)S(1)}, bf16[1024,512]{1,0:T(8,128)(2,1)S(1)}, u32[]{:S(2)}, u32[]{:S(2)}) collective-permute-start(bf16[1024,512]{1,0:T(8,128)(2,1)S(1)} %pack.3), channel_id=1, source_target_pairs={{0,1},{1,0},{2,3},{3,2},{4,5},{5,4},{6,7},{7,6},{8,9},{9,8},{10,11... | collective-permute-start | bytes 3145736 | tf_op jit(solution)/shard_map/ppermute | solution.py:37
  74.4 13.9 %collective-permute-start.19 = (s16[400,512]{1,0:T(8,128)(2,1)S(1)}, s16[400,512]{1,0:T(8,128)(2,1)S(1)}, u32[]{:S(2)}, u32[]{:S(2)}) collective-permute-start(s16[400,512]{1,0:T(8,128)(2,1)S(1)} %give.3), channel_id=1, source_target_pairs={{0,16},{16,0},{1,17},{17,1},{2,18},{18,2},{3,19},{19,3},{4,20},{20... | collective-permute-start | bytes 1228808 | tf_op jit(solution)/shard_map/ppermute | solution.py:37
  75.6 12.7 %collective-permute-start.18 = (s16[144,512]{1,0:T(8,128)(2,1)S(1)}, s16[144,512]{1,0:T(8,128)(2,1)S(1)}, u32[]{:S(2)}, u32[]{:S(2)}) collective-permute-start(s16[144,512]{1,0:T(8,128)(2,1)S(1)} %give.2), channel_id=1, source_target_pairs={{0,16},{16,0},{1,17},{17,1},{2,18},{18,2},{3,19},{19,3},{4,20},{20... | collective-permute-start | bytes 442376 | tf_op jit(solution)/shard_map/ppermute | solution.py:37
